TPU v7x, 32 devices: a whole 2x2x4 slice. The times are simulated.
32 devices in a mesh: rows: 8 (over z, x), scene: 4 (over y, core).
Axes of the slice: x: 2, y: 2, z: 4, core: 2. Of those that a mesh axis runs over, the one named last changes fastest.
Arguments:
- points: bfloat16 [32, 9, 32, 6144], P('scene', None, None, 'rows'), may hold values from -8 to 8
- pillar_counts: int32 [32, 6144], P('scene', 'rows'), may hold values from 0 to 32, as said below
- pillar_pixels: int32 [32, 6144], P('scene', 'rows'), may hold values from 0 to 8191, as said below
- point_weight: bfloat16 [9, 64], replicated, may hold values from -2 to 2
- point_master: float32 [9, 64], replicated, may hold values from -2 to 2
- point_states: float32 [3, 9, 64], replicated, as said below
- norm_weight: bfloat16 [4, 64], replicated, may hold values from -1.5 to 1.5, as said below
- norm_master: float32 [4, 64], replicated, may hold values from -1.5 to 1.5, as said below
- norm_states: float32 [3, 4, 64], replicated, as said below
- kernel_weight: bfloat16 [576, 64], P('rows'), may hold values from -0.25 to 0.25
- kernel_master: float32 [576, 64], P('rows'), may hold values from -0.25 to 0.25
- kernel_states: float32 [3, 576, 64], P(None, 'rows'), as said below
- step_count: int32 [1], replicated, may hold values from 1 to 20
- cotangent: bfloat16 [64, 32, 64, 256], P('rows', 'scene'), may hold values from -6 to 6
Outputs:
- result: bfloat16 [64, 32, 64, 256], P('rows', 'scene')
- point_master_new: float32 [9, 64], replicated
- point_states_new: float32 [2, 9, 64], replicated
- point_average_new: float32 [9, 64], replicated
- point_copy: bfloat16 [9, 64], replicated
- norm_master_new: float32 [4, 64], replicated
- norm_states_new: float32 [2, 4, 64], replicated
- norm_average_new: float32 [4, 64], replicated
- norm_copy: bfloat16 [4, 64], replicated
- kernel_master_new: float32 [576, 64], P('rows')
- kernel_states_new: float32 [2, 576, 64], P(None, 'rows')
- kernel_average_new: float32 [576, 64], P('rows')
- kernel_copy: bfloat16 [576, 64], P('rows')
Inputs may be any that keep to these rules, and one draw needn't show every extreme that they name: `pillar_counts`: within each device's list of 768 slots the live pillars (count 1 or more) come first and the others have count 0; the first slot of every list holds 32 points; some device's list is live in every slot in every draw. `pillar_pixels`: A slot's cell is its row within the device's 16 rows times 512 plus its column; the cells of one device's list are distinct; the first 48 slots of each list lie in the device's last row and no other slot does; the first slot holds the device's last cell. `norm_weight`: rows 0 and 2 are gains, rows 1 and 3 biases. `norm_master`: rows 0 and 2 are gains, rows 1 and 3 biases. `point_states`: second moments are positive. `norm_states`: second moments are positive. `kernel_states`: second moments are positive.
All inputs are finite; a program needn't handle non-finite values.
Results may differ from a plain program's by a relative error of at most 0.002.
The roundings to bfloat16 on the way count: a program that leaves them out, or rounds other values in their place, can miss the bound.
Values may be sent and summed in bfloat16 or wider, within the bound.
No kernel may reach another device: no remote copies, remote signals or barrier semaphores. Data moves between devices by JAX's collectives and lax.ppermute only.
A program may use at most 256 MiB of HBM per device.

v0:
```python
import jax
import jax.numpy as jnp
from jax import lax
from jax.sharding import PartitionSpec as P

beta_one = 0.9
beta_two = 0.999
adam_eps = 1e-08
decay_rate = 0.01
average_keep = 0.99
norm_eps = 1e-05
rate_points = 0.3
rate_norms = 0.2
rate_kernel = 0.04


def shifted(x, axis, by):
    length = lax.axis_size(axis)
    pairs = [(i, i + by) for i in range(length) if 0 <= i + by < length]
    return lax.ppermute(x, axis, pairs)


def adam_step(master, states, gradient, step_count, step_rate):
    moment = beta_one * states[0] + (1.0 - beta_one) * gradient
    second = beta_two * states[1] + (1.0 - beta_two) * gradient * gradient
    steps_done = step_count[0].astype(jnp.float32)
    first_fix = 1.0 - beta_one**steps_done
    second_fix = 1.0 - beta_two**steps_done
    fresh = master - step_rate * (
        moment / first_fix / (jnp.sqrt(second / second_fix) + adam_eps) + decay_rate * master
    )
    average = average_keep * states[2] + (1.0 - average_keep) * fresh
    return (fresh, jnp.stack([moment, second]), average, fresh.astype(jnp.bfloat16))


def earlier_column(block):
    blank = jnp.zeros(block.shape[:-1] + (1,), block.dtype)
    return jnp.concatenate([blank, block[..., :-1]], axis=-1)


def later_column(block):
    blank = jnp.zeros(block.shape[:-1] + (1,), block.dtype)
    return jnp.concatenate([block[..., 1:], blank], axis=-1)


def tap_windows(canvas, rim_row):
    rows_even = canvas[0::2]
    rows_odd = canvas[1::2]
    rows_prev = jnp.concatenate([rim_row, rows_odd[:-1]], axis=0)
    windows = []
    for row_block in (rows_prev, rows_even, rows_odd):
        cols_even = row_block[..., 0::2]
        cols_odd = row_block[..., 1::2]
        windows.append((earlier_column(cols_odd), cols_even, cols_odd))
    return windows


def tap_back(source, kernels, tap_row, tap_col):
    return jnp.einsum(
        "rsow,co->rscw", source, kernels[tap_row, tap_col], preferred_element_type=jnp.float32
    )


def body(
    points,
    pillar_counts,
    pillar_pixels,
    point_weight,
    point_master,
    point_states,
    norm_weight,
    norm_master,
    norm_states,
    kernel_weight,
    kernel_master,
    kernel_states,
    step_count,
    cotangent,
):
    out_rows = cotangent.shape[0]
    scenes_here = cotangent.shape[1]
    channels = cotangent.shape[2]
    out_columns = cotangent.shape[3]
    rows_here = 2 * out_rows
    columns = 2 * out_columns
    depth = points.shape[2]
    cell_base = jnp.arange(columns)[None, None, :]
    kernel_full = lax.all_gather(kernel_weight, "rows", axis=0, tiled=True)
    kernels = kernel_full.reshape(3, 3, channels, channels)
    norm_values = norm_weight.astype(jnp.float32)
    live_mask = (jnp.arange(depth)[None, :, None] < pillar_counts[:, None, :]).astype(jnp.float32)[
        :, None
    ]
    lifted_features = jnp.einsum(
        "sinp,ic->scnp", points, point_weight, preferred_element_type=jnp.float32
    )
    masked = lifted_features * live_mask
    sum_one, sum_two, total_count = lax.psum(
        (
            jnp.sum(masked, axis=(0, 2, 3)),
            jnp.sum(masked * lifted_features, axis=(0, 2, 3)),
            jnp.sum(live_mask),
        ),
        ("rows", "scene"),
    )
    point_batch_mean = sum_one / total_count
    inverse_point_std = lax.rsqrt(
        sum_two / total_count - point_batch_mean * point_batch_mean + norm_eps
    )
    normalized_points = (
        lifted_features - point_batch_mean[None, :, None, None]
    ) * inverse_point_std[None, :, None, None]
    points_before_norm = (
        norm_values[0][None, :, None, None] * normalized_points
        + norm_values[1][None, :, None, None]
    )
    activated = jax.nn.relu(points_before_norm) * live_mask
    pooled = jnp.max(activated, axis=2)
    pooled_low = pooled.astype(jnp.bfloat16)

    def cell_table(row_index):
        return (pillar_pixels[:, :, None] == row_index * columns + cell_base).astype(jnp.bfloat16)

    def place_row(row_index):
        return jnp.einsum(
            "scp,spw->scw", pooled_low, cell_table(row_index), preferred_element_type=jnp.float32
        ).astype(jnp.bfloat16)

    canvas = lax.map(place_row, jnp.arange(rows_here))
    rim_row = shifted(canvas[-1:], "rows", 1)
    windows = tap_windows(canvas, rim_row)
    convolved_output = jnp.zeros((out_rows, scenes_here, channels, out_columns), jnp.float32)
    for tap_row in range(3):
        for tap_col in range(3):
            convolved_output = convolved_output + jnp.einsum(
                "rscw,co->rsow",
                windows[tap_row][tap_col],
                kernels[tap_row, tap_col],
                preferred_element_type=jnp.float32,
            )
    cells_all = float(
        out_rows * scenes_here * out_columns * lax.axis_size("rows") * lax.axis_size("scene")
    )
    sum_conv, square_conv = lax.psum(
        (
            jnp.sum(convolved_output, axis=(0, 1, 3)),
            jnp.sum(convolved_output * convolved_output, axis=(0, 1, 3)),
        ),
        ("rows", "scene"),
    )
    conv_batch_mean = sum_conv / cells_all
    inverse_conv_std = lax.rsqrt(
        square_conv / cells_all - conv_batch_mean * conv_batch_mean + norm_eps
    )
    normalized_conv = (convolved_output - conv_batch_mean[None, None, :, None]) * inverse_conv_std[
        None, None, :, None
    ]
    conv_before_norm = (
        norm_values[2][None, None, :, None] * normalized_conv + norm_values[3][None, None, :, None]
    )
    result = jax.nn.relu(conv_before_norm).astype(jnp.bfloat16)
    backward_conv_grad = cotangent.astype(jnp.float32) * (conv_before_norm > 0)
    bias_conv_grad, conv_gain_gradient = lax.psum(
        (
            jnp.sum(backward_conv_grad, axis=(0, 1, 3)),
            jnp.sum(backward_conv_grad * normalized_conv, axis=(0, 1, 3)),
        ),
        ("rows", "scene"),
    )
    scale_conv = norm_values[2] * inverse_conv_std / cells_all
    conv_grad = (
        scale_conv[None, None, :, None]
        * (
            cells_all * backward_conv_grad
            - bias_conv_grad[None, None, :, None]
            - normalized_conv * conv_gain_gradient[None, None, :, None]
        )
    ).astype(jnp.bfloat16)
    first_grad = conv_grad[:1]
    next_grad = shifted(first_grad, "rows", -1)
    later_grad = jnp.concatenate([conv_grad[1:], next_grad], axis=0)
    kernel_parts = []
    for tap_row in range(3):
        for tap_col in range(3):
            kernel_parts.append(
                jnp.einsum(
                    "rscw,rsow->co",
                    windows[tap_row][tap_col],
                    conv_grad,
                    preferred_element_type=jnp.float32,
                )
            )
    kernel_grad = jnp.stack(kernel_parts).reshape(9 * channels, channels)
    own_rows = kernel_master.shape[0]
    even_even = tap_back(conv_grad, kernels, 1, 1)
    even_odd = later_column(tap_back(conv_grad, kernels, 1, 0)) + tap_back(conv_grad, kernels, 1, 2)
    odd_even = tap_back(later_grad, kernels, 0, 1) + tap_back(conv_grad, kernels, 2, 1)
    odd_odd = (
        later_column(tap_back(later_grad, kernels, 0, 0) + tap_back(conv_grad, kernels, 2, 0))
        + tap_back(later_grad, kernels, 0, 2)
        + tap_back(conv_grad, kernels, 2, 2)
    )
    even_rows = jnp.stack([even_even, even_odd], axis=-1).reshape(
        out_rows, scenes_here, channels, columns
    )
    odd_rows = jnp.stack([odd_even, odd_odd], axis=-1).reshape(
        out_rows, scenes_here, channels, columns
    )
    canvas_back = jnp.stack([even_rows, odd_rows], axis=1).reshape(
        rows_here, scenes_here, channels, columns
    )
    canvas_low = canvas_back.astype(jnp.bfloat16)

    def take_row(carry, inputs):
        row_index, row_grad = inputs
        return (
            carry
            + jnp.einsum(
                "scw,spw->scp", row_grad, cell_table(row_index), preferred_element_type=jnp.float32
            ),
            None,
        )

    pooled_grad, unused = lax.scan(
        take_row, jnp.zeros(pooled.shape, jnp.float32), (jnp.arange(rows_here), canvas_low)
    )
    winners = (activated == pooled[:, :, None, :]).astype(jnp.float32)
    backward_point_grad = (
        pooled_grad[:, :, None, :]
        * winners
        / jnp.sum(winners, axis=2, keepdims=True)
        * live_mask
        * (points_before_norm > 0)
    )
    bias_point_grad, point_gain_gradient = lax.psum(
        (
            jnp.sum(backward_point_grad, axis=(0, 2, 3)),
            jnp.sum(backward_point_grad * normalized_points, axis=(0, 2, 3)),
        ),
        ("rows", "scene"),
    )
    scale_points = norm_values[0] * inverse_point_std / total_count
    lifted_grad = (
        live_mask
        * scale_points[None, :, None, None]
        * (
            total_count * backward_point_grad
            - bias_point_grad[None, :, None, None]
            - normalized_points * point_gain_gradient[None, :, None, None]
        )
    )
    point_grad = jnp.einsum(
        "sinp,scnp->ic", points.astype(jnp.float32), lifted_grad, precision=lax.Precision.HIGHEST
    )
    kernel_total, point_total = lax.psum((kernel_grad, point_grad), ("rows", "scene"))
    kernel_own = lax.dynamic_slice_in_dim(
        kernel_total, lax.axis_index("rows") * own_rows, own_rows, 0
    )
    norm_grad = jnp.stack(
        [point_gain_gradient, bias_point_grad, conv_gain_gradient, bias_conv_grad]
    )
    point_new, point_states_new, point_average_new, point_copy = adam_step(
        point_master, point_states, point_total, step_count, rate_points
    )
    norm_new, norm_states_new, norm_average_new, norm_copy = adam_step(
        norm_master, norm_states, norm_grad, step_count, rate_norms
    )
    kernel_new, kernel_states_new, kernel_average_new, kernel_copy = adam_step(
        kernel_master, kernel_states, kernel_own, step_count, rate_kernel
    )
    return (
        result,
        point_new,
        point_states_new,
        point_average_new,
        point_copy,
        norm_new,
        norm_states_new,
        norm_average_new,
        norm_copy,
        kernel_new,
        kernel_states_new,
        kernel_average_new,
        kernel_copy,
    )


def solution(mesh):
    placed = (
        P("scene", None, None, "rows"),
        P("scene", "rows"),
        P("scene", "rows"),
        P(),
        P(),
        P(),
        P(),
        P(),
        P(),
        P("rows", None),
        P("rows", None),
        P(None, "rows", None),
        P(),
        P("rows", "scene", None, None),
    )
    return jax.shard_map(
        body,
        mesh=mesh,
        in_specs=placed,
        out_specs=(
            P("rows", "scene", None, None),
            P(),
            P(),
            P(),
            P(),
            P(),
            P(),
            P(),
            P(),
            P("rows", None),
            P(None, "rows", None),
            P("rows", None),
            P("rows", None),
        ),
        check_vma=False,
    )
```

profile of v0, /device:TPU:0, one launch (start us, length us, event | category | flops | bytes accessed | tf_op | source)
XLA Modules:
  0.0 1354.4 jit_solution(15801590165573061488)
XLA Ops:
  11.8 21.9 %fusion.26 = (f32[64]{0:T(128)S(1)}, f32[64]{0:T(128)S(1)}, f32[64,8,32,768]{3,0,2,1:T(8,128)}) fusion(f32[8,32,768]{2,1,0:T(8,128)} %fusion.88, bf16[8,9,32,768]{3,2,1,0:T(8,128)(2,1)S(1)} %copy-done, bf16[9,64]{1,0:T(8,128)(2,1)} %param.21), kind=kOutput, calls=%fused_computation.21 | convolution fusion | flops 276823936 | bytes 54658688 | tf_op jit(solution)/shard_map/sinp,ic->scnp/dot_general | solution.py:94
  33.8 42.3 %all-reduce.8 = (f32[64]{0:T(128)}, f32[]{:T(128)}, f32[64]{0:T(128)}) all-reduce(f32[64]{0:T(128)S(1)} %get-tuple-element.177, f32[]{:T(128)} %convert_reduce_fusion.1, f32[64]{0:T(128)S(1)} %get-tuple-element.176), channel_id=1, replica_groups=mesh['rows'=8,'scene'=4] {'rows','scene'}, use_global_device_ids=true, to_apply=%region_1.0 | all-reduce | flops 129 | bytes 1032 | tf_op jit(solution)/shard_map/psum | solution.py:98
  77.9 23.1 %fusion.31 = f32[8,64,768]{2,1,0:T(8,128)} fusion(f32[64,8,32,768]{3,0,2,1:T(8,128)} %get-tuple-element.247, f32[64]{0:T(128)S(1)} %get-tuple-element.242, f32[64]{0:T(128)S(1)} %get-tuple-element.220, f32[64]{0:T(128)S(1)} %get-tuple-element.221, f32[8,32,768]{2,1,0:T(8,128)} %fusion.88, f32[64]{0:T(128)} %get-tuple-element.243), kind=kLoop, calls=%fused_computation.33 | loop fusion | flops 87687168 | bytes 52691968 | tf_op jit(solution)/shard_map/reduce_max | solution.py:118
  103.9 95.8 %while.22 = (s32[]{:T(128)}, bf16[16,8,64,512]{3,2,1,0:T(8,128)(2,1)}, s32[8,768]{1,0:T(8,128)}, s32[16]{0:T(128)}, bf16[8,64,768]{2,1,0:T(8,128)(2,1)}, /*index=5*/s32[]{:T(128)}, s32[1]{0:T(128)}) while((s32[]{:T(128)}, bf16[16,8,64,512]{3,2,1,0:T(8,128)(2,1)}, s32[8,768]{1,0:T(8,128)}, s32[16]{0:T(128)}, ...), condition=%wide.region_8.9_spmd.clone, body=%wide.region_7.8_spmd.clone.sunk | while | flops 406061568 | bytes 1340009 | solution.py:129
  216.0 73.1 %slice.147 = bf16[8,8,64,256]{3,2,1,0:T(8,128)(2,1)} slice(bf16[8,8,64,512]{3,2,1,0:T(8,128)(2,1)} %copy-done.9), slice={[0:8:1], [0:8:1], [0:64:1], [1:512:2]} | slice | bytes 4194304 | tf_op jit(solution)/shard_map/slice | solution.py:53
  289.0 73.1 %slice.150 = bf16[8,8,64,256]{3,2,1,0:T(8,128)(2,1)} slice(bf16[8,8,64,512]{3,2,1,0:T(8,128)(2,1)} %copy-done.9), slice={[0:8:1], [0:8:1], [0:64:1], [0:512:2]} | slice | bytes 4194304 | tf_op jit(solution)/shard_map/slice | solution.py:52
  362.1 73.1 %slice.141 = bf16[8,8,64,256]{3,2,1,0:T(8,128)(2,1)} slice(bf16[8,8,64,512]{3,2,1,0:T(8,128)(2,1)} %get-tuple-element.226), slice={[0:8:1], [0:8:1], [0:64:1], [1:512:2]} | slice | bytes 4194304 | tf_op jit(solution)/shard_map/slice | solution.py:53
  435.2 73.1 %slice.144 = bf16[8,8,64,256]{3,2,1,0:T(8,128)(2,1)} slice(bf16[8,8,64,512]{3,2,1,0:T(8,128)(2,1)} %get-tuple-element.226), slice={[0:8:1], [0:8:1], [0:64:1], [0:512:2]} | slice | bytes 4194304 | tf_op jit(solution)/shard_map/slice | solution.py:52
  508.3 29.2 %convert_reduce_fusion = (f32[8,64,768]{2,1,0:T(8,128)}, pred[8,64,32,768]{3,1,2,0:T(8,128)(4,1)}) fusion(f32[8,64,768]{2,1,0:T(8,128)} %fusion.31, f32[8,32,768]{2,1,0:T(8,128)} %fusion.88, f32[64]{0:T(128)S(1)} %get-tuple-element.242, f32[64]{0:T(128)S(1)} %get-tuple-element.220, f32[64]{0:T(128)S(1)} %get-tuple-element.221, ...), kind=kLoop, calls=%fused_computation.29 | loop fusion | flops 112852992 | bytes 66847744 | tf_op jit(solution)/shard_map/reduce_sum | solution.py:231
  537.5 32.7 %all-gather = bf16[8,72,64]{1,2,0:T(8,128)(2,1)} all-gather(bf16[1,72,64]{1,2,0:T(8,128)(2,1)S(1)} %bitcast.446), channel_id=1, replica_groups=mesh['rows'=8,'scene'=4] {'rows'}, dimensions={0}, use_global_device_ids=true | all-gather | bytes 82944 | tf_op jit(solution)/shard_map/all_gather | solution.py:88
  600.5 73.1 %slice.137 = bf16[8,8,64,256]{3,2,1,0:T(8,128)(2,1)} slice(bf16[8,8,64,512]{3,2,1,0:T(8,128)(2,1)} %pad_maximum_fusion.1), slice={[0:8:1], [0:8:1], [0:64:1], [0:512:2]} | slice | bytes 4194304 | tf_op jit(solution)/shard_map/slice | solution.py:52
  673.6 73.1 %slice.134 = bf16[8,8,64,256]{3,2,1,0:T(8,128)(2,1)} slice(bf16[8,8,64,512]{3,2,1,0:T(8,128)(2,1)} %pad_maximum_fusion.1), slice={[0:8:1], [0:8:1], [0:64:1], [1:512:2]} | slice | bytes 4194304 | tf_op jit(solution)/shard_map/slice | solution.py:53
  754.9 12.1 fusion.124
  767.0 37.1 %all-reduce.7 = (f32[64]{0:T(128)}, f32[64]{0:T(128)}) all-reduce(f32[64]{0:T(128)} %get-tuple-element.181, f32[64]{0:T(128)S(1)} %get-tuple-element.180), channel_id=1, replica_groups=mesh['rows'=8,'scene'=4] {'rows','scene'}, use_global_device_ids=true, to_apply=%region_12.13 | all-reduce | flops 128 | bytes 1024 | tf_op jit(solution)/shard_map/psum | solution.py:144
  811.3 42.1 %all-reduce.6 = (f32[64]{0:T(128)S(1)}, f32[64]{0:T(128)}) all-reduce(f32[64]{0:T(128)} %get-tuple-element.183, f32[64]{0:T(128)} %get-tuple-element.182), channel_id=1, replica_groups=mesh['rows'=8,'scene'=4] {'rows','scene'}, use_global_device_ids=true, to_apply=%region_16.17 | all-reduce | flops 128 | bytes 1024 | tf_op jit(solution)/shard_map/psum | solution.py:163
  891.0 10.9 copy.148
  903.2 99.8 %all-reduce.11.cloned.1.call-done = f32[576,64]{0,1:T(8,128)} async-done(((f32[576,64]{0,1:T(8,128)}), f32[576,64]{0,1:T(8,128)}) %all-reduce.11.cloned.1.call-update) | async-done | bytes 147472 | tf_op jit(solution)/shard_map/psum | solution.py:255
  1030.2 14.7 %pad_maximum_fusion = bf16[8,2,8,64,512]{3,2,4,0,1:T(8,128)(2,1)} fusion(bf16[8,1,8,64,512]{3,2,4,0,1:T(8,128)(2,1)} %bitcast.423, bf16[8,1,8,64,512]{3,2,4,0,1:T(8,128)(2,1)} %bitcast.422), kind=kLoop, calls=%fused_computation.34 | loop fusion | flops 4194304 | bytes 16777216 | tf_op jit(solution)/shard_map/stack | solution.py:209
  1044.9 18.3 %copy.156 = bf16[8,2,8,64,512]{4,3,2,1,0:T(8,128)(2,1)} copy(bf16[8,2,8,64,512]{3,2,4,0,1:T(8,128)(2,1)} %pad_maximum_fusion) | data formatting | bytes 16777216 | tf_op jit(solution)/shard_map/stack | solution.py:209
  1063.3 103.3 %while.23 = (s32[]{:T(128)}, f32[8,64,768]{2,1,0:T(8,128)}, bf16[16,8,64,512]{3,2,1,0:T(8,128)(2,1)}, s32[8,768]{1,0:T(8,128)}, s32[16]{0:T(128)S(1)}, /*index=5*/s32[]{:T(128)}, s32[1]{0:T(128)}, s32[]{:T(128)}) while((s32[]{:T(128)}, f32[8,64,768]{2,1,0:T(8,128)}, bf16[16,8,64,512]{3,2,1,0:T(8,128)(2,1)}, ...), condition=%wide.region_18.19_spmd.clone, body=%wide.region_17.18_spmd.clone.sunk | while | flops 406585856 | bytes 3699323 | solution.py:224
  1166.6 41.4 %fusion.123 = (f32[64]{0:T(128)}, f32[64]{0:T(128)}, f32[8,64,32,768]{3,1,2,0:T(8,128)}) fusion(f32[64]{0:T(128)S(1)} %get-tuple-element.220, f32[64]{0:T(128)S(1)} %get-tuple-element.221, f32[64,8,32,768]{3,0,2,1:T(8,128)} %get-tuple-element.247, f32[8,32,768]{2,1,0:T(8,128)} %fusion.88, f32[8,64,768]{2,1,0:T(8,128)} %get-tuple-element.224, ...), kind=kLoop, calls=%fused_computation.180 | loop fusion | flops 150994816 | bytes 117179904 | tf_op jit(solution)/shard_map/reduce_sum | solution.py:237
  1208.0 42.7 %all-reduce.5 = (f32[64]{0:T(128)S(1)}, f32[64]{0:T(128)S(1)}) all-reduce(f32[64]{0:T(128)} %get-tuple-element.179, f32[64]{0:T(128)} %get-tuple-element.178), channel_id=1, replica_groups=mesh['rows'=8,'scene'=4] {'rows','scene'}, use_global_device_ids=true, to_apply=%region_23.24 | all-reduce | flops 128 | bytes 1024 | tf_op jit(solution)/shard_map/psum | solution.py:235
  1252.6 49.6 %fusion.83 = f32[9,64]{1,0:T(8,128)} fusion(bf16[8,9,32,768]{3,2,1,0:T(8,128)(2,1)S(1)} %copy-done, f32[8,64,32,768]{3,1,2,0:T(8,128)} %get-tuple-element.222, f32[64,8,32,768]{3,0,2,1:T(8,128)} %get-tuple-element.247, f32[64]{0:T(128)} %copy-done.34, f32[64]{0:T(128)} %copy-done.35, f32[]{:T(128)} %get-tuple-element.211, f32[64]{0:T(128)} %get-tuple-element.219, ...), kind=kOutput, calls=%fused_computation.99 | convolution fusion | flops 1459617792 | bytes 104992256 | tf_op jit(solution)/shard_map/sinp,scnp->ic/dot_general | solution.py:252
  1302.3 40.3 %psum.86 = f32[9,64]{1,0:T(8,128)S(1)} all-reduce(f32[9,64]{1,0:T(8,128)} %fusion.83), channel_id=1, replica_groups=mesh['rows'=8,'scene'=4] {'rows','scene'}, use_global_device_ids=true, to_apply=%region_24.25 | all-reduce | flops 576 | bytes 4608 | tf_op jit(solution)/shard_map/psum | solution.py:255
  (238 shorter events, 320.8 us)
Async XLA Ops:
  7.2 4.7 copy-start
  7.2 995.8 %all-reduce.11.cloned.1.call-start = ((), (), s32[]{:S(2)}) async-start(), calls=%async_computation | async-start | bytes 327680 | tf_op jit(solution)/shard_map/psum | solution.py:255
  11.8 496.5 %copy-start.30 = (f32[64]{0:T(128)}, f32[64]{0:T(128)S(1)}, u32[]{:S(2)}) copy-start(f32[64]{0:T(128)S(1)} %get-tuple-element.242) | copy-start | bytes 772
  77.9 1088.7 %copy-start.28 = (f32[64]{0:T(128)}, f32[64]{0:T(128)S(1)}, u32[]{:S(2)}) copy-start(f32[64]{0:T(128)S(1)} %get-tuple-element.220) | copy-start | bytes 772
  77.9 1088.7 %copy-start.29 = (f32[64]{0:T(128)}, f32[64]{0:T(128)S(1)}, u32[]{:S(2)}) copy-start(f32[64]{0:T(128)S(1)} %get-tuple-element.221) | copy-start | bytes 772
  201.5 395.6 %collective-permute-start = (bf16[1,8,64,512]{3,2,1,0:T(8,128)(2,1)}, bf16[1,8,64,512]{3,2,1,0:T(8,128)(2,1)}, u32[]{:S(2)}, u32[]{:S(2)}) collective-permute-start(bf16[1,8,64,512]{3,2,1,0:T(8,128)(2,1)} %slice.131), channel_id=1, source_target_pairs={{0,4},{4,8},{8,12},{12,16},{16,20},{20,24},{24,28},{1,5},{5,9},{9,... | collective-permute-start | bytes 1572872 | tf_op jit(solution)/shard_map/ppermute | solution.py:20
  508.3 29.2 %copy-start.27 = (bf16[72,64]{0,1:T(8,128)(2,1)S(1)}, bf16[72,64]{0,1:T(8,128)(2,1)}, u32[]{:S(2)}) copy-start(bf16[72,64]{0,1:T(8,128)(2,1)} %param.27) | copy-start | bytes 27652
  571.9 4.4 copy-start.3
  576.3 3.6 copy-start.5
  583.5 3.6 copy-start.11
  591.3 5.8 copy-start.19
  746.7 4.5 copy-start.7
  746.7 8.2 copy-start.18
  751.2 3.7 copy-start.17
  805.3 6.0 copy-start.32
  853.4 4.9 copy-start.33
  853.4 4.9 copy-start.8
  858.4 19.6 %copy-start.1 = (bf16[8,8,64,256]{3,2,1,0:T(8,128)(2,1)}, bf16[8,8,64,256]{3,2,1,0:T(8,128)(2,1)S(1)}, u32[]{:S(2)}) copy-start(bf16[8,8,64,256]{3,2,1,0:T(8,128)(2,1)S(1)} %fusion.41) | copy-start | bytes 6291460
  881.2 3.5 copy-start.2
  901.9 104.7 %collective-permute-start.1 = (bf16[1,8,64,256]{3,2,1,0:T(8,128)(2,1)}, bf16[1,8,64,256]{3,2,1,0:T(8,128)(2,1)}, u32[]{:S(2)}, u32[]{:S(2)}) collective-permute-start(bf16[1,8,64,256]{3,2,1,0:T(8,128)(2,1)} %slice.182), channel_id=1, source_target_pairs={{4,0},{8,4},{12,8},{16,12},{20,16},{24,20},{28,24},{5,1},{9,5},{13... | collective-permute-start | bytes 786440 | tf_op jit(solution)/shard_map/ppermute | solution.py:20
  1010.2 2.7 copy-start.16
  1166.6 84.1 %copy-start.26 = (f32[3,4,64]{2,1,0:T(4,128)S(1)}, f32[3,4,64]{2,1,0:T(4,128)}, u32[]{:S(2)}) copy-start(f32[3,4,64]{2,1,0:T(4,128)} %param.26) | copy-start | bytes 9220
  1252.6 89.9 %copy-start.25 = (f32[1,9,64]{2,0,1:T(1,128)S(1)}, f32[1,9,64]{2,0,1:T(1,128)}, u32[]{:S(2)}) copy-start(f32[1,9,64]{2,0,1:T(1,128)} %get-tuple-element.234) | copy-start | bytes 6916
  1343.9 3.3 copy-start.24
  (15 other events, 25.5 us)
Sparse Core Ops, SparseCore 0:
  881.3 121.6 all-reduce.10
where the time goes:
time: 1360 us; the launch traced here: 1350 us
  local copies, waits for them, and re-layouts  536 us (39%)
  matrix products  292 us (21%)
  blocking collectives  237 us (17%)
  other arithmetic  147 us (11%)
  waiting for transfers between devices  99.8 us (7%)
  loops' own time  21.2 us (2%)
  between operations  15.6 us (1%)
    slice x3, local copies, waits for them, and re-layouts, tap_windows(): cols_even = row_block[..., 0::2]  219 us
    slice x3, local copies, waits for them, and re-layouts, tap_windows(): cols_odd = row_block[..., 1::2]  219 us
    psum x1, waiting for transfers between devices, body(): lax.psum((kernel_grad, point_grad), ('rows', 'scene'))  99.8 us
    dot_general x16, matrix products, take_row(): jnp.einsum('scw,spw->scp', row_grad, cell_table(row_index), preferred_ele...  83.3 us
    dot_general x16, matrix products, place_row(): jnp.einsum('scp,spw->scw', pooled_low, cell_table(row_index), preferred_e...  65.3 us
    dot_general x1, matrix products, body(): jnp.einsum('sinp,scnp->ic', points.astype(jnp.float32), lifted_grad, prec...  49.6 us
    dot_general x9, matrix products, body(): jnp.einsum('rscw,co->rsow', windows[tap_row][tap_col], kernels[tap_row, t...  43.2 us
    psum x1, blocking collectives, body(): lax.psum((jnp.sum(backward_point_grad, axis=(0, 2, 3)), jnp.sum(backward_...  42.7 us
  transfers between devices with their start and end apart: 3, of which 1 were waited for; matrix products, arithmetic and copies ran while one was open for 28% of the time, Pallas kernels for 0%

commit v1 on v0

v1 whole, which is shorter than its diff:
```python
import functools

import jax
import jax.numpy as jnp
from jax import lax
from jax.experimental import pallas as pl
from jax.experimental.pallas import tpu as pltpu
from jax.sharding import PartitionSpec as P

beta_one = 0.9
beta_two = 0.999
adam_eps = 1e-08
decay_rate = 0.01
average_keep = 0.99
norm_eps = 1e-05
rate_points = 0.3
rate_norms = 0.2
rate_kernel = 0.04

EDGE = 48
BIG = 1e30
PACK = 16
PAD = 8
f32 = jnp.float32
bf16 = jnp.bfloat16


def iota(shape, dim):
    return lax.broadcasted_iota(jnp.int32, shape, dim)


def dot_nn(a, b):
    return lax.dot_general(a, b, (((1,), (0,)), ((), ())), preferred_element_type=f32)


def dot_nt(a, b):
    return lax.dot_general(a, b, (((1,), (1,)), ((), ())), preferred_element_type=f32)


def dot_tn(a, b):
    return lax.dot_general(a, b, (((0,), (0,)), ((), ())), preferred_element_type=f32)


def split3(x):
    a = x.astype(bf16)
    r = x - a.astype(f32)
    b = r.astype(bf16)
    c = (r - b.astype(f32)).astype(bf16)
    return a, b, c


def column(row, size):
    full = jnp.broadcast_to(row, (128, 128))
    return jnp.transpose(full)[:size]


def wide(row):
    return jnp.concatenate([row, jnp.zeros_like(row)], axis=1)


def lift_tables(weights, table):
    channels = weights.shape[1]
    cols = table.shape[1]
    spread = (iota((16, cols), 1) // PACK == iota((16, cols), 0)).astype(f32).astype(bf16)
    base = dot_tn(weights, spread)
    slot = iota(base.shape, 1) % PACK
    for n in range(PACK):
        table[n * channels : (n + 1) * channels, :] = jnp.where(slot == n, base, 0.0).astype(bf16)


def lift_inputs(points, count, half):
    feats = points.shape[0]
    size = points.shape[2]
    pts = points[:, half * PACK : (half + 1) * PACK, :]
    live = (iota((PACK, size), 0) + half * PACK < count).astype(f32)
    low = live.astype(bf16)
    dead = ((live - 1.0) * BIG).astype(bf16)
    kept = (pts * low[None]).reshape(feats * PACK, size)
    return jnp.concatenate([kept, low, dead], axis=0)


def lift_body(points, counts, pixels, weights, plain, z, edge, stats, moments, table, gram):
    s = pl.program_id(0)
    channels = weights.shape[1]
    feats = points.shape[1]
    depth = points.shape[2]
    size = points.shape[3]
    rows = (feats + 1) * PACK

    @pl.when(s == 0)
    def _():
        lift_tables(weights[...], table)
        gram[...] = jnp.zeros_like(gram)
        edge[...] = jnp.zeros_like(edge)

    count = counts[pl.ds(s, 1), :]
    tile = 256
    quads = PACK // 4
    best = [None] * (size // tile)
    total = None
    for half in range(depth // PACK):
        xin = lift_inputs(points.at[0], count, half)
        part = dot_nt(xin[:rows], xin[:rows])
        total = part if total is None else total + part
        for q in range(quads):
            lhs = table[q * 4 * channels : (q + 1) * 4 * channels, :]
            for t in range(size // tile):
                l = dot_nn(lhs, xin[:, t * tile : (t + 1) * tile])
                m = jnp.maximum(
                    jnp.maximum(l[:channels], l[channels : 2 * channels]),
                    jnp.maximum(l[2 * channels : 3 * channels], l[3 * channels :]),
                )
                best[t] = m if best[t] is None else jnp.maximum(best[t], m)
    gram[...] += total
    for t in range(size // tile):
        z[0, :, t * tile : (t + 1) * tile] = best[t]

    lanes = edge.shape[1]
    pix = pixels[pl.ds(s, 1), :][:, :128].astype(f32)
    flag = jnp.where(iota((8, 128), 0) == 0, pix, 1.0)
    head = jnp.concatenate([best[0][:, :128], flag], axis=0)
    head = jnp.concatenate([head, jnp.zeros((channels + 8, lanes - 128), f32)], axis=1)
    head = pltpu.roll(head, s * EDGE, axis=1)
    lane = iota((channels + 8, lanes), 1)
    edge[...] = jnp.where((lane >= s * EDGE) & (lane < (s + 1) * EDGE), head, edge[...])

    @pl.when(s == pl.num_programs(0) - 1)
    def _():
        g = gram[...]
        g = jnp.where(iota(g.shape, 0) % PACK == iota(g.shape, 1) % PACK, g, 0.0)
        pick = (iota((rows, 128), 0) // PACK == iota((rows, 128), 1)).astype(f32).astype(bf16)
        pick_t = (iota((16, rows), 1) // PACK == iota((16, rows), 0)).astype(f32).astype(bf16)
        a, b, c = split3(g)
        y = dot_nn(a, pick) + (dot_nn(b, pick) + dot_nn(c, pick))
        a, b, c = split3(y)
        m = dot_nn(pick_t, a) + (dot_nn(pick_t, b) + dot_nn(pick_t, c))
        moments[...] = m
        w = plain[...]
        a, b, c = split3(m[:, :16])
        aw = dot_nn(a, w) + (dot_nn(b, w) + dot_nn(c, w))
        two = jnp.sum(aw * w.astype(f32), axis=0, keepdims=True)
        one = aw[feats : feats + 1]
        row = jnp.concatenate([one, two, m[feats : feats + 1]], axis=1)
        stats[...] = jnp.broadcast_to(row, stats.shape)


def lift(points, counts, pixels, weights, plain, peers):
    scenes, feats, depth, size = points.shape
    channels = weights.shape[1]
    cols = (feats + 2) * PACK
    rows = (feats + 1) * PACK
    lanes = scenes * EDGE
    return pl.pallas_call(
        lift_body,
        grid=(scenes,),
        in_specs=[
            pl.BlockSpec((1, feats, depth, size), lambda s: (s, 0, 0, 0)),
            pl.BlockSpec((scenes, size), lambda s: (0, 0)),
            pl.BlockSpec((scenes, size), lambda s: (0, 0)),
            pl.BlockSpec((16, channels), lambda s: (0, 0)),
            pl.BlockSpec((16, channels), lambda s: (0, 0)),
        ],
        out_specs=[
            pl.BlockSpec((1, channels, size), lambda s: (s, 0, 0)),
            pl.BlockSpec((channels + 8, lanes), lambda s: (0, 0)),
            pl.BlockSpec((peers, 256), lambda s: (0, 0)),
            pl.BlockSpec((16, 128), lambda s: (0, 0)),
        ],
        out_shape=[
            jax.ShapeDtypeStruct((scenes, channels, size), f32),
            jax.ShapeDtypeStruct((channels + 8, lanes), f32),
            jax.ShapeDtypeStruct((peers, 256), f32),
            jax.ShapeDtypeStruct((16, 128), f32),
        ],
        scratch_shapes=[
            pltpu.VMEM((PACK * channels, cols), bf16),
            pltpu.VMEM((rows, rows), f32),
        ],
        name="lift",
    )(points, counts, pixels, weights, plain)


def conv_body(idx, stats, z, edge, norm, taps, conv, pooled, sums, params, rows_t, grid, carry, acc):
    s = pl.program_id(0)
    channels = z.shape[1]
    size = z.shape[2]
    out_rows = conv.shape[1]
    wide_cols = conv.shape[3]
    block = wide_cols + PAD
    half = (2 * out_rows + 1) * block

    @pl.when(s == 0)
    def _():
        tot = jnp.sum(stats[:, :256], axis=0, keepdims=True)
        count = tot[:, 137:138]
        mean = tot[:, :channels] / count
        inv = lax.rsqrt(tot[:, channels : 2 * channels] / count - mean * mean + norm_eps)
        params[0] = column(wide(mean), channels)
        params[1] = column(wide(inv), channels)
        nw = norm[...].astype(f32)
        params[2] = column(wide(nw[0:1]), channels)
        params[3] = column(wide(nw[1:2]), channels)
        grid[...] = jnp.zeros_like(grid)
        acc[...] = jnp.zeros_like(acc)

    def pool(x, ok):
        gain = params[2][:, :1]
        sign = jnp.where(gain > 0, 1.0, jnp.where(gain < 0, -1.0, 0.0))
        pre = gain * ((x * sign - params[0][:, :1]) * params[1][:, :1]) + params[3][:, :1]
        return jnp.where(ok, jnp.maximum(pre, 0.0), 0.0).astype(bf16)

    zs = z[0]
    own = pool(zs, zs > -0.5 * BIG)
    lanes = edge.shape[1]
    moved = pltpu.roll(edge[...], (lanes - s * EDGE) % lanes, axis=1)[:, :128]
    ze = moved[:channels]
    ok = (ze > -0.5 * BIG) & (moved[channels + 1 : channels + 2] > 0.5) & (iota((channels, 128), 1) < EDGE)
    far = pool(ze, ok)
    both = jnp.concatenate([own, far], axis=1)
    pooled[0] = both
    wf = both.astype(f32)
    rows_t[...] = jnp.transpose(jnp.concatenate([wf, wf], axis=0))

    step = 16

    def place(i, _):
        for j in range(step):
            p = i * step + j
            grid[pl.ds(idx[0, 0, p], 1), :] = rows_t[pl.ds(p, 1), :]
        return 0

    lax.fori_loop(0, (size + EDGE) // step, place, 0)

    low = iota((wide_cols, 128), 1) < channels

    def window(h):
        base = h * block + PAD
        even = grid[pl.ds(base, wide_cols), :]
        odd = grid[pl.ds(half + base, wide_cols), :]
        prev = grid[pl.ds(half + base - 1, wide_cols), :]
        both = jnp.where(low, even, odd)
        return jnp.concatenate([both, prev], axis=1).astype(bf16)

    def clear(h):
        base = pl.multiple_of(h * block + PAD, 8)
        grid[pl.ds(base, wide_cols), :] = jnp.zeros((wide_cols, 128), f32)
        grid[pl.ds(pl.multiple_of(half + base, 8), wide_cols), :] = jnp.zeros((wide_cols, 128), f32)

    carry[...] = dot_nt(taps[:channels], window(0))
    clear(0)

    def one_row(r, _):
        mid = dot_nt(taps[channels : 2 * channels], window(2 * r + 1))
        last = window(2 * r + 2)
        out = carry[...] + mid + dot_nt(taps[2 * channels :], last)
        carry[...] = dot_nt(taps[:channels], last)
        clear(2 * r + 1)
        clear(2 * r + 2)
        conv[0, r] = out
        square = out * out
        for t in range(wide_cols // 128):
            acc[:channels] += out[:, t * 128 : (t + 1) * 128]
            acc[channels:] += square[:, t * 128 : (t + 1) * 128]
        return 0

    lax.fori_loop(0, out_rows, one_row, 0)

    @pl.when(s == pl.num_programs(0) - 1)
    def _():
        row = jnp.sum(jnp.transpose(acc[...]), axis=0, keepdims=True)
        sums[...] = jnp.broadcast_to(row, sums.shape)


def convolve(idx, stats, z, edge, norm, taps, out_rows, wide_cols):
    scenes, channels, size = z.shape
    peers = stats.shape[0]
    lanes = edge.shape[1]
    block = wide_cols + PAD
    half = (2 * out_rows + 1) * block
    return pl.pallas_call(
        conv_body,
        grid=(scenes,),
        in_specs=[
            pl.BlockSpec((1, 1, idx.shape[2]), lambda s: (s, 0, 0), memory_space=pltpu.SMEM),
            pl.BlockSpec(stats.shape, lambda s: (0, 0)),
            pl.BlockSpec((1, channels, size), lambda s: (s, 0, 0)),
            pl.BlockSpec((channels + 8, lanes), lambda s: (0, 0)),
            pl.BlockSpec((4, channels), lambda s: (0, 0)),
            pl.BlockSpec((3 * channels, 4 * channels), lambda s: (0, 0)),
        ],
        out_specs=[
            pl.BlockSpec((1, out_rows, channels, wide_cols), lambda s: (s, 0, 0, 0)),
            pl.BlockSpec((1, channels, size + 128), lambda s: (s, 0, 0)),
            pl.BlockSpec((peers, 128), lambda s: (0, 0)),
        ],
        out_shape=[
            jax.ShapeDtypeStruct((scenes, out_rows, channels, wide_cols), f32),
            jax.ShapeDtypeStruct((scenes, channels, size + 128), bf16),
            jax.ShapeDtypeStruct((peers, 128), f32),
        ],
        scratch_shapes=[
            pltpu.VMEM((4, channels, 128), f32),
            pltpu.VMEM((size + 128, 128), f32),
            pltpu.VMEM((2 * half, 128), f32),
            pltpu.VMEM((channels, wide_cols), f32),
            pltpu.VMEM((2 * channels, 128), f32),
        ],
        name="convolve",
    )(idx, stats, z, edge, norm, taps)


def conv_params(cells, stats, norm, params):
    channels = params.shape[1]
    tot = jnp.sum(stats[...], axis=0, keepdims=True)
    mean = tot[:, :channels] / cells
    inv = lax.rsqrt(tot[:, channels:] / cells - mean * mean + norm_eps)
    nw = norm[...].astype(f32)
    params[0] = column(wide(mean), channels)
    params[1] = column(wide(inv), channels)
    params[2] = column(wide(nw[2:3]), channels)
    params[3] = column(wide(nw[3:4]), channels)


def norm_body(cells, stats, conv, cot, norm, result, sums, params, acc):
    s = pl.program_id(0)
    channels = conv.shape[2]

    @pl.when(s == 0)
    def _():
        conv_params(cells, stats, norm, params)
        acc[...] = jnp.zeros_like(acc)

    bias = jnp.zeros((channels, 128), f32)
    gain = jnp.zeros((channels, 128), f32)
    for r in range(conv.shape[1]):
        xhat = (conv[0, r] - params[0][:, :1]) * params[1][:, :1]
        pre = params[2][:, :1] * xhat + params[3][:, :1]
        result[r, 0] = jnp.maximum(pre, 0.0).astype(bf16)
        back = jnp.where(pre > 0, cot[r, 0].astype(f32), 0.0)
        prod = back * xhat
        for t in range(conv.shape[3] // 128):
            bias = bias + back[:, t * 128 : (t + 1) * 128]
            gain = gain + prod[:, t * 128 : (t + 1) * 128]
    acc[:channels] += bias
    acc[channels:] += gain

    @pl.when(s == pl.num_programs(0) - 1)
    def _():
        row = jnp.sum(jnp.transpose(acc[...]), axis=0, keepdims=True)
        sums[...] = jnp.broadcast_to(row, sums.shape)


def normalize(cells, stats, conv, cot, norm):
    scenes, out_rows, channels, wide_cols = conv.shape
    peers = stats.shape[0]
    return pl.pallas_call(
        functools.partial(norm_body, cells),
        grid=(scenes,),
        in_specs=[
            pl.BlockSpec((peers, 128), lambda s: (0, 0)),
            pl.BlockSpec((1, out_rows, channels, wide_cols), lambda s: (s, 0, 0, 0)),
            pl.BlockSpec((out_rows, 1, channels, wide_cols), lambda s: (0, s, 0, 0)),
            pl.BlockSpec((4, channels), lambda s: (0, 0)),
        ],
        out_specs=[
            pl.BlockSpec((out_rows, 1, channels, wide_cols), lambda s: (0, s, 0, 0)),
            pl.BlockSpec((peers, 128), lambda s: (0, 0)),
        ],
        out_shape=[
            jax.ShapeDtypeStruct((out_rows, scenes, channels, wide_cols), bf16),
            jax.ShapeDtypeStruct((peers, 128), f32),
        ],
        scratch_shapes=[pltpu.VMEM((4, channels, 128), f32), pltpu.VMEM((2 * channels, 128), f32)],
        name="normalize",
    )(stats, conv, cot, norm)


def grad_body(
    cells, idx, stats, sums, conv, cot, norm, pooled, phase, taps, slots, slots_far, kgrad, params, field, left, right, acc
):
    s = pl.program_id(0)
    channels = conv.shape[2]
    out_rows = conv.shape[1]
    cols = conv.shape[3]
    size = slots.shape[2]

    @pl.when(s == 0)
    def _():
        conv_params(cells, stats, norm, params)
        tot = jnp.sum(sums[...], axis=0, keepdims=True)
        params[4] = column(wide(tot[:, :channels]), channels)
        params[5] = column(wide(tot[:, channels:]), channels)
        params[6] = params[2] * params[1] / cells
        field[...] = jnp.zeros_like(field)
        left[...] = jnp.zeros_like(left)
        right[...] = jnp.zeros_like(right)
        acc[...] = jnp.zeros_like(acc)
        slots_far[...] = jnp.zeros_like(slots_far)

    inside = iota((channels, cols), 1) < cols - 1
    for r in range(out_rows):
        xhat = (conv[0, r] - params[0][:, :1]) * params[1][:, :1]
        pre = params[2][:, :1] * xhat + params[3][:, :1]
        back = jnp.where(pre > 0, cot[r, 0].astype(f32), 0.0)
        grad = params[6][:, :1] * (cells * back - params[4][:, :1] - xhat * params[5][:, :1])
        grad = grad.astype(bf16).astype(f32)
        after = jnp.where(inside, pltpu.roll(grad, cols - 1, axis=1), 0.0)
        field[(r + 1) * cols : (r + 2) * cols, :] = jnp.transpose(jnp.concatenate([grad, after], axis=0))

    step = 16

    def take(i, _):
        for j in range(step):
            p = i * step + j
            k = idx[0, 0, p]
            left[pl.ds(p, 1), :] = field[pl.ds(k, 1), :]
            right[pl.ds(p, 1), :] = field[pl.ds(k + cols, 1), :]
        return 0

    lax.fori_loop(0, (size + EDGE) // step, take, 0)

    total = None
    start = 0
    while start < size + 128:
        tile = min(256, size + 128 - start)
        part = jnp.concatenate([left[start : start + tile], right[start : start + tile]], axis=1).astype(bf16)
        ph = phase[0, :, start : start + tile]
        out = dot_nt(taps[...], part)
        value = jnp.where(
            ph < 2,
            jnp.where(ph == 0, out[:channels], out[channels : 2 * channels]),
            jnp.where(ph == 2, out[2 * channels : 3 * channels], out[3 * channels :]),
        )
        if start < size:
            slots[0, :, start : start + tile] = value
        else:
            lanes = slots_far.shape[1]
            far = jnp.concatenate([value, jnp.zeros((channels, lanes - 128), f32)], axis=1)
            far = pltpu.roll(far, s * EDGE, axis=1)
            lane = iota((channels, lanes), 1)
            slots_far[...] = jnp.where((lane >= s * EDGE) & (lane < (s + 1) * EDGE), far, slots_far[...])
        pf = pooled[0, :, start : start + tile].astype(f32)
        split = jnp.concatenate([jnp.where(ph == k, pf, 0.0) for k in range(4)], axis=0).astype(bf16)
        prod = dot_nn(split, part)
        total = prod if total is None else total + prod
        start += tile
    acc[...] += total

    @pl.when(s == pl.num_programs(0) - 1)
    def _():
        full = acc[...]
        for a in range(3):
            for b in range(3):
                hp, dr = ((1, 1), (0, 0), (1, 0))[a]
                up, dw = ((1, 1), (0, 0), (1, 0))[b]
                row, col = hp * 2 + up, dr * 2 + dw
                tap = 3 * a + b
                kgrad[tap * channels : (tap + 1) * channels, :] = full[
                    row * channels : (row + 1) * channels, col * channels : (col + 1) * channels
                ]


def gradients(cells, idx, stats, sums, conv, cot, norm, pooled, phase, taps):
    scenes, out_rows, channels, wide_cols = conv.shape
    peers = stats.shape[0]
    size = pooled.shape[2] - 128
    lanes = scenes * EDGE
    return pl.pallas_call(
        functools.partial(grad_body, cells),
        grid=(scenes,),
        in_specs=[
            pl.BlockSpec((1, 1, idx.shape[2]), lambda s: (s, 0, 0), memory_space=pltpu.SMEM),
            pl.BlockSpec((peers, 128), lambda s: (0, 0)),
            pl.BlockSpec((peers, 128), lambda s: (0, 0)),
            pl.BlockSpec((1, out_rows, channels, wide_cols), lambda s: (s, 0, 0, 0)),
            pl.BlockSpec((out_rows, 1, channels, wide_cols), lambda s: (0, s, 0, 0)),
            pl.BlockSpec((4, channels), lambda s: (0, 0)),
            pl.BlockSpec((1, channels, size + 128), lambda s: (s, 0, 0)),
            pl.BlockSpec((1, 1, size + 128), lambda s: (s, 0, 0)),
            pl.BlockSpec((4 * channels, 4 * channels), lambda s: (0, 0)),
        ],
        out_specs=[
            pl.BlockSpec((1, channels, size), lambda s: (s, 0, 0)),
            pl.BlockSpec((channels, lanes), lambda s: (0, 0)),
            pl.BlockSpec((9 * channels, channels), lambda s: (0, 0)),
        ],
        out_shape=[
            jax.ShapeDtypeStruct((scenes, channels, size), f32),
            jax.ShapeDtypeStruct((channels, lanes), f32),
            jax.ShapeDtypeStruct((9 * channels, channels), f32),
        ],
        scratch_shapes=[
            pltpu.VMEM((7, channels, 128), f32),
            pltpu.VMEM(((out_rows + 2) * wide_cols, 128), f32),
            pltpu.VMEM((size + 128, 128), f32),
            pltpu.VMEM((size + 128, 128), f32),
            pltpu.VMEM((4 * channels, 4 * channels), f32),
        ],
        name="gradients",
    )(idx, stats, sums, conv, cot, norm, pooled, phase, taps)


def unlift_body(points, counts, weights, z, pooled, slots, slots_far, out, table, acc, mult):
    s = pl.program_id(0)
    channels = weights.shape[1]
    feats = points.shape[1]
    depth = points.shape[2]
    size = points.shape[3]
    cols = (feats + 2) * PACK
    rows = (feats + 1) * PACK

    @pl.when(s == 0)
    def _():
        lift_tables(weights[...], table)
        acc[...] = jnp.zeros_like(acc)

    count = counts[pl.ds(s, 1), :]
    tile = 256
    quads = PACK // 4
    zs = z[0]
    live = zs > -0.5 * BIG
    zs = jnp.where(live, zs, BIG)
    lanes = slots_far.shape[1]
    far = pltpu.roll(slots_far[...], (lanes - s * EDGE) % lanes, axis=1)[:, :128]
    far = jnp.where(iota((channels, 128), 1) < EDGE, far, 0.0)
    raw = slots[0]
    raw = jnp.concatenate([raw[:, :128] + far, raw[:, 128:]], axis=1)
    grad = jnp.where(pooled[0].astype(f32) > 0, raw.astype(bf16).astype(f32), 0.0)

    def visit(fn):
        for half in range(depth // PACK):
            xin = lift_inputs(points.at[0], count, half)
            for q in range(quads):
                lhs = table[q * 4 * channels : (q + 1) * 4 * channels, :]
                pieces = []
                for t in range(size // tile):
                    l = dot_nn(lhs, xin[:, t * tile : (t + 1) * tile])
                    sub = []
                    for k in range(4):
                        sub.append(fn(t, l[k * channels : (k + 1) * channels] == zs[:, t * tile : (t + 1) * tile]))
                    pieces.append(jnp.concatenate(sub, axis=0))
                yield q, xin[:rows], jnp.concatenate(pieces, axis=1)

    def fold(q, prod):
        slot = iota((channels, rows), 1) % PACK
        part = None
        for k in range(4):
            one = jnp.where(slot == q * 4 + k, prod[k * channels : (k + 1) * channels], 0.0)
            part = one if part is None else part + one
        return part

    ties = [jnp.zeros((channels, tile), f32) for _ in range(size // tile)]

    def first(t, win):
        ties[t] = ties[t] + jnp.where(win, 1.0, 0.0)
        return jnp.where(win, grad[:, t * tile : (t + 1) * tile], 0.0)

    total = None
    for q, xin, value in visit(first):
        part = fold(q, dot_nt(value.astype(bf16), xin))
        total = part if total is None else total + part
    acc[...] += total
    most = ties[0]
    for t in range(1, size // tile):
        most = jnp.maximum(most, ties[t])
    for t in range(size // tile):
        mult[:, t * tile : (t + 1) * tile] = ties[t]

    @pl.when(jnp.max(most) > 1.5)
    def _():
        scaled = jnp.where(mult[...] > 1.5, grad / jnp.maximum(mult[...], 1.0) - grad, 0.0)

        def second(t, win):
            return jnp.where(win, scaled[:, t * tile : (t + 1) * tile], 0.0)

        more = None
        for q, xin, value in visit(second):
            a, b, c = split3(value)
            part = fold(q, dot_nt(a, xin) + (dot_nt(b, xin) + dot_nt(c, xin)))
            more = part if more is None else more + part
        acc[...] += more

    @pl.when(s == pl.num_programs(0) - 1)
    def _():
        pick_t = (iota((16, rows), 1) // PACK == iota((16, rows), 0)).astype(f32).astype(bf16)
        a, b, c = split3(acc[...])
        out[...] = dot_nt(pick_t, a) + (dot_nt(pick_t, b) + dot_nt(pick_t, c))


def unlift(points, counts, weights, z, pooled, slots, slots_far):
    scenes, feats, depth, size = points.shape
    channels = weights.shape[1]
    cols = (feats + 2) * PACK
    rows = (feats + 1) * PACK
    lanes = scenes * EDGE
    return pl.pallas_call(
        unlift_body,
        grid=(scenes,),
        in_specs=[
            pl.BlockSpec((1, feats, depth, size), lambda s: (s, 0, 0, 0)),
            pl.BlockSpec((scenes, size), lambda s: (0, 0)),
            pl.BlockSpec((16, channels), lambda s: (0, 0)),
            pl.BlockSpec((1, channels, size), lambda s: (s, 0, 0)),
            pl.BlockSpec((1, channels, size), lambda s: (s, 0, 0)),
            pl.BlockSpec((1, channels, size), lambda s: (s, 0, 0)),
            pl.BlockSpec((channels, lanes), lambda s: (0, 0)),
        ],
        out_specs=pl.BlockSpec((16, channels), lambda s: (0, 0)),
        out_shape=jax.ShapeDtypeStruct((16, channels), f32),
        scratch_shapes=[
            pltpu.VMEM((PACK * channels, cols), bf16),
            pltpu.VMEM((channels, rows), f32),
            pltpu.VMEM((channels, size), f32),
        ],
        name="unlift",
    )(points, counts, weights, z, pooled, slots, slots_far)


def adam_step(master, states, gradient, step_count, step_rate):
    moment = beta_one * states[0] + (1.0 - beta_one) * gradient
    second = beta_two * states[1] + (1.0 - beta_two) * gradient * gradient
    steps_done = step_count[0].astype(jnp.float32)
    first_fix = 1.0 - beta_one**steps_done
    second_fix = 1.0 - beta_two**steps_done
    fresh = master - step_rate * (
        moment / first_fix / (jnp.sqrt(second / second_fix) + adam_eps) + decay_rate * master
    )
    average = average_keep * states[2] + (1.0 - average_keep) * fresh
    return (fresh, jnp.stack([moment, second]), average, fresh.astype(jnp.bfloat16))


def shifted(x, by):
    length = lax.axis_size("rows")
    pairs = [(i, i + by) for i in range(length) if 0 <= i + by < length]
    return lax.ppermute(x, "rows", pairs)


def exchange(x):
    return lax.all_to_all(x, ("rows", "scene"), 0, 0, tiled=True)


def scene_sum(x):
    length = lax.axis_size("scene")
    if length & (length - 1):
        return lax.psum(x, "scene")
    by = 1
    while by < length:
        x = x + lax.ppermute(x, "scene", [(i, i ^ by) for i in range(length)])
        by *= 2
    return x


def body(
    points,
    pillar_counts,
    pillar_pixels,
    point_weight,
    point_master,
    point_states,
    norm_weight,
    norm_master,
    norm_states,
    kernel_weight,
    kernel_master,
    kernel_states,
    step_count,
    cotangent,
):
    feats = points.shape[1]
    size = points.shape[3]
    out_rows, scenes, channels, out_cols = cotangent.shape
    cols = 2 * out_cols
    row_devices = lax.axis_size("rows")
    scene_devices = lax.axis_size("scene")
    peers = row_devices * scene_devices
    cells = float(out_rows * scenes * out_cols * peers)
    own = kernel_weight.shape[0]
    share = own * channels
    cut = scene_devices if share % (scene_devices * 128) == 0 else 1
    mine = lax.axis_index("scene") if cut > 1 else 0

    def my_part(flat):
        return lax.dynamic_index_in_dim(flat.reshape(-1, cut, share // cut), mine, 1, keepdims=False)

    gain_row = norm_weight[0:1].astype(f32)
    sign = jnp.sign(gain_row)
    plain = jnp.zeros((16, channels), f32).at[:feats].set(point_weight.astype(f32))
    signed = (plain * sign).at[feats + 1].set(1.0).astype(bf16)
    plain = plain.astype(bf16)

    z, edge, stats, moments = lift(points, pillar_counts, pillar_pixels, signed, plain, peers)
    edge = shifted(edge, 1)
    kpart = my_part(kernel_weight.astype(f32).reshape(1, share))
    got = exchange(jnp.concatenate([stats, jnp.broadcast_to(kpart, (peers, share // cut))], axis=1))
    stats = got[:, :256]
    kern = got[:, 256:].reshape(row_devices, scene_devices, share // cut)
    if cut == 1:
        kern = kern[:, :1]
    kern = kern.reshape(3, 3, channels, channels)

    far_pixels = edge[channels].reshape(scenes, EDGE).astype(jnp.int32)
    far_row = jnp.full((scenes, EDGE), -1, jnp.int32)
    row_at = jnp.concatenate([pillar_pixels // cols, far_row], axis=1)
    col_at = jnp.concatenate([pillar_pixels % cols, far_pixels % cols], axis=1)
    odd_col = col_at % 2
    at = col_at // 2
    place_at = odd_col * ((2 * out_rows + 1) * (out_cols + PAD)) + (row_at + 1) * (out_cols + PAD) + PAD + at
    take_at = ((row_at + 2) // 2) * out_cols + at
    phase = (row_at % 2) * 2 + odd_col
    phase = jnp.pad(phase, ((0, 0), (0, 128 - EDGE)))

    back_taps = jnp.transpose(kern, (0, 3, 1, 2))
    zero = jnp.zeros((3, channels, channels), f32)
    fore = jnp.stack([back_taps[:, :, 1], back_taps[:, :, 2], back_taps[:, :, 0], zero], axis=2)
    fore = fore.reshape(3 * channels, 4 * channels).astype(bf16)
    blocks = []
    none = jnp.zeros((channels, channels), f32)
    tap_of = ((1, None), (2, 0))
    for hp in range(2):
        for up in range(2):
            line = []
            for dr in range(2):
                for dw in range(2):
                    a, b = tap_of[hp][dr], tap_of[up][dw]
                    line.append(none if a is None or b is None else kern[a, b])
            blocks.append(jnp.concatenate(line, axis=1))
    aft = jnp.concatenate(blocks, axis=0).astype(bf16)

    conv, pooled, sums = convolve(place_at[:, None], stats, z, edge, norm_weight, fore, out_rows, out_cols)
    conv_stats = exchange(sums)
    result, sums = normalize(cells, conv_stats, conv, cotangent, norm_weight)
    grad_sums = exchange(sums)
    slots, slots_far, kgrad = gradients(
        cells, take_at[:, None], conv_stats, grad_sums, conv, cotangent, norm_weight, pooled, phase[:, None], aft
    )
    slots_far = shifted(slots_far, -1)
    kgrad = scene_sum(kgrad)
    cross = unlift(points, pillar_counts, signed, z, pooled, slots, slots_far)

    kpart = my_part(kgrad.reshape(row_devices, share))
    kpart = jnp.broadcast_to(kpart[:, None], (row_devices, scene_devices, share // cut)).reshape(peers, -1)
    rest = jnp.concatenate([cross[: feats + 1].reshape(-1), moments[: feats + 1, :16].reshape(-1)])
    pad = -rest.shape[0] % 128
    rest = jnp.broadcast_to(jnp.pad(rest, (0, pad))[None], (peers, rest.shape[0] + pad))
    got = exchange(jnp.concatenate([kpart, rest], axis=1))
    kernel_own = jnp.sum(got[:, : share // cut].reshape(row_devices, scene_devices, share // cut), axis=0)
    if cut == 1:
        kernel_own = kernel_own[:1]
    kernel_own = kernel_own.reshape(own, channels)
    rest = jnp.sum(got[:, share // cut :], axis=0)
    cross = rest[: (feats + 1) * channels].reshape(feats + 1, channels)
    moments = rest[(feats + 1) * channels : (feats + 1) * (channels + 16)].reshape(feats + 1, 16)[:, : feats + 1]

    weight = point_weight.astype(f32)
    total = moments[feats, feats]
    firsts = moments[:feats, feats]
    mixed = jnp.sum(moments[:feats, :feats, None] * weight[None], axis=1)
    mean = jnp.sum(firsts[:, None] * weight, axis=0) / total
    inv = lax.rsqrt(jnp.sum(mixed * weight, axis=0) / total - mean * mean + norm_eps)
    bias_p = cross[feats]
    gain_p = inv * (jnp.sum(weight * cross[:feats], axis=0) - mean * bias_p)
    spread = inv * (mixed - firsts[:, None] * mean)
    point_total = (norm_weight[0].astype(f32) * inv) * (
        cross[:feats] - (firsts[:, None] * bias_p + spread * gain_p) / total
    )
    both = jnp.sum(grad_sums, axis=0)
    norm_grad = jnp.stack([gain_p, bias_p, both[channels:], both[:channels]])

    outs = [result]
    outs += adam_step(point_master, point_states, point_total, step_count, rate_points)
    outs += adam_step(norm_master, norm_states, norm_grad, step_count, rate_norms)
    outs += adam_step(kernel_master, kernel_states, kernel_own, step_count, rate_kernel)
    return tuple(outs)


def solution(mesh):
    placed = (
        P("scene", None, None, "rows"),
        P("scene", "rows"),
        P("scene", "rows"),
        P(),
        P(),
        P(),
        P(),
        P(),
        P(),
        P("rows", None),
        P("rows", None),
        P(None, "rows", None),
        P(),
        P("rows", "scene", None, None),
    )
    return jax.shard_map(
        body,
        mesh=mesh,
        in_specs=placed,
        out_specs=(
            P("rows", "scene", None, None),
            P(),
            P(),
            P(),
            P(),
            P(),
            P(),
            P(),
            P(),
            P("rows", None),
            P(None, "rows", None),
            P("rows", None),
            P("rows", None),
        ),
        check_vma=False,
    )
```

time: 1360 us -> 185 us (0.14)
  local copies, waits for them, and re-layouts: 536 us -> 15.3 us
  matrix products: 292 us -> 0 us
  blocking collectives: 237 us -> 0 us
  other arithmetic: 147 us -> 10.4 us
  Pallas kernels: 0 us -> 98.4 us
  waiting for transfers between devices: 99.8 us -> 30.2 us
  loops' own time: 21.2 us -> 0 us
  starting transfers between devices: 6.53 us -> 27.2 us
  between operations: 15.6 us -> 1.85 us
    slice x13 -> x10, local copies, waits for them, and re-layouts: 454 us -> 1.57 us  [the longest x1 0.62 us: body(): stats = got[:, :256]]
    dot_general x61 -> x0, matrix products: 292 us -> none  [the longest x16 83.3 us: take_row(): jnp.einsum('scw,spw->scp', row_grad, cell_table(row_index), preferred_ele...]
    psum x5 -> x0, blocking collectives: 204 us -> none  [the longest x1 42.7 us: body(): lax.psum((jnp.sum(backward_point_grad, axis=(0, 2, 3)), jnp.sum(backward_...]
    psum x1 -> x0, waiting for transfers between devices: 99.8 us -> none  [body(): lax.psum((kernel_grad, point_grad), ('rows', 'scene'))]
    pallas_call x0 -> x5, Pallas kernels: none -> 98.4 us  [the longest x1 31.3 us: convolve(): pl.pallas_call(conv_body, grid=(scenes,), in_specs=[pl.BlockSpec((1, 1, i...]
    reduce_sum x4 -> x5, other arithmetic: 78.1 us -> 0.29 us  [the longest x1 0.09 us: body(): mixed = jnp.sum(moments[:feats, :feats, None] * weight[None], axis=1)]
    another operation x3 -> x8, local copies, waits for them, and re-layouts: 40.2 us -> 1.48 us  [the longest x3 1.02 us: my_part(): flat.reshape(-1, cut, share // cut)]
    all_gather x1 -> x0, blocking collectives: 32.7 us -> none  [body(): kernel_full = lax.all_gather(kernel_weight, 'rows', axis=0, tiled=True)]
  transfers between devices with their start and end apart: 3 -> 8, of which waited for: 1 -> 6; matrix products, arithmetic and copies ran while one was open for 28% -> 3% of each run, Pallas kernels for 0% -> 10%
where the time goes in v1:
time: 185 us; the launch traced here: 183 us
  Pallas kernels  98.4 us (53%)
  waiting for transfers between devices  30.2 us (16%)
  starting transfers between devices  27.2 us (15%)
  local copies, waits for them, and re-layouts  15.3 us (8%)
  other arithmetic  10.4 us (6%)
  between operations  1.85 us (1%)
    pallas_call x1, Pallas kernels, convolve(): pl.pallas_call(conv_body, grid=(scenes,), in_specs=[pl.BlockSpec((1, 1, i...  31.3 us
    pallas_call x1, Pallas kernels, gradients(): pl.pallas_call(functools.partial(grad_body, cells), grid=(scenes,), in_sp...  28.7 us
    all_to_all x4, waiting for transfers between devices, exchange(): return lax.all_to_all(x, ('rows', 'scene'), 0, 0, tiled=True)  22.6 us
    all_to_all x4, starting transfers between devices, exchange(): return lax.all_to_all(x, ('rows', 'scene'), 0, 0, tiled=True)  21.4 us
    pallas_call x1, Pallas kernels, unlift(): pl.pallas_call(unlift_body, grid=(scenes,), in_specs=[pl.BlockSpec((1, fe...  18.3 us
    pallas_call x1, Pallas kernels, lift(): pl.pallas_call(lift_body, grid=(scenes,), in_specs=[pl.BlockSpec((1, feat...  12.1 us
    pallas_call x1, Pallas kernels, normalize(): pl.pallas_call(functools.partial(norm_body, cells), grid=(scenes,), in_sp...  8.05 us
    ppermute x2, waiting for transfers between devices, shifted(): return lax.ppermute(x, 'rows', pairs)  7.22 us
  transfers between devices with their start and end apart: 8, of which 6 were waited for; matrix products, arithmetic and copies ran while one was open for 3% of the time, Pallas kernels for 10%

profile of v1, /device:TPU:0, one launch (start us, length us, event | category | flops | bytes accessed | tf_op | source)
XLA Modules:
  0.0 183.3 jit_solution(5515262351736314843)
XLA Ops:
  2.0 0.8 copy.87
  4.2 12.1 %lift.1 = (f32[8,64,768]{2,1,0:T(8,128)}, f32[72,384]{1,0:T(8,128)}, f32[32,256]{1,0:T(8,128)}, f32[16,128]{1,0:T(8,128)}) custom-call(bf16[8,9,32,768]{3,2,1,0:T(8,128)(2,1)} %points.3, s32[8,768]{1,0:T(8,128)} %counts.3, s32[8,768]{1,0:T(8,128)} %pixels.1, bf16[16,64]{1,0:T(8,128)(2,1)} %copy-done.7, bf16[16,64]{1,0:T(8,128)(2,1)} %get-tuple-element.164.plain), custom_call_target="tpu_custom_call" | custom-call | tf_op jit(solution)/shard_map/lift/pallas_call | solution.py:153
  17.1 0.8 all_to_all.30
  17.9 7.3 %all-to-all-start = ((f32[32,1,1408]{2,1,0:T(1,128)}), f32[32,1,1408]{2,1,0:T(1,128)S(1)}, u32[]{:S(2)}, u32[]{:S(2)}) async-start(f32[32,1,1408]{2,1,0:T(1,128)} %all_to_all.30), calls=%async_computation | async-start | bytes 360448 | tf_op jit(solution)/shard_map/all_to_all | solution.py:639
  25.2 3.7 %collective-permute-start = (f32[72,384]{1,0:T(8,128)}, f32[72,384]{1,0:T(8,128)S(1)}, u32[]{:S(2)}, u32[]{:S(2)}) collective-permute-start(f32[72,384]{1,0:T(8,128)} %get-tuple-element.49), channel_id=1, source_target_pairs={{0,4},{4,8},{8,12},{12,16},{16,20},{20,24},{24,28},{1,5},{5,9},{9,... | collective-permute-start | bytes 331784 | tf_op jit(solution)/shard_map/ppermute | solution.py:635
  29.0 3.4 %collective-permute-done.edge = f32[72,384]{1,0:T(8,128)S(1)} collective-permute-done((f32[72,384]{1,0:T(8,128)}, f32[72,384]{1,0:T(8,128)S(1)}, u32[]{:S(2)}, u32[]{:S(2)}) %collective-permute-start) | collective-permute-done | bytes 110624 | tf_op jit(solution)/shard_map/ppermute | solution.py:635
  35.6 0.8 convert_element_type.49.taps
  36.4 31.3 %convolve.1 = (f32[8,8,64,256]{3,2,1,0:T(8,128)}, bf16[8,64,896]{2,1,0:T(8,128)(2,1)}, f32[32,128]{1,0:T(8,128)}) custom-call(s32[8,1,816]{2,1,0:T(1,128)} %copy.89.idx, f32[32,256]{1,0:T(8,128)} %slice.225.stats, f32[8,64,768]{2,1,0:T(8,128)} %get-tuple-element.51.z, f32[72,384]{1,0:T(8,128)} %copy-done.3, bf16[4,64]{1,0:T(4,128)(2,1)} %norm.5, ...), custom_call_target="tpu_custom_call" | custom-call | tf_op jit(solution)/shard_map/convolve/pallas_call | solution.py:280
  67.7 6.1 %all-to-all-start.1 = ((f32[32,1,128]{2,1,0:T(1,128)}), f32[32,1,128]{2,1,0:T(1,128)S(1)}, u32[]{:S(2)}, u32[]{:S(2)}) async-start(f32[32,1,128]{2,1,0:T(1,128)} %bitcast.152), calls=%async_computation.1 | async-start | bytes 32768 | tf_op jit(solution)/shard_map/all_to_all | solution.py:639
  73.8 7.1 %all-to-all-done.1 = f32[32,1,128]{2,1,0:T(1,128)S(1)} async-done(((f32[32,1,128]{2,1,0:T(1,128)}), f32[32,1,128]{2,1,0:T(1,128)S(1)}, u32[]{:S(2)}, u32[]{:S(2)}) %all-to-all-start.1) | async-done | bytes 16416 | tf_op jit(solution)/shard_map/all_to_all | solution.py:639
  81.4 8.0 %normalize.1 = (bf16[8,8,64,256]{3,2,1,0:T(8,128)(2,1)}, f32[32,128]{1,0:T(8,128)}) custom-call(f32[32,128]{1,0:T(8,128)} %bitcast.144, f32[8,8,64,256]{3,2,1,0:T(8,128)} %get-tuple-element.53.conv, bf16[8,8,64,256]{3,2,1,0:T(8,128)(2,1)} %cot.3, bf16[4,64]{1,0:T(4,128)(2,1)} %norm.5), custom_call_target="tpu_custom_call" | custom-call | tf_op jit(solution)/shard_map/normalize/pallas_call | solution.py:356
  89.5 2.5 %all-to-all-start.2 = ((f32[32,1,128]{2,1,0:T(1,128)}), f32[32,1,128]{2,1,0:T(1,128)S(1)}, u32[]{:S(2)}, u32[]{:S(2)}) async-start(f32[32,1,128]{2,1,0:T(1,128)} %bitcast.153), calls=%async_computation.2 | async-start | bytes 32768 | tf_op jit(solution)/shard_map/all_to_all | solution.py:639
  92.1 0.8 fusion.3.taps
  92.8 6.3 %all-to-all-done.2 = f32[32,1,128]{2,1,0:T(1,128)S(1)} async-done(((f32[32,1,128]{2,1,0:T(1,128)}), f32[32,1,128]{2,1,0:T(1,128)S(1)}, u32[]{:S(2)}, u32[]{:S(2)}) %all-to-all-start.2) | async-done | bytes 16416 | tf_op jit(solution)/shard_map/all_to_all | solution.py:639
  99.7 28.7 %gradients.1 = (f32[8,64,768]{2,1,0:T(8,128)}, f32[64,384]{1,0:T(8,128)}, f32[576,64]{1,0:T(8,128)}) custom-call(s32[8,1,816]{2,1,0:T(1,128)} %copy.93.idx, f32[32,128]{1,0:T(8,128)} %bitcast.145, f32[32,128]{1,0:T(8,128)} %bitcast.146, f32[8,8,64,256]{3,2,1,0:T(8,128)} %get-tuple-element.53.conv, bf16[8,8,64,256]{3,2,1,0:T(8,128)(2,1)} %cot.3, ...), custom_call_target="tpu_custom_call" | custom-call | tf_op jit(solution)/shard_map/gradients/pallas_call | solution.py:468
  128.5 1.5 collective-permute-start.3
  130.3 1.0 add.196
  132.0 3.8 %collective-permute-done.3.slots_far = f32[64,384]{1,0:T(8,128)S(1)} collective-permute-done((f32[64,384]{1,0:T(8,128)}, f32[64,384]{1,0:T(8,128)S(1)}, u32[]{:S(2)}, u32[]{:S(2)}) %collective-permute-start.3) | collective-permute-done | bytes 98336 | tf_op jit(solution)/shard_map/ppermute | solution.py:635
  136.5 18.3 %unlift.1 = f32[16,64]{1,0:T(8,128)} custom-call(bf16[8,9,32,768]{3,2,1,0:T(8,128)(2,1)} %points.3, s32[8,768]{1,0:T(8,128)} %counts.3, bf16[16,64]{1,0:T(8,128)(2,1)} %copy-done.7, f32[8,64,768]{2,1,0:T(8,128)} %get-tuple-element.51.z, bf16[8,64,896]{2,1,0:T(8,128)(2,1)} %get-tuple-element.56.pooled, f32[8,64,768]{2,1,0:T(8,128)} %get-tuple-element.58.slots, ...), custom_call_target="tpu_custom_call" | custom-call | tf_op jit(solution)/shard_map/unlift/pallas_call | solution.py:596
  154.8 0.8 reshape.783
  156.1 0.9 all_to_all.39
  157.0 5.5 %all-to-all-start.3 = ((f32[32,1,2048]{2,1,0:T(1,128)}), f32[32,1,2048]{2,1,0:T(1,128)S(1)}, u32[]{:S(2)}, u32[]{:S(2)}) async-start(f32[32,1,2048]{2,1,0:T(1,128)} %all_to_all.39), calls=%async_computation.3 | async-start | bytes 524288 | tf_op jit(solution)/shard_map/all_to_all | solution.py:639
  163.7 9.3 %all-to-all-done.3 = f32[32,1,2048]{2,1,0:T(1,128)S(1)} async-done(((f32[32,1,2048]{2,1,0:T(1,128)}), f32[32,1,2048]{2,1,0:T(1,128)S(1)}, u32[]{:S(2)}, u32[]{:S(2)}) %all-to-all-start.3) | async-done | bytes 262176 | tf_op jit(solution)/shard_map/all_to_all | solution.py:639
  180.8 1.3 fusion.56
  (122 shorter events, 19.4 us)
Async XLA Ops:
  4.2 24.7 %copy-start.5 = (s32[8,768]{1,0:T(8,128)S(1)}, s32[8,768]{1,0:T(8,128)}, u32[]{:S(2)}) copy-start(s32[8,768]{1,0:T(8,128)} %pixels.1) | copy-start | bytes 73732
  17.9 16.6 %all-to-all-start = ((f32[32,1,1408]{2,1,0:T(1,128)}), f32[32,1,1408]{2,1,0:T(1,128)S(1)}, u32[]{:S(2)}, u32[]{:S(2)}) async-start(f32[32,1,1408]{2,1,0:T(1,128)} %all_to_all.30), calls=%async_computation | async-start | bytes 360448 | tf_op jit(solution)/shard_map/all_to_all | solution.py:639
  25.2 7.2 %collective-permute-start = (f32[72,384]{1,0:T(8,128)}, f32[72,384]{1,0:T(8,128)S(1)}, u32[]{:S(2)}, u32[]{:S(2)}) collective-permute-start(f32[72,384]{1,0:T(8,128)} %get-tuple-element.49), channel_id=1, source_target_pairs={{0,4},{4,8},{8,12},{12,16},{16,20},{20,24},{24,28},{1,5},{5,9},{9,... | collective-permute-start | bytes 331784 | tf_op jit(solution)/shard_map/ppermute | solution.py:635
  32.4 4.0 %copy-start.3 = (f32[72,384]{1,0:T(8,128)}, f32[72,384]{1,0:T(8,128)S(1)}, u32[]{:S(2)}) copy-start(f32[72,384]{1,0:T(8,128)S(1)} %collective-permute-done.edge) | copy-start | bytes 331780
  67.7 13.2 %all-to-all-start.1 = ((f32[32,1,128]{2,1,0:T(1,128)}), f32[32,1,128]{2,1,0:T(1,128)S(1)}, u32[]{:S(2)}, u32[]{:S(2)}) async-start(f32[32,1,128]{2,1,0:T(1,128)} %bitcast.152), calls=%async_computation.1 | async-start | bytes 32768 | tf_op jit(solution)/shard_map/all_to_all | solution.py:639
  80.8 0.6 copy-start
  89.5 9.6 %all-to-all-start.2 = ((f32[32,1,128]{2,1,0:T(1,128)}), f32[32,1,128]{2,1,0:T(1,128)S(1)}, u32[]{:S(2)}, u32[]{:S(2)}) async-start(f32[32,1,128]{2,1,0:T(1,128)} %bitcast.153), calls=%async_computation.2 | async-start | bytes 32768 | tf_op jit(solution)/shard_map/all_to_all | solution.py:639
  99.7 32.2 %copy-start.15 = (f32[16,128]{1,0:T(8,128)S(1)}, f32[16,128]{1,0:T(8,128)}, u32[]{:S(2)}) copy-start(f32[16,128]{1,0:T(8,128)} %get-tuple-element.60) | copy-start | bytes 24580
  128.4 1.9 %collective-permute-start.1 = (f32[576,64]{1,0:T(8,128)}, f32[576,64]{1,0:T(8,128)S(1)}, u32[]{:S(2)}, u32[]{:S(2)}) collective-permute-start(f32[576,64]{1,0:T(8,128)} %get-tuple-element.57), channel_id=1, source_target_pairs={{0,1},{1,0},{2,3},{3,2},{4,5},{5,4},{6,7},{7,6},{8,9},{9,8},{10,11... | collective-permute-start | bytes 442376 | tf_op jit(solution)/shard_map/ppermute | solution.py:648
  128.5 7.3 %collective-permute-start.3 = (f32[64,384]{1,0:T(8,128)}, f32[64,384]{1,0:T(8,128)S(1)}, u32[]{:S(2)}, u32[]{:S(2)}) collective-permute-start(f32[64,384]{1,0:T(8,128)} %get-tuple-element.59), channel_id=1, source_target_pairs={{4,0},{8,4},{12,8},{16,12},{20,16},{24,20},{28,24},{5,1},{9,5},{13... | collective-permute-start | bytes 294920 | tf_op jit(solution)/shard_map/ppermute | solution.py:635
  131.3 24.3 %collective-permute-start.2 = (f32[576,64]{1,0:T(8,128)S(1)}, f32[576,64]{1,0:T(8,128)S(1)}, u32[]{:S(2)}, u32[]{:S(2)}) collective-permute-start(f32[576,64]{1,0:T(8,128)S(1)} %add.196), channel_id=1, source_target_pairs={{0,2},{1,3},{2,0},{3,1},{4,6},{5,7},{6,4},{7,5},{8,10},{9,11},{10,... | collective-permute-start | bytes 442376 | tf_op jit(solution)/shard_map/ppermute | solution.py:648
  135.8 0.6 copy-start.4
  154.8 7.7 %copy-start.6 = (f32[3,72,64]{1,2,0:T(8,128)S(1)}, f32[3,72,64]{1,2,0:T(8,128)}, u32[]{:S(2)}) copy-start(f32[3,72,64]{1,2,0:T(8,128)} %param.29) | copy-start | bytes 165892
  154.8 8.6 %copy-start.8 = (f32[72,64]{0,1:T(8,128)S(1)}, f32[72,64]{0,1:T(8,128)}, u32[]{:S(2)}) copy-start(f32[72,64]{0,1:T(8,128)} %param.28) | copy-start | bytes 55300
  154.8 8.8 %copy-start.13 = (f32[3,9,64]{2,0,1:T(4,128)S(1)}, f32[3,9,64]{2,0,1:T(4,128)}, u32[]{:S(2)}) copy-start(f32[3,9,64]{2,0,1:T(4,128)} %param.23) | copy-start | bytes 20740
  154.8 8.8 %copy-start.2 = (f32[32,1,128]{2,1,0:T(1,128)S(1)}, f32[32,1,128]{2,1,0:T(1,128)}, u32[]{:S(2)}) copy-start(f32[32,1,128]{2,1,0:T(1,128)} %copy-done.1) | copy-start | bytes 49156
  156.0 21.4 %copy-start.11 = (bf16[9,64]{1,0:T(8,128)(2,1)S(1)}, bf16[9,64]{1,0:T(8,128)(2,1)}, u32[]{:S(2)}) copy-start(bf16[9,64]{1,0:T(8,128)(2,1)} %param.21) | copy-start | bytes 3460
  156.0 21.5 %copy-start.12 = (bf16[4,64]{1,0:T(4,128)(2,1)S(1)}, bf16[4,64]{1,0:T(4,128)(2,1)}, u32[]{:S(2)}) copy-start(bf16[4,64]{1,0:T(4,128)(2,1)} %norm.5) | copy-start | bytes 1540
  156.0 22.2 %copy-start.10 = (f32[3,4,64]{2,1,0:T(4,128)S(1)}, f32[3,4,64]{2,1,0:T(4,128)}, u32[]{:S(2)}) copy-start(f32[3,4,64]{2,1,0:T(4,128)} %param.26) | copy-start | bytes 9220
  156.1 22.2 %copy-start.17 = (f32[4,64]{1,0:T(4,128)S(1)}, f32[4,64]{1,0:T(4,128)}, u32[]{:S(2)}) copy-start(f32[4,64]{1,0:T(4,128)} %param.25) | copy-start | bytes 3076
  156.1 24.7 %copy-start.14 = (f32[9,64]{1,0:T(8,128)S(1)}, f32[9,64]{1,0:T(8,128)}, u32[]{:S(2)}) copy-start(f32[9,64]{1,0:T(8,128)} %param.22) | copy-start | bytes 6916
  157.0 16.1 %all-to-all-start.3 = ((f32[32,1,2048]{2,1,0:T(1,128)}), f32[32,1,2048]{2,1,0:T(1,128)S(1)}, u32[]{:S(2)}, u32[]{:S(2)}) async-start(f32[32,1,2048]{2,1,0:T(1,128)} %all_to_all.39), calls=%async_computation.3 | async-start | bytes 524288 | tf_op jit(solution)/shard_map/all_to_all | solution.py:639
  178.9 4.5 %copy-start.16 = (f32[4,64]{1,0:T(4,128)}, f32[4,64]{1,0:T(4,128)S(1)}, u32[]{:S(2)}) copy-start(f32[4,64]{1,0:T(4,128)S(1)} %get-tuple-element.132) | copy-start | bytes 3076
  182.1 1.2 copy-start.9
  (2 other events, 1.2 us)

commit v2 on v0

v2 whole, which is shorter than its diff:
```python
import functools

import jax
import jax.numpy as jnp
from jax import lax
from jax.experimental import pallas as pl
from jax.experimental.pallas import tpu as pltpu
from jax.sharding import PartitionSpec as P

beta_one = 0.9
beta_two = 0.999
adam_eps = 1e-08
decay_rate = 0.01
average_keep = 0.99
norm_eps = 1e-05
rate_points = 0.3
rate_norms = 0.2
rate_kernel = 0.04

EDGE = 48
BIG = 1e30
PACK = 16
TILE = 256
LANES = 128
f32 = jnp.float32
bf16 = jnp.bfloat16


def iota(shape, dim):
    return lax.broadcasted_iota(jnp.int32, shape, dim)


def dot_nn(a, b):
    return lax.dot_general(a, b, (((1,), (0,)), ((), ())), preferred_element_type=f32)


def dot_nt(a, b):
    return lax.dot_general(a, b, (((1,), (1,)), ((), ())), preferred_element_type=f32)


def dot_tn(a, b):
    return lax.dot_general(a, b, (((0,), (0,)), ((), ())), preferred_element_type=f32)


def split3(x):
    a = x.astype(bf16)
    r = x - a.astype(f32)
    b = r.astype(bf16)
    c = (r - b.astype(f32)).astype(bf16)
    return a, b, c


def exact_left(x, y):
    a, b, c = split3(x)
    return dot_nn(a, y) + (dot_nn(b, y) + dot_nn(c, y))


def exact_right(x, y):
    a, b, c = split3(y)
    return dot_nn(x, a) + (dot_nn(x, b) + dot_nn(x, c))


def swap_halves(x):
    return pltpu.roll(x, x.shape[1] // 2, axis=1)


def twice(row):
    return jnp.concatenate([row, row], axis=1)


def one_hot_rows(rows, cols):
    return (iota((rows, cols), 0) // PACK == iota((rows, cols), 1)).astype(f32).astype(bf16)


def one_hot_cols(rows, cols):
    return (iota((rows, cols), 1) // PACK == iota((rows, cols), 0)).astype(f32).astype(bf16)


def lift_table(weight, norm, table):
    feats, channels = weight.shape
    rows = table.shape[0]
    gain = norm[0:1, :].astype(f32)
    sign = jnp.where(gain > 0, 1.0, jnp.where(gain < 0, -1.0, 0.0))
    signed = weight[...].astype(f32) * sign
    full = jnp.concatenate([signed, jnp.zeros((1, channels), f32), jnp.ones((1, channels), f32)], axis=0)
    full = jnp.concatenate([full, jnp.zeros((16 - feats - 2, channels), f32)], axis=0)
    base = dot_nn(one_hot_rows(rows, 16), twice(full).astype(bf16))
    slot = iota(base.shape, 0) % PACK
    half = iota(base.shape, 1) // channels
    for m in range(PACK // 2):
        table[:, m * LANES : (m + 1) * LANES] = jnp.where(slot == 2 * m + half, base, 0.0).astype(bf16)


def lift_inputs(points, count, half):
    feats = points.shape[0]
    size = points.shape[2]
    pts = points[:, half * PACK : (half + 1) * PACK, :]
    live = (iota((PACK, size), 0) + half * PACK < count).astype(f32)
    low = live.astype(bf16)
    dead = ((live - 1.0) * BIG).astype(bf16)
    kept = (pts * low[None]).reshape(feats * PACK, size)
    return jnp.concatenate([kept, low, dead], axis=0)


def lift_body(mine, points, counts, pixels, weight, norm, kernel, z, edge, payload, moments, table, gram, best, wide):
    s = pl.program_id(0)
    scenes = pl.num_programs(0)
    feats, channels = weight.shape
    depth = points.shape[2]
    size = points.shape[3]
    rows = (feats + 1) * PACK

    @pl.when(s == 0)
    def _():
        lift_table(weight, norm, table)
        gram[...] = jnp.zeros_like(gram)
        edge[...] = jnp.zeros_like(edge)
        wide[...] = kernel[...].astype(f32)

    count = counts[pl.ds(s, 1), :]
    tiles = size // TILE
    total = None
    for half in range(depth // PACK):
        xin = lift_inputs(points.at[0], count, half)
        part = dot_nt(xin[:rows], xin[:rows])
        total = part if total is None else total + part
        turned = [jnp.transpose(xin[:, t * TILE : (t + 1) * TILE]) for t in range(tiles)]
        for q in range(PACK // 4):
            rhs = table[:, q * 256 : (q + 1) * 256]
            for t in range(tiles):
                l = dot_nn(turned[t], rhs)
                m = jnp.maximum(l[:, :LANES], l[:, LANES:])
                at = slice(t * TILE, (t + 1) * TILE)
                if half == 0 and q == 0:
                    best[at, :] = m
                elif half == depth // PACK - 1 and q == PACK // 4 - 1:
                    m = jnp.maximum(best[at, :], m)
                    m = jnp.maximum(m, swap_halves(m))
                    z[0, at, :] = m
                else:
                    best[at, :] = jnp.maximum(best[at, :], m)
    gram[...] += total

    lower = iota((EDGE, LANES), 1) < channels
    spot = pl.ds(pl.multiple_of((s % (scenes // 2)) * EDGE, 8), EDGE)
    first = s < scenes // 2
    edge[spot, :] = jnp.where(lower == first, z[0, :EDGE, :], edge[spot, :])

    @pl.when(s == scenes - 1)
    def _():
        count_rows = edge.shape[0] - 2 * scenes
        edge[count_rows : count_rows + scenes, :] = pixels[:, :LANES].astype(f32)
        edge[count_rows + scenes :, :] = jnp.ones((scenes, LANES), f32)
        g = gram[...]
        g = jnp.where(iota(g.shape, 0) % PACK == iota(g.shape, 1) % PACK, g, 0.0)
        y = exact_left(g, one_hot_rows(rows, LANES))
        m = exact_right(one_hot_cols(16, rows), y)
        moments[...] = m
        w = jnp.concatenate([weight[...].astype(f32), jnp.zeros((16 - feats, channels), f32)], axis=0)
        aw = exact_left(m[:, :16], w.astype(bf16))
        two = jnp.sum(aw * w, axis=0, keepdims=True)
        one = aw[feats : feats + 1]
        pieces = [one, two, m[feats : feats + 1]]
        share = (payload.shape[1] - 256) // channels
        for j in range(share):
            pieces.append(wide[pl.ds(mine[0, 0] * share + j, 1), :])
        payload[...] = jnp.broadcast_to(jnp.concatenate(pieces, axis=1), payload.shape)


def lift(mine, points, counts, pixels, weight, norm, kernel, peers, share):
    scenes, feats, depth, size = points.shape
    channels = weight.shape[1]
    full = (feats + 2) * PACK
    rows = (feats + 1) * PACK
    edge_rows = scenes // 2 * EDGE + 2 * scenes
    fixed = lambda s: (0, 0)
    return pl.pallas_call(
        lift_body,
        grid=(scenes,),
        in_specs=[
            pl.BlockSpec((1, 1), fixed, memory_space=pltpu.SMEM),
            pl.BlockSpec((1, feats, depth, size), lambda s: (s, 0, 0, 0)),
            pl.BlockSpec((scenes, size), fixed),
            pl.BlockSpec((scenes, size), fixed),
            pl.BlockSpec(weight.shape, fixed),
            pl.BlockSpec(norm.shape, fixed),
            pl.BlockSpec(kernel.shape, fixed),
        ],
        out_specs=[
            pl.BlockSpec((1, size, LANES), lambda s: (s, 0, 0)),
            pl.BlockSpec((edge_rows, LANES), fixed),
            pl.BlockSpec((peers, 256 + share), fixed),
            pl.BlockSpec((16, LANES), fixed),
        ],
        out_shape=[
            jax.ShapeDtypeStruct((scenes, size, LANES), f32),
            jax.ShapeDtypeStruct((edge_rows, LANES), f32),
            jax.ShapeDtypeStruct((peers, 256 + share), f32),
            jax.ShapeDtypeStruct((16, LANES), f32),
        ],
        scratch_shapes=[
            pltpu.VMEM((full, PACK * channels), bf16),
            pltpu.VMEM((rows, rows), f32),
            pltpu.VMEM((size, LANES), f32),
            pltpu.VMEM(kernel.shape, f32),
        ],
        name="lift",
    )(mine, points, counts, pixels, weight, norm, kernel)


def gather_kernel(got, kern, devices, parts):
    channels = kern.shape[1]
    share = kern.shape[0] // devices // parts
    peers = got.shape[0]
    for j in range(share):
        lanes = slice(256 + j * channels, 256 + (j + 1) * channels)
        if parts > 1:
            kern[pl.ds(j, peers, stride=share), :] = got[:, lanes]
        else:
            for r in range(devices):
                at = r * (peers // devices)
                kern[r * share + j : r * share + j + 1, :] = got[at : at + 1, lanes]


def tap(kern, a, b):
    channels = kern.shape[1]
    if a is None or b is None:
        return jnp.zeros((channels, channels), f32)
    return kern[(3 * a + b) * channels : (3 * a + b + 1) * channels, :]


def edge_rows_of(block, s, scenes, lower):
    spot = pl.ds(pl.multiple_of((s % (scenes // 2)) * EDGE, 8), EDGE)
    rows = jnp.where(lower == (s < scenes // 2), block[spot, :], 0.0)
    return rows + swap_halves(rows)


def conv_body(
    devices, parts, pix, far_pix, got, z, edge, norm, conv, pooled, sums, kernel, params, source, kern, taps, grid_a, grid_b, side, acc
):
    i = pl.program_id(0)
    scenes = pl.num_programs(0) - 1
    s = jnp.minimum(i, scenes - 1)
    channels = norm.shape[1]
    size = z.shape[1]
    pairs = conv.shape[1]
    out_cols = conv.shape[2]
    cols = 2 * out_cols
    last_row = (4 * pairs - 1) * cols
    strip = out_cols + 8

    @pl.when(i == 0)
    def _():
        tot = jnp.sum(got[:, :256], axis=0, keepdims=True)
        count = tot[:, 2 * channels + 9 : 2 * channels + 10]
        mean = tot[:, :channels] / count
        inv = lax.rsqrt(tot[:, channels : 2 * channels] / count - mean * mean + norm_eps)
        nw = norm[...].astype(f32)
        gain = nw[0:1]
        sign = jnp.where(gain > 0, 1.0, jnp.where(gain < 0, -1.0, 0.0))
        params[0:1] = twice(mean)
        params[1:2] = twice(inv)
        params[2:3] = twice(gain)
        params[3:4] = twice(nw[1:2])
        params[4:5] = twice(sign)
        gather_kernel(got, kern, devices, parts)
        kernel[...] = kern[...].astype(bf16)
        for w, (low, high) in enumerate(((0, None), (1, None), (2, 0), (None, 1), (None, 2))):
            none = tap(kern, None, None)
            top = jnp.concatenate([tap(kern, low, 1), tap(kern, high, 1), none, none], axis=1)
            end = jnp.concatenate(
                [tap(kern, low, 2), tap(kern, high, 2), tap(kern, low, 0), tap(kern, high, 0)], axis=1
            )
            taps[w] = jnp.concatenate([top, end], axis=0).astype(bf16)
        source[...] = jnp.zeros_like(source)
        grid_a[...] = jnp.zeros_like(grid_a)
        grid_b[...] = jnp.zeros_like(grid_b)
        side[...] = jnp.zeros_like(side)
        acc[...] = jnp.zeros_like(acc)

    def pool(x, ok):
        pre = params[2:3] * ((x * params[4:5] - params[0:1]) * params[1:2]) + params[3:4]
        return jnp.where(ok, jnp.maximum(pre, 0.0), 0.0).astype(bf16)

    def work(dst, src):
        zs = z[0]
        own = pool(zs, zs > -0.5 * BIG)
        pooled[0, :size] = own
        source[:size] = own.astype(f32)
        far = edge_rows_of(edge, s, scenes, iota((EDGE, LANES), 1) < channels)
        flag = edge[edge.shape[0] - scenes : edge.shape[0] - scenes + 1, :]
        far = pool(far, (far > -0.5 * BIG) & (flag > 0.5))
        pooled[0, size:] = jnp.concatenate([far, jnp.zeros((LANES - EDGE, LANES), bf16)], axis=0)
        source[size : size + EDGE] = far.astype(f32)

        for p in range(size):
            dst[pl.ds(pix[s, p] + (8 + cols), 1), :] = source[p : p + 1, :]
        for p in range(EDGE):
            at = jnp.maximum(far_pix[s, p], last_row)
            dst[pl.ds(at + (8 - last_row), 1), :] = source[size + p : size + p + 1, :]

        left = iota((out_cols, LANES), 1) < channels

        def window(h):
            base = 8 + (h + 1) * cols
            even = src[pl.ds(base, out_cols, stride=2), :]
            odd = src[pl.ds(base + 1, out_cols, stride=2), :]
            return jnp.where(left, even, odd).astype(bf16)

        held = window(-1)
        for j in range(pairs):
            out = dot_nn(held, taps[0])
            for w in range(1, 5):
                held = window(4 * j - 1 + w)
                out = out + dot_nn(held, taps[w])
            side[j * strip + 8 : (j + 1) * strip, :] = out[:, LANES:]
            value = out[:, :LANES] + side[j * strip + 7 : j * strip + 7 + out_cols, :]
            conv[0, j] = value
            acc[0:8] += jnp.sum(value.reshape(out_cols // 8, 8, LANES), axis=0)
            acc[8:16] += jnp.sum((value * value).reshape(out_cols // 8, 8, LANES), axis=0)
        src[...] = jnp.zeros_like(src)

    @pl.when(i % 2 == 0)
    def _():
        work(grid_a, grid_b)

    @pl.when(i % 2 == 1)
    def _():
        work(grid_b, grid_a)

    @pl.when(i == scenes)
    def _():
        sums[...] = jnp.broadcast_to(both_sums(acc, channels), sums.shape)


def both_sums(acc, channels):
    one = jnp.sum(acc[0:8], axis=0, keepdims=True)
    two = jnp.sum(acc[8:16], axis=0, keepdims=True)
    one = one + swap_halves(one)
    two = two + swap_halves(two)
    return jnp.where(iota((1, LANES), 1) < channels, one, two)


def convolve(devices, parts, pix, far_pix, got, z, edge, norm, pairs, out_cols):
    scenes, size, _ = z.shape
    peers = got.shape[0]
    channels = norm.shape[1]
    cells = 8 + (4 * pairs + 1) * 2 * out_cols + 8
    fixed = lambda i: (0, 0)
    now = lambda i: (jnp.minimum(i, scenes - 1), 0, 0)
    return pl.pallas_call(
        functools.partial(conv_body, devices, parts),
        grid=(scenes + 1,),
        in_specs=[
            pl.BlockSpec(pix.shape, fixed, memory_space=pltpu.SMEM),
            pl.BlockSpec(far_pix.shape, fixed, memory_space=pltpu.SMEM),
            pl.BlockSpec(got.shape, fixed),
            pl.BlockSpec((1, size, LANES), now),
            pl.BlockSpec(edge.shape, fixed),
            pl.BlockSpec(norm.shape, fixed),
        ],
        out_specs=[
            pl.BlockSpec((1, pairs, out_cols, LANES), lambda i: (jnp.maximum(i - 1, 0), 0, 0, 0)),
            pl.BlockSpec((1, size + LANES, LANES), now),
            pl.BlockSpec((peers, LANES), fixed),
            pl.BlockSpec((9 * channels, channels), fixed),
        ],
        out_shape=[
            jax.ShapeDtypeStruct((scenes, pairs, out_cols, LANES), f32),
            jax.ShapeDtypeStruct((scenes, size + LANES, LANES), bf16),
            jax.ShapeDtypeStruct((peers, LANES), f32),
            jax.ShapeDtypeStruct((9 * channels, channels), bf16),
        ],
        scratch_shapes=[
            pltpu.VMEM((8, LANES), f32),
            pltpu.VMEM((size + LANES, LANES), f32),
            pltpu.VMEM((9 * channels, channels), f32),
            pltpu.VMEM((5, LANES, 2 * LANES), bf16),
            pltpu.VMEM((cells, LANES), f32),
            pltpu.VMEM((cells, LANES), f32),
            pltpu.VMEM((pairs * (out_cols + 8), LANES), f32),
            pltpu.VMEM((16, LANES), f32),
        ],
        name="convolve",
    )(pix, far_pix, got, z, edge, norm)


def split_sums(stats, channels):
    tot = jnp.sum(stats[...], axis=0, keepdims=True)
    lower = iota((1, LANES), 1) < channels
    turned = swap_halves(tot)
    return jnp.where(lower, tot, turned), jnp.where(lower, turned, tot)


def conv_params(cells, stats, norm):
    one, two = split_sums(stats, norm.shape[1])
    mean = one / cells
    inv = lax.rsqrt(two / cells - mean * mean + norm_eps)
    nw = norm[...].astype(f32)
    return mean, inv, twice(nw[2:3]), twice(nw[3:4])


def turned_pair(block, j, k):
    _, _, channels, cols = block.shape
    return jnp.transpose(block[2 * j : 2 * j + 2, k].reshape(2 * channels, cols)).astype(f32)


def norm_body(cells, stats, conv, cot, norm, result, sums, acc):
    i = pl.program_id(0)
    channels = norm.shape[1]
    scenes, pairs, out_cols, _ = conv.shape
    mean, inv, gain, bias = conv_params(cells, stats, norm)

    @pl.when(i == 0)
    def _():
        acc[...] = jnp.zeros_like(acc)

    for k in range(scenes):
        for j in range(pairs):
            xhat = (conv[k, j] - mean) * inv
            pre = gain * xhat + bias
            out = jnp.transpose(jnp.maximum(pre, 0.0).astype(bf16))
            result[2 * j : 2 * j + 2, k] = out.reshape(2, channels, out_cols)
            back = jnp.where(pre > 0, turned_pair(cot, j, k), 0.0)
            acc[0:8] += jnp.sum(back.reshape(out_cols // 8, 8, LANES), axis=0)
            acc[8:16] += jnp.sum((back * xhat).reshape(out_cols // 8, 8, LANES), axis=0)

    @pl.when(i == pl.num_programs(0) - 1)
    def _():
        sums[...] = jnp.broadcast_to(both_sums(acc, channels), sums.shape)


def normalize(cells, stats, conv, cot, norm):
    scenes, pairs, out_cols, _ = conv.shape
    rows, _, channels, _ = cot.shape
    peers = stats.shape[0]
    chunk = 2
    fixed = lambda i: (0, 0)
    return pl.pallas_call(
        functools.partial(norm_body, cells),
        grid=(scenes // chunk,),
        in_specs=[
            pl.BlockSpec((peers, LANES), fixed),
            pl.BlockSpec((chunk, pairs, out_cols, LANES), lambda i: (i, 0, 0, 0)),
            pl.BlockSpec((rows, chunk, channels, out_cols), lambda i: (0, i, 0, 0)),
            pl.BlockSpec(norm.shape, fixed),
        ],
        out_specs=[
            pl.BlockSpec((rows, chunk, channels, out_cols), lambda i: (0, i, 0, 0)),
            pl.BlockSpec((peers, LANES), fixed),
        ],
        out_shape=[
            jax.ShapeDtypeStruct(cot.shape, bf16),
            jax.ShapeDtypeStruct((peers, LANES), f32),
        ],
        scratch_shapes=[pltpu.VMEM((16, LANES), f32)],
        name="normalize",
    )(stats, conv, cot, norm)


def grad_body(
    cells, devices, parts, idx, stats, sums, conv, cot, norm, pooled, phase, kernel, slots, far, kgrad, taps, field_a, field_b, taken, acc, rows_k
):
    i = pl.program_id(0)
    scenes = pl.num_programs(0) - 1
    s = jnp.maximum(i - 1, 0)
    channels = norm.shape[1]
    pairs = conv.shape[1]
    out_cols = conv.shape[2]
    size = slots.shape[1]
    strip = out_cols + 8

    @pl.when(i == 0)
    def _():
        for hp in range(2):
            for up in range(2):
                line = []
                for dw in range(2):
                    for dr in range(2):
                        a = ((1, None), (2, 0))[hp][dr]
                        b = ((1, None), (2, 0))[up][dw]
                        if a is None or b is None:
                            line.append(jnp.zeros((channels, channels), f32))
                        else:
                            at = (3 * a + b) * channels
                            line.append(kernel[at : at + channels, :].astype(f32))
                ph = 2 * hp + up
                taps[ph * channels : (ph + 1) * channels, :] = jnp.concatenate(line, axis=1).astype(bf16)
        field_a[...] = jnp.zeros_like(field_a)
        field_b[...] = jnp.zeros_like(field_b)
        taken[...] = jnp.zeros_like(taken)
        acc[...] = jnp.zeros_like(acc)
        far[...] = jnp.zeros_like(far)

    mean, inv, gain, bias = conv_params(cells, stats, norm)
    bias_grad, gain_grad = split_sums(sums, channels)
    scale = gain * inv / cells

    def work(dst, src):
        left = iota((out_cols, LANES), 1) < channels
        before = jnp.zeros((out_cols, LANES), f32)
        for j in range(pairs):
            xhat = (conv[0, j] - mean) * inv
            pre = gain * xhat + bias
            back = jnp.where(pre > 0, turned_pair(cot, j, 0), 0.0)
            grad = scale * (cells * back - bias_grad - xhat * gain_grad)
            grad = grad.astype(bf16).astype(f32)
            turned = swap_halves(grad)
            dst[2 * j * strip : 2 * j * strip + out_cols, :] = jnp.where(left, before, turned)
            dst[(2 * j + 1) * strip : (2 * j + 1) * strip + out_cols, :] = grad
            before = turned
        dst[2 * pairs * strip : 2 * pairs * strip + out_cols, :] = jnp.where(left, before, 0.0)

        for p in range(size + EDGE):
            taken[2 * p : 2 * p + 2, :] = src[pl.ds(idx[s, p], 2), :]

        total = None
        start = 0
        while start < size + LANES:
            tile = min(TILE, size + LANES - start)
            zero_w = taken[pl.ds(2 * start, tile, stride=2), :]
            one_w = taken[pl.ds(2 * start + 1, tile, stride=2), :]
            part = jnp.concatenate([zero_w, one_w], axis=1).astype(bf16)
            out = dot_nt(part, taps[...])
            ph = []
            for c in range(tile // LANES):
                row = phase[0, :, start + c * LANES : start + (c + 1) * LANES]
                ph.append(jnp.transpose(jnp.broadcast_to(row, (LANES, LANES))))
            ph = jnp.concatenate(ph, axis=0)
            half = (iota((tile, LANES), 1) >= channels).astype(f32)
            is_even = ph == half
            is_odd = ph == half + 2.0
            value = jnp.where(is_even, out[:, :LANES], 0.0) + jnp.where(is_odd, out[:, LANES:], 0.0)
            value = value + swap_halves(value)
            pf = pooled[0, start : start + tile, :].astype(f32)
            value = jnp.where(pf > 0, value, 0.0)
            if start < size:
                slots[0, start : start + tile, :] = value
            else:
                spot = pl.ds(pl.multiple_of((s % (scenes // 2)) * EDGE, 8), EDGE)
                lower = iota((EDGE, LANES), 1) < channels
                far[spot, :] = jnp.where(lower == (s < scenes // 2), value[:EDGE], far[spot, :])
            split = jnp.concatenate([jnp.where(is_even, pf, 0.0), jnp.where(is_odd, pf, 0.0)], axis=1)
            prod = dot_tn(split.astype(bf16), part)
            total = prod if total is None else total + prod
            start += tile
        acc[...] += total

    @pl.when(i % 2 == 0)
    def _():
        work(field_a, field_b)

    @pl.when(i % 2 == 1)
    def _():
        work(field_b, field_a)

    @pl.when(i == scenes)
    def _():
        for a in range(3):
            for b in range(3):
                hp, dr = ((1, 1), (0, 0), (1, 0))[a]
                up, dw = ((1, 1), (0, 0), (1, 0))[b]
                row, col = hp * 2 + up, dw * 2 + dr
                at = (3 * a + b) * channels
                rows_k[at : at + channels, :] = acc[
                    row * channels : (row + 1) * channels, col * channels : (col + 1) * channels
                ]
        own = rows_k.shape[0] // devices
        share = own // parts
        for q in range(parts):
            for j in range(share):
                lanes = slice(j * channels, (j + 1) * channels)
                kgrad[q * devices : (q + 1) * devices, lanes] = rows_k[pl.ds(q * share + j, devices, stride=own), :]


def gradients(cells, devices, parts, idx, stats, sums, conv, cot, norm, pooled, phase, kernel):
    scenes, pairs, out_cols, _ = conv.shape
    rows, _, channels, _ = cot.shape
    peers = stats.shape[0]
    size = pooled.shape[1] - LANES
    fixed = lambda i: (0, 0)
    return pl.pallas_call(
        functools.partial(grad_body, cells, devices, parts),
        grid=(scenes + 1,),
        in_specs=[
            pl.BlockSpec(idx.shape, fixed, memory_space=pltpu.SMEM),
            pl.BlockSpec((peers, LANES), fixed),
            pl.BlockSpec((peers, LANES), fixed),
            pl.BlockSpec((1, pairs, out_cols, LANES), lambda i: (jnp.minimum(i, scenes - 1), 0, 0, 0)),
            pl.BlockSpec((rows, 1, channels, out_cols), lambda i: (0, jnp.minimum(i, scenes - 1), 0, 0)),
            pl.BlockSpec(norm.shape, fixed),
            pl.BlockSpec((1, size + LANES, LANES), lambda i: (jnp.maximum(i - 1, 0), 0, 0)),
            pl.BlockSpec((1, 1, size + LANES), lambda i: (jnp.maximum(i - 1, 0), 0, 0)),
            pl.BlockSpec(kernel.shape, fixed),
        ],
        out_specs=[
            pl.BlockSpec((1, size, LANES), lambda i: (jnp.maximum(i - 1, 0), 0, 0)),
            pl.BlockSpec((scenes // 2 * EDGE, LANES), fixed),
            pl.BlockSpec((parts * devices, 9 * channels * channels // devices // parts), fixed),
        ],
        out_shape=[
            jax.ShapeDtypeStruct((scenes, size, LANES), f32),
            jax.ShapeDtypeStruct((scenes // 2 * EDGE, LANES), f32),
            jax.ShapeDtypeStruct((parts * devices, 9 * channels * channels // devices // parts), f32),
        ],
        scratch_shapes=[
            pltpu.VMEM((4 * channels, 4 * channels), bf16),
            pltpu.VMEM(((2 * pairs + 1) * (out_cols + 8), LANES), f32),
            pltpu.VMEM(((2 * pairs + 1) * (out_cols + 8), LANES), f32),
            pltpu.VMEM((2 * (size + LANES), LANES), f32),
            pltpu.VMEM((4 * channels, 4 * channels), f32),
            pltpu.VMEM((9 * channels, channels), f32),
        ],
        name="gradients",
    )(idx, stats, sums, conv, cot, norm, pooled, phase, kernel)


def unlift_body(points, counts, weight, norm, z, slots, far, moments, rest, table, acc, mult):
    s = pl.program_id(0)
    scenes = pl.num_programs(0)
    feats, channels = weight.shape
    depth = points.shape[2]
    size = points.shape[3]
    rows = (feats + 1) * PACK
    tiles = size // TILE

    @pl.when(s == 0)
    def _():
        lift_table(weight, norm, table)
        acc[...] = jnp.zeros_like(acc)

    count = counts[pl.ds(s, 1), :]
    extra = edge_rows_of(far, s, scenes, iota((EDGE, LANES), 1) < channels)
    best, grad = [], []
    for t in range(tiles):
        at = slice(t * TILE, (t + 1) * TILE)
        zs = z[0, at, :]
        best.append(jnp.where(zs > -0.5 * BIG, zs, BIG))
        raw = slots[0, at, :]
        if t == 0:
            raw = jnp.concatenate([raw[:EDGE] + extra, raw[EDGE:]], axis=0)
        grad.append(raw.astype(bf16).astype(f32))

    def visit(fn):
        for half in range(depth // PACK):
            xin = lift_inputs(points.at[0], count, half)
            turned = [jnp.transpose(xin[:, t * TILE : (t + 1) * TILE]) for t in range(tiles)]
            for q in range(PACK // 4):
                rhs = table[:, q * 256 : (q + 1) * 256]
                total = None
                for t in range(tiles):
                    l = dot_nn(turned[t], rhs)
                    total = fn(t, l, xin[:rows, t * TILE : (t + 1) * TILE], total)
                yield q, total

    def fold(q, prod):
        slot = iota((rows, LANES), 0) % PACK - 4 * q
        upper = (iota((rows, LANES), 1) >= channels).astype(jnp.int32)
        return jnp.where(slot == upper, prod[:, :LANES], 0.0) + jnp.where(slot == upper + 2, prod[:, LANES:], 0.0)

    ties = [jnp.zeros((TILE, LANES), f32) for _ in range(tiles)]

    def first(t, l, xin, total):
        one = l[:, :LANES] == best[t]
        two = l[:, LANES:] == best[t]
        ties[t] = ties[t] + (jnp.where(one, 1.0, 0.0) + jnp.where(two, 1.0, 0.0))
        value = jnp.concatenate([jnp.where(one, grad[t], 0.0), jnp.where(two, grad[t], 0.0)], axis=1)
        part = dot_nn(xin, value.astype(bf16))
        return part if total is None else total + part

    for q, total in visit(first):
        acc[...] += fold(q, total)
    most = None
    for t in range(tiles):
        both = ties[t] + swap_halves(ties[t])
        mult[t * TILE : (t + 1) * TILE, :] = both
        most = both if most is None else jnp.maximum(most, both)

    @pl.when(jnp.max(most) > 1.5)
    def _():
        def second(t, l, xin, total):
            many = mult[t * TILE : (t + 1) * TILE, :]
            scaled = jnp.where(many > 1.5, grad[t] / jnp.maximum(many, 1.0) - grad[t], 0.0)
            one = jnp.where(l[:, :LANES] == best[t], scaled, 0.0)
            two = jnp.where(l[:, LANES:] == best[t], scaled, 0.0)
            part = exact_right(xin, jnp.concatenate([one, two], axis=1))
            return part if total is None else total + part

        for q, total in visit(second):
            acc[...] += fold(q, total)

    @pl.when(s == scenes - 1)
    def _():
        out = exact_right(one_hot_cols(16, rows), acc[...])
        out = out + swap_halves(out)
        pieces = [out[i : i + 1, :channels] for i in range(feats + 1)]
        pieces += [moments[i : i + 1, :16] for i in range(feats + 1)]
        width = (feats + 1) * (channels + 16)
        pieces.append(jnp.zeros((1, rest.shape[1] - width), f32))
        rest[...] = jnp.concatenate(pieces, axis=1)


def unlift(points, counts, weight, norm, z, slots, far, moments):
    scenes, feats, depth, size = points.shape
    channels = weight.shape[1]
    full = (feats + 2) * PACK
    rows = (feats + 1) * PACK
    width = -(-(feats + 1) * (channels + 16) // LANES) * LANES
    fixed = lambda s: (0, 0)
    return pl.pallas_call(
        unlift_body,
        grid=(scenes,),
        in_specs=[
            pl.BlockSpec((1, feats, depth, size), lambda s: (s, 0, 0, 0)),
            pl.BlockSpec((scenes, size), fixed),
            pl.BlockSpec(weight.shape, fixed),
            pl.BlockSpec(norm.shape, fixed),
            pl.BlockSpec((1, size, LANES), lambda s: (s, 0, 0)),
            pl.BlockSpec((1, size, LANES), lambda s: (s, 0, 0)),
            pl.BlockSpec(far.shape, fixed),
            pl.BlockSpec(moments.shape, fixed),
        ],
        out_specs=pl.BlockSpec((1, width), fixed),
        out_shape=jax.ShapeDtypeStruct((1, width), f32),
        scratch_shapes=[
            pltpu.VMEM((full, PACK * channels), bf16),
            pltpu.VMEM((rows, LANES), f32),
            pltpu.VMEM((size, LANES), f32),
        ],
        name="unlift",
    )(points, counts, weight, norm, z, slots, far, moments)


def adam(fixes, master, states, grad, rate, fresh, moments, average, copy):
    w = master[...]
    moment = beta_one * states[0] + (1.0 - beta_one) * grad
    second = beta_two * states[1] + (1.0 - beta_two) * grad * grad
    new = w - rate * (moment / fixes[0] / (jnp.sqrt(second / fixes[1]) + adam_eps) + decay_rate * w)
    fresh[...] = new
    moments[0] = moment
    moments[1] = second
    average[...] = average_keep * states[2] + (1.0 - average_keep) * new
    copy[...] = new.astype(bf16)


def step_body(devices, parts, fix, got, sums, weight, norm, *refs):
    pm, ps, nm, ns, km, ks = refs[:6]
    outs = refs[6:18]
    kgrad = refs[18]
    feats, channels = weight.shape
    own = km.shape[0]
    share = own // parts
    peers = got.shape[0]
    scenes = peers // devices
    fixes = (fix[0], fix[1])

    width = share * channels
    tot = None
    for r in range(devices):
        part = got[r * scenes : (r + 1) * scenes, :width]
        tot = part if tot is None else tot + part
    for j in range(share):
        piece = tot[:parts, j * channels : (j + 1) * channels]
        if parts > 1:
            kgrad[pl.ds(j, parts, stride=share), :] = piece
        else:
            kgrad[j : j + 1, :] = piece
    adam(fixes, km, ks, kgrad[...], rate_kernel, *outs[8:12])

    row = jnp.sum(got[:, width:], axis=0, keepdims=True)
    cross = jnp.concatenate([row[:, i * channels : (i + 1) * channels] for i in range(feats + 1)], axis=0)
    base = (feats + 1) * channels
    moments = jnp.concatenate([row[:, base + i * 16 : base + (i + 1) * 16] for i in range(feats + 1)], axis=0)
    w = weight[...].astype(f32)
    nw = norm[...].astype(f32)
    total = moments[feats : feats + 1, feats : feats + 1]
    firsts = moments[:feats, feats : feats + 1]
    mixed = None
    first_sum = None
    for i in range(feats):
        part = moments[:feats, i : i + 1] * w[i : i + 1]
        mixed = part if mixed is None else mixed + part
        part = moments[feats : feats + 1, i : i + 1] * w[i : i + 1]
        first_sum = part if first_sum is None else first_sum + part
    mean = first_sum / total
    inv = lax.rsqrt(jnp.sum(mixed * w, axis=0, keepdims=True) / total - mean * mean + norm_eps)
    bias_p = cross[feats : feats + 1]
    gain_p = inv * (jnp.sum(w * cross[:feats], axis=0, keepdims=True) - mean * bias_p)
    spread = inv * (mixed - firsts * mean)
    point_grad = (nw[0:1] * inv) * (cross[:feats] - (firsts * bias_p + spread * gain_p) / total)
    adam(fixes, pm, ps, point_grad, rate_points, *outs[0:4])
    both = jnp.sum(sums[...], axis=0, keepdims=True)
    norm_grad = jnp.concatenate([gain_p, bias_p, both[:, channels:], both[:, :channels]], axis=0)
    adam(fixes, nm, ns, norm_grad, rate_norms, *outs[4:8])


def update(devices, parts, fix, got, sums, weight, norm, pm, ps, nm, ns, km, ks):
    shapes = []
    for m in (pm, nm, km):
        shapes.append(jax.ShapeDtypeStruct(m.shape, f32))
        shapes.append(jax.ShapeDtypeStruct((2,) + m.shape, f32))
        shapes.append(jax.ShapeDtypeStruct(m.shape, f32))
        shapes.append(jax.ShapeDtypeStruct(m.shape, bf16))
    vmem = pl.BlockSpec(memory_space=pltpu.VMEM)
    return pl.pallas_call(
        functools.partial(step_body, devices, parts),
        in_specs=[pl.BlockSpec(memory_space=pltpu.SMEM)] + [vmem] * 10,
        out_specs=[vmem] * 12,
        out_shape=shapes,
        scratch_shapes=[pltpu.VMEM(km.shape, f32)],
        name="update",
    )(fix, got, sums, weight, norm, pm, ps, nm, ns, km, ks)


def shifted(x, by):
    length = lax.axis_size("rows")
    pairs = [(i, i + by) for i in range(length) if 0 <= i + by < length]
    return lax.ppermute(x, "rows", pairs)


def exchange(x):
    return lax.all_to_all(x, ("rows", "scene"), 0, 0, tiled=True)


def body(
    points,
    pillar_counts,
    pillar_pixels,
    point_weight,
    point_master,
    point_states,
    norm_weight,
    norm_master,
    norm_states,
    kernel_weight,
    kernel_master,
    kernel_states,
    step_count,
    cotangent,
):
    size = points.shape[3]
    out_rows, scenes, channels, out_cols = cotangent.shape
    cols = 2 * out_cols
    devices = lax.axis_size("rows")
    scene_devices = lax.axis_size("scene")
    peers = devices * scene_devices
    cells = float(out_rows * scenes * out_cols * peers)
    own = kernel_weight.shape[0]
    parts = scene_devices if own % scene_devices == 0 else 1
    share = own // parts * channels
    mine = lax.axis_index("scene") if parts > 1 else jnp.int32(0)

    z, edge, stats, moments = lift(
        mine.reshape(1, 1), points, pillar_counts, pillar_pixels, point_weight, norm_weight, kernel_weight, peers, share
    )
    edge = shifted(edge, 1)
    got = exchange(stats)
    held = scenes // 2 * EDGE
    far_pixels = edge[held : held + scenes].astype(jnp.int32)
    conv, pooled, sums, kernel = convolve(
        devices, parts, pillar_pixels, far_pixels, got, z, edge, norm_weight, out_rows // 2, out_cols
    )
    conv_stats = exchange(sums)

    far_pixels = far_pixels[:, :EDGE]
    at = (pillar_pixels % cols) // 2
    own_at = (pillar_pixels // (2 * cols) + 1) * (out_cols + 8) + at
    take_at = jnp.concatenate([own_at, (far_pixels % cols) // 2], axis=1)
    own_phase = (pillar_pixels // cols % 2) * 2 + pillar_pixels % 2
    phase = jnp.concatenate([own_phase, 2 + far_pixels % 2], axis=1)
    phase = jnp.pad(phase, ((0, 0), (0, LANES - EDGE))).astype(f32)[:, None]

    result, sums = normalize(cells, conv_stats, conv, cotangent, norm_weight)
    grad_sums = exchange(sums)
    slots, far, kgrad = gradients(
        cells, devices, parts, take_at, conv_stats, grad_sums, conv, cotangent, norm_weight, pooled, phase, kernel
    )
    far = shifted(far, -1)
    if parts > 1:
        kgrad = lax.all_to_all(kgrad, "scene", 0, 0, tiled=True)
    else:
        kgrad = lax.psum(kgrad, "scene")
    rest = unlift(points, pillar_counts, point_weight, norm_weight, z, slots, far, moments)
    if parts > 1:
        kgrad = jnp.sum(kgrad.reshape(scene_devices, devices, share), axis=0)
    kgrad = jnp.broadcast_to(kgrad[:, None], (devices, scene_devices, share)).reshape(peers, share)
    got = exchange(jnp.concatenate([kgrad, jnp.broadcast_to(rest, (peers, rest.shape[1]))], axis=1))
    steps_done = step_count[0].astype(f32)
    fix = jnp.stack([1.0 - beta_one**steps_done, 1.0 - beta_two**steps_done])
    outs = update(
        devices,
        parts,
        fix,
        got,
        grad_sums,
        point_weight,
        norm_weight,
        point_master,
        point_states,
        norm_master,
        norm_states,
        kernel_master,
        kernel_states,
    )
    return (result, *outs)


def solution(mesh):
    placed = (
        P("scene", None, None, "rows"),
        P("scene", "rows"),
        P("scene", "rows"),
        P(),
        P(),
        P(),
        P(),
        P(),
        P(),
        P("rows", None),
        P("rows", None),
        P(None, "rows", None),
        P(),
        P("rows", "scene", None, None),
    )
    return jax.shard_map(
        body,
        mesh=mesh,
        in_specs=placed,
        out_specs=(
            P("rows", "scene", None, None),
            P(),
            P(),
            P(),
            P(),
            P(),
            P(),
            P(),
            P(),
            P("rows", None),
            P(None, "rows", None),
            P("rows", None),
            P("rows", None),
        ),
        check_vma=False,
    )
```

time: 1360 us -> 163 us (0.12)
  local copies, waits for them, and re-layouts: 536 us -> 17.4 us
  matrix products: 292 us -> 0 us
  blocking collectives: 237 us -> 0 us
  other arithmetic: 147 us -> 2.05 us
  Pallas kernels: 0 us -> 81.6 us
  waiting for transfers between devices: 99.8 us -> 34.4 us
  loops' own time: 21.2 us -> 0 us
  starting transfers between devices: 6.53 us -> 27.1 us
  between operations: 15.6 us -> 1.6 us
    slice x14 -> x0, local copies, waits for them, and re-layouts: 456 us -> none  [the longest x3 219 us: tap_windows(): cols_even = row_block[..., 0::2]]
    dot_general x61 -> x0, matrix products: 292 us -> none  [the longest x16 83.3 us: take_row(): jnp.einsum('scw,spw->scp', row_grad, cell_table(row_index), preferred_ele...]
    psum x5 -> x0, blocking collectives: 204 us -> none  [the longest x1 42.7 us: body(): lax.psum((jnp.sum(backward_point_grad, axis=(0, 2, 3)), jnp.sum(backward_...]
    psum x1 -> x0, waiting for transfers between devices: 99.8 us -> none  [body(): lax.psum((kernel_grad, point_grad), ('rows', 'scene'))]
    pallas_call x0 -> x6, Pallas kernels: none -> 81.6 us  [the longest x1 24.6 us: unlift(): pl.pallas_call(unlift_body, grid=(scenes,), in_specs=[pl.BlockSpec((1, fe...]
    reduce_sum x4 -> x1, other arithmetic: 78.1 us -> 0.01 us  [body(): kgrad = jnp.sum(kgrad.reshape(scene_devices, devices, share), axis=0)]
    another operation x3 -> x0, local copies, waits for them, and re-layouts: 40.2 us -> none  [the longest x1 18.3 us: body(): jnp.stack([even_rows, odd_rows], axis=1)]
    all_gather x1 -> x0, blocking collectives: 32.7 us -> none  [body(): kernel_full = lax.all_gather(kernel_weight, 'rows', axis=0, tiled=True)]
  transfers between devices with their start and end apart: 3 -> 7, of which waited for: 1 -> 5; matrix products, arithmetic and copies ran while one was open for 28% -> 4% of each run, Pallas kernels for 0% -> 15%
where the time goes in v2:
time: 163 us; the launch traced here: 164 us
  Pallas kernels  81.6 us (50%)
  waiting for transfers between devices  34.4 us (21%)
  starting transfers between devices  27.1 us (17%)
  local copies, waits for them, and re-layouts  17.4 us (11%)
  other arithmetic  2.05 us (1%)
    all_to_all x4, waiting for transfers between devices, exchange(): return lax.all_to_all(x, ('rows', 'scene'), 0, 0, tiled=True)  28.6 us
    pallas_call x1, Pallas kernels, unlift(): pl.pallas_call(unlift_body, grid=(scenes,), in_specs=[pl.BlockSpec((1, fe...  24.6 us
    pallas_call x1, Pallas kernels, convolve(): pl.pallas_call(functools.partial(conv_body, devices, parts), grid=(scenes...  18.3 us
    pallas_call x1, Pallas kernels, gradients(): pl.pallas_call(functools.partial(grad_body, cells, devices, parts), grid=...  17.9 us
    all_to_all x4, starting transfers between devices, exchange(): return lax.all_to_all(x, ('rows', 'scene'), 0, 0, tiled=True)  17.4 us
    unnamed x29, local copies, waits for them, and re-layouts  14.1 us
    pallas_call x1, Pallas kernels, lift(): pl.pallas_call(lift_body, grid=(scenes,), in_specs=[pl.BlockSpec((1, 1),...  13.1 us
    ppermute x2, starting transfers between devices, shifted(): return lax.ppermute(x, 'rows', pairs)  6.33 us
  transfers between devices with their start and end apart: 7, of which 5 were waited for; matrix products, arithmetic and copies ran while one was open for 4% of the time, Pallas kernels for 15%

profile of v2, /device:TPU:0, one launch (start us, length us, event | category | flops | bytes accessed | tf_op | source)
XLA Modules:
  0.0 164.2 jit_solution(9842744813482877357)
XLA Ops:
  0.7 1.4 copy.36.kernel
  2.1 13.1 %lift.1 = (f32[8,768,128]{2,1,0:T(8,128)}, f32[208,128]{1,0:T(8,128)}, f32[32,1408]{1,0:T(8,128)}, f32[16,128]{1,0:T(8,128)}) custom-call(s32[1,1]{1,0:T(1,128)} %bitcast.mine, bf16[8,9,32,768]{3,2,1,0:T(8,128)(2,1)} %points.3, s32[8,768]{1,0:T(8,128)} %counts.3, s32[8,768]{1,0:T(8,128)} %pix.1, bf16[9,64]{1,0:T(8,128)(2,1)} %weight.5, bf16[4,64]{1,0:T(4,128)(2,1)} %norm.11, ...), custom_call_target="tpu_custom_call" | custom-call | tf_op jit(solution)/shard_map/lift/pallas_call | solution.py:177
  15.2 4.9 %collective-permute-start = (f32[208,128]{1,0:T(8,128)}, f32[208,128]{1,0:T(8,128)S(1)}, u32[]{:S(2)}, u32[]{:S(2)}) collective-permute-start(f32[208,128]{1,0:T(8,128)} %get-tuple-element.38), channel_id=1, source_target_pairs={{0,4},{4,8},{8,12},{12,16},{16,20},{20,24},{24,28},{1,5},{5,9},{9,... | collective-permute-start | bytes 319496 | tf_op jit(solution)/shard_map/ppermute | solution.py:818
  20.0 1.8 %copy.37 = f32[32,1,1408]{2,1,0:T(1,128)} copy(f32[32,1,1408]{2,0,1:T(8,128)} %bitcast.19) | data formatting | bytes 360448 | tf_op jit(solution)/shard_map/all_to_all | solution.py:822
  21.8 4.9 %all-to-all-start = ((f32[32,1,1408]{2,1,0:T(1,128)}), f32[32,1,1408]{2,1,0:T(1,128)S(1)}, u32[]{:S(2)}, u32[]{:S(2)}) async-start(f32[32,1,1408]{2,1,0:T(1,128)} %copy.37), calls=%async_computation | async-start | bytes 360448 | tf_op jit(solution)/shard_map/all_to_all | solution.py:822
  26.9 8.5 %all-to-all-done = f32[32,1,1408]{2,1,0:T(1,128)S(1)} async-done(((f32[32,1,1408]{2,1,0:T(1,128)}), f32[32,1,1408]{2,1,0:T(1,128)S(1)}, u32[]{:S(2)}, u32[]{:S(2)}) %all-to-all-start) | async-done | bytes 180256 | tf_op jit(solution)/shard_map/all_to_all | solution.py:822
  36.2 18.3 %convolve.1 = (f32[8,4,256,128]{3,2,1,0:T(8,128)}, bf16[8,896,128]{2,1,0:T(8,128)(2,1)}, f32[32,128]{1,0:T(8,128)}, bf16[576,64]{1,0:T(8,128)(2,1)}) custom-call(s32[8,768]{1,0:T(8,128)} %pix.1, s32[8,128]{1,0:T(8,128)} %copy-done.6, f32[32,1408]{1,0:T(8,128)} %bitcast.18, f32[8,768,128]{2,1,0:T(8,128)} %get-tuple-element.40.z, f32[208,128]{1,0:T(8,128)} %copy-done.3, ...), custom_call_target="tpu_custom_call" | custom-call | tf_op jit(solution)/shard_map/convolve/pallas_call | solution.py:351
  54.5 2.6 %all-to-all-start.1 = ((f32[32,1,128]{2,1,0:T(1,128)}), f32[32,1,128]{2,1,0:T(1,128)S(1)}, u32[]{:S(2)}, u32[]{:S(2)}) async-start(f32[32,1,128]{2,1,0:T(1,128)} %bitcast.25), calls=%async_computation.1 | async-start | bytes 32768 | tf_op jit(solution)/shard_map/all_to_all | solution.py:822
  57.1 7.1 %all-to-all-done.1 = f32[32,1,128]{2,1,0:T(1,128)S(1)} async-done(((f32[32,1,128]{2,1,0:T(1,128)}), f32[32,1,128]{2,1,0:T(1,128)S(1)}, u32[]{:S(2)}, u32[]{:S(2)}) %all-to-all-start.1) | async-done | bytes 16416 | tf_op jit(solution)/shard_map/all_to_all | solution.py:822
  64.8 5.6 %normalize.1 = (bf16[8,8,64,256]{3,2,1,0:T(8,128)(2,1)}, f32[32,128]{1,0:T(8,128)}) custom-call(f32[32,128]{1,0:T(8,128)} %bitcast.20, f32[8,4,256,128]{3,2,1,0:T(8,128)} %get-tuple-element.42.conv, bf16[8,8,64,256]{3,2,1,0:T(8,128)(2,1)} %cot.3, bf16[4,64]{1,0:T(4,128)(2,1)} %norm.11), custom_call_target="tpu_custom_call" | custom-call | tf_op jit(solution)/shard_map/normalize/pallas_call | solution.py:439
  70.3 2.5 %all-to-all-start.2 = ((f32[32,1,128]{2,1,0:T(1,128)}), f32[32,1,128]{2,1,0:T(1,128)S(1)}, u32[]{:S(2)}, u32[]{:S(2)}) async-start(f32[32,1,128]{2,1,0:T(1,128)} %bitcast.26), calls=%async_computation.2 | async-start | bytes 32768 | tf_op jit(solution)/shard_map/all_to_all | solution.py:822
  74.1 5.8 %all-to-all-done.2 = f32[32,1,128]{2,1,0:T(1,128)S(1)} async-done(((f32[32,1,128]{2,1,0:T(1,128)}), f32[32,1,128]{2,1,0:T(1,128)S(1)}, u32[]{:S(2)}, u32[]{:S(2)}) %all-to-all-start.2) | async-done | bytes 16416 | tf_op jit(solution)/shard_map/all_to_all | solution.py:822
  80.6 17.9 %gradients.1 = (f32[8,768,128]{2,1,0:T(8,128)}, f32[192,128]{1,0:T(8,128)}, f32[32,1152]{1,0:T(8,128)}) custom-call(s32[8,816]{1,0:T(8,128)} %pad_add_fusion.idx, f32[32,128]{1,0:T(8,128)} %bitcast.21, f32[32,128]{1,0:T(8,128)} %bitcast.22, f32[8,4,256,128]{3,2,1,0:T(8,128)} %get-tuple-element.42.conv, bf16[8,8,64,256]{3,2,1,0:T(8,128)(2,1)} %cot.3, ...), custom_call_target="tpu_custom_call" | custom-call | tf_op jit(solution)/shard_map/gradients/pallas_call | solution.py:582
  98.5 3.3 %all-to-all-start.3 = ((f32[4,8,1152]{2,1,0:T(8,128)}), f32[4,8,1152]{2,1,0:T(8,128)S(1)}, u32[]{:S(2)}, u32[]{:S(2)}) async-start(f32[4,8,1152]{2,1,0:T(8,128)} %bitcast.24), calls=%async_computation.3 | async-start | bytes 294912 | tf_op jit(solution)/shard_map/all_to_all | solution.py:880
  101.9 1.5 collective-permute-start.1
  103.4 5.8 %collective-permute-done.1.far = f32[192,128]{1,0:T(8,128)S(1)} collective-permute-done((f32[192,128]{1,0:T(8,128)}, f32[192,128]{1,0:T(8,128)S(1)}, u32[]{:S(2)}, u32[]{:S(2)}) %collective-permute-start.1) | collective-permute-done | bytes 98336 | tf_op jit(solution)/shard_map/ppermute | solution.py:818
  109.8 24.6 %unlift.1 = f32[1,896]{1,0:T(1,128)} custom-call(bf16[8,9,32,768]{3,2,1,0:T(8,128)(2,1)} %points.3, s32[8,768]{1,0:T(8,128)} %counts.3, bf16[9,64]{1,0:T(8,128)(2,1)} %weight.5, bf16[4,64]{1,0:T(4,128)(2,1)} %norm.11, f32[8,768,128]{2,1,0:T(8,128)} %get-tuple-element.40.z, f32[8,768,128]{2,1,0:T(8,128)} %get-tuple-element.48.slots, f32[192,128]{1,0:T(8,128)} %copy-done.4, ...), custom_call_target="tpu_custom_call" | custom-call | tf_op jit(solution)/shard_map/unlift/pallas_call | solution.py:710
  136.1 7.4 %all-to-all-start.4 = ((f32[32,1,2048]{2,1,0:T(1,128)}), f32[32,1,2048]{2,1,0:T(1,128)S(1)}, u32[]{:S(2)}, u32[]{:S(2)}) async-start(f32[32,1,2048]{2,1,0:T(1,128)} %all_to_all.45), calls=%async_computation.4 | async-start | bytes 524288 | tf_op jit(solution)/shard_map/all_to_all | solution.py:822
  146.9 7.2 %all-to-all-done.4 = f32[32,1,2048]{2,1,0:T(1,128)S(1)} async-done(((f32[32,1,2048]{2,1,0:T(1,128)}), f32[32,1,2048]{2,1,0:T(1,128)S(1)}, u32[]{:S(2)}, u32[]{:S(2)}) %all-to-all-start.4) | async-done | bytes 262176 | tf_op jit(solution)/shard_map/all_to_all | solution.py:822
  154.9 2.0 %update.1 = (f32[9,64]{1,0:T(8,128)}, f32[2,9,64]{2,1,0:T(8,128)}, f32[9,64]{1,0:T(8,128)}, bf16[9,64]{1,0:T(8,128)(2,1)}, f32[4,64]{1,0:T(4,128)}, /*index=5*/f...) custom-call(f32[2]{0:T(128)} %pad_maximum_fusion.1.fix, ...), custom_call_target="tpu_custom_call" | custom-call | tf_op jit(solution)/shard_map/update/pallas_call | solution.py:805
  156.9 1.6 copy.45
  158.5 1.5 copy.44
  160.0 1.5 copy.46
  161.4 1.4 copy.47
  (42 shorter events, 10.4 us)
Async XLA Ops:
  0.6 26.1 %copy-start = (s32[8,768]{1,0:T(8,128)S(1)}, s32[8,768]{1,0:T(8,128)}, u32[]{:S(2)}) copy-start(s32[8,768]{1,0:T(8,128)} %pix.1) | copy-start | bytes 73732
  15.2 11.7 %collective-permute-start = (f32[208,128]{1,0:T(8,128)}, f32[208,128]{1,0:T(8,128)S(1)}, u32[]{:S(2)}, u32[]{:S(2)}) collective-permute-start(f32[208,128]{1,0:T(8,128)} %get-tuple-element.38), channel_id=1, source_target_pairs={{0,4},{4,8},{8,12},{12,16},{16,20},{20,24},{24,28},{1,5},{5,9},{9,... | collective-permute-start | bytes 319496 | tf_op jit(solution)/shard_map/ppermute | solution.py:818
  21.8 13.7 %all-to-all-start = ((f32[32,1,1408]{2,1,0:T(1,128)}), f32[32,1,1408]{2,1,0:T(1,128)S(1)}, u32[]{:S(2)}, u32[]{:S(2)}) async-start(f32[32,1,1408]{2,1,0:T(1,128)} %copy.37), calls=%async_computation | async-start | bytes 360448 | tf_op jit(solution)/shard_map/all_to_all | solution.py:822
  26.8 9.3 %copy-start.3 = (f32[208,128]{1,0:T(8,128)}, f32[208,128]{1,0:T(8,128)S(1)}, u32[]{:S(2)}) copy-start(f32[208,128]{1,0:T(8,128)S(1)} %collective-permute-done.edge) | copy-start | bytes 319492
  26.9 9.3 %copy-start.6 = (s32[8,128]{1,0:T(8,128)}, s32[8,128]{1,0:T(8,128)S(1)}, u32[]{:S(2)}) copy-start(s32[8,128]{1,0:T(8,128)S(1)} %slice_convert_fusion.far_pix) | copy-start | bytes 12292
  54.5 9.6 %all-to-all-start.1 = ((f32[32,1,128]{2,1,0:T(1,128)}), f32[32,1,128]{2,1,0:T(1,128)S(1)}, u32[]{:S(2)}, u32[]{:S(2)}) async-start(f32[32,1,128]{2,1,0:T(1,128)} %bitcast.25), calls=%async_computation.1 | async-start | bytes 32768 | tf_op jit(solution)/shard_map/all_to_all | solution.py:822
  64.1 0.6 copy-start.1
  70.3 9.6 %all-to-all-start.2 = ((f32[32,1,128]{2,1,0:T(1,128)}), f32[32,1,128]{2,1,0:T(1,128)S(1)}, u32[]{:S(2)}, u32[]{:S(2)}) async-start(f32[32,1,128]{2,1,0:T(1,128)} %bitcast.26), calls=%async_computation.2 | async-start | bytes 32768 | tf_op jit(solution)/shard_map/all_to_all | solution.py:822
  80.0 0.6 copy-start.2
  98.5 36.5 %all-to-all-start.3 = ((f32[4,8,1152]{2,1,0:T(8,128)}), f32[4,8,1152]{2,1,0:T(8,128)S(1)}, u32[]{:S(2)}, u32[]{:S(2)}) async-start(f32[4,8,1152]{2,1,0:T(8,128)} %bitcast.24), calls=%async_computation.3 | async-start | bytes 294912 | tf_op jit(solution)/shard_map/all_to_all | solution.py:880
  101.9 7.3 %collective-permute-start.1 = (f32[192,128]{1,0:T(8,128)}, f32[192,128]{1,0:T(8,128)S(1)}, u32[]{:S(2)}, u32[]{:S(2)}) collective-permute-start(f32[192,128]{1,0:T(8,128)} %get-tuple-element.49), channel_id=1, source_target_pairs={{4,0},{8,4},{12,8},{16,12},{20,16},{24,20},{28,24},{5,1},{9,5},{13... | collective-permute-start | bytes 294920 | tf_op jit(solution)/shard_map/ppermute | solution.py:818
  109.1 0.6 copy-start.4
  109.8 34.5 %copy-start.5 = (f32[3,72,64]{1,2,0:T(8,128)S(1)}, f32[3,72,64]{1,2,0:T(8,128)}, u32[]{:S(2)}) copy-start(f32[3,72,64]{1,2,0:T(8,128)} %param.25) | copy-start | bytes 165892
  109.8 35.2 %copy-start.7 = (f32[72,64]{0,1:T(8,128)S(1)}, f32[72,64]{0,1:T(8,128)}, u32[]{:S(2)}) copy-start(f32[72,64]{0,1:T(8,128)} %param.24) | copy-start | bytes 55300
  109.8 35.9 %copy-start.8 = (f32[3,9,64]{2,0,1:T(4,128)S(1)}, f32[3,9,64]{2,0,1:T(4,128)}, u32[]{:S(2)}) copy-start(f32[3,9,64]{2,0,1:T(4,128)} %param.19) | copy-start | bytes 20740
  136.1 18.0 %all-to-all-start.4 = ((f32[32,1,2048]{2,1,0:T(1,128)}), f32[32,1,2048]{2,1,0:T(1,128)S(1)}, u32[]{:S(2)}, u32[]{:S(2)}) async-start(f32[32,1,2048]{2,1,0:T(1,128)} %all_to_all.45), calls=%async_computation.4 | async-start | bytes 524288 | tf_op jit(solution)/shard_map/all_to_all | solution.py:822

commit v3 on v2

v3 whole, which is shorter than its diff:
```python
import functools

import jax
import jax.numpy as jnp
from jax import lax
from jax.experimental import pallas as pl
from jax.experimental.pallas import tpu as pltpu
from jax.sharding import PartitionSpec as P

beta_one = 0.9
beta_two = 0.999
adam_eps = 1e-08
decay_rate = 0.01
average_keep = 0.99
norm_eps = 1e-05
rate_points = 0.3
rate_norms = 0.2
rate_kernel = 0.04

EDGE = 48
BIG = 1e30
PACK = 8
TILE = 256
SCOPE = 40 << 20
LANES = 128
f32 = jnp.float32
bf16 = jnp.bfloat16


def iota(shape, dim):
    return lax.broadcasted_iota(jnp.int32, shape, dim)


def dot_nn(a, b):
    return lax.dot_general(a, b, (((1,), (0,)), ((), ())), preferred_element_type=f32)


def dot_nt(a, b):
    return lax.dot_general(a, b, (((1,), (1,)), ((), ())), preferred_element_type=f32)


def dot_tn(a, b):
    return lax.dot_general(a, b, (((0,), (0,)), ((), ())), preferred_element_type=f32)


def split3(x):
    a = x.astype(bf16)
    r = x - a.astype(f32)
    b = r.astype(bf16)
    c = (r - b.astype(f32)).astype(bf16)
    return a, b, c


def exact_left(x, y):
    a, b, c = split3(x)
    return dot_nn(a, y) + (dot_nn(b, y) + dot_nn(c, y))


def exact_right(x, y):
    a, b, c = split3(y)
    return dot_nn(x, a) + (dot_nn(x, b) + dot_nn(x, c))


def swap_halves(x):
    return pltpu.roll(x, x.shape[1] // 2, axis=1)


def twice(row):
    return jnp.concatenate([row, row], axis=1)


def one_hot_rows(rows, cols):
    return (iota((rows, cols), 0) // PACK == iota((rows, cols), 1)).astype(f32).astype(bf16)


def one_hot_cols(rows, cols):
    return (iota((rows, cols), 1) // PACK == iota((rows, cols), 0)).astype(f32).astype(bf16)


def lift_table(weight, norm, table):
    feats, channels = weight.shape
    rows = table.shape[0]
    gain = norm[0:1, :].astype(f32)
    sign = jnp.where(gain > 0, 1.0, jnp.where(gain < 0, -1.0, 0.0))
    signed = weight[...].astype(f32) * sign
    full = jnp.concatenate([signed, jnp.zeros((1, channels), f32), jnp.ones((1, channels), f32)], axis=0)
    full = jnp.concatenate([full, jnp.zeros((16 - feats - 2, channels), f32)], axis=0)
    base = dot_nn(one_hot_rows(rows, 16), twice(full).astype(bf16))
    slot = iota(base.shape, 0) % PACK
    half = iota(base.shape, 1) // channels
    for m in range(PACK // 2):
        table[:, m * LANES : (m + 1) * LANES] = jnp.where(slot == 2 * m + half, base, 0.0).astype(bf16)


def lift_inputs(pts, count, part):
    feats, _, size = pts.shape
    live = (iota((PACK, size), 0) + part * PACK < count).astype(f32)
    kept = (pts.astype(f32) * live[None]).reshape(feats * PACK, size)
    return jnp.concatenate([kept, live, (live - 1.0) * BIG], axis=0).astype(bf16)


def copy_in(source, target, sems, s):
    return pltpu.make_async_copy(source.at[s], target.at[s], sems.at[s])


def half_store(block, s, scenes, value):
    channels = LANES // 2
    spot = pl.ds(pl.multiple_of((s % (scenes // 2)) * EDGE, 8), EDGE)
    lower = iota((EDGE, LANES), 1) < channels
    block[spot, :] = jnp.where(lower == (s < scenes // 2), value, block[spot, :])


def lift_body(
    mine, points, counts, pixels, weight, norm, kernel, z_out, winner_out, edge, payload, moments,
    table, gram, wide, pts, z, low, high, winner, sems,
):
    feats, channels = weight.shape
    scenes, _, depth, size = points.shape
    rows = (feats + 1) * PACK
    for s in range(scenes):
        copy_in(points, pts, sems.at[0], s).start()
    lift_table(weight, norm, table)
    gram[...] = jnp.zeros_like(gram)
    edge[...] = jnp.zeros_like(edge)
    second_half = (iota((1, LANES), 1) >= channels).astype(f32)

    def scene(s, _):
        copy_in(points, pts, sems.at[0], s).wait()
        count = counts[pl.ds(s, 1), :]
        total = None
        for part in range(depth // PACK):
            xin = lift_inputs(pts[s, :, part * PACK : (part + 1) * PACK, :], count, part)
            prod = dot_nt(xin[:rows], xin[:rows])
            total = prod if total is None else total + prod
            for t in range(size // TILE):
                at = slice(t * TILE, (t + 1) * TILE)
                turned = jnp.transpose(xin[:, at])
                for q in range(PACK // 4):
                    l = dot_nn(turned, table[:, q * 256 : (q + 1) * 256])
                    one, two = l[:, :LANES], l[:, LANES:]
                    n_one = second_half + float(part * PACK + q * 4)
                    n_two = n_one + 2.0
                    m = jnp.maximum(one, two)
                    first = jnp.where(two > one, n_two, n_one)
                    last = jnp.where(two >= one, n_two, n_one)
                    if part > 0 or q > 0:
                        old = z[s, at, :]
                        first = jnp.where(m > old, first, low[at, :])
                        last = jnp.where(m >= old, last, high[at, :])
                        m = jnp.maximum(old, m)
                    if part == depth // PACK - 1 and q == PACK // 4 - 1:
                        other = swap_halves(m)
                        first = jnp.where(other > m, swap_halves(first), first)
                        last = jnp.where(other >= m, swap_halves(last), last)
                        m = jnp.maximum(m, other)
                        only = jnp.where(first == last, first, -1.0)
                        winner[s, at, :] = jnp.where(m > -0.5 * BIG, only, 99.0)
                    else:
                        low[at, :] = first
                        high[at, :] = last
                    z[s, at, :] = m
        gram[...] += total
        copy_in(z, z_out, sems.at[1], s).start()
        copy_in(winner, winner_out, sems.at[2], s).start()
        half_store(edge, s, scenes, z[s, :EDGE, :])
        return 0

    lax.fori_loop(0, scenes, scene, 0)

    count_rows = edge.shape[0] - 2 * scenes
    edge[count_rows : count_rows + scenes, :] = pixels[:, :LANES].astype(f32)
    edge[count_rows + scenes :, :] = jnp.ones((scenes, LANES), f32)
    g = gram[...]
    g = jnp.where(iota(g.shape, 0) % PACK == iota(g.shape, 1) % PACK, g, 0.0)
    y = exact_left(g, one_hot_rows(rows, LANES))
    m = exact_right(one_hot_cols(16, rows), y)
    moments[...] = m
    w = jnp.concatenate([weight[...].astype(f32), jnp.zeros((16 - feats, channels), f32)], axis=0)
    aw = exact_left(m[:, :16], w.astype(bf16))
    two = jnp.sum(aw * w, axis=0, keepdims=True)
    one = aw[feats : feats + 1]
    own = kernel.shape[1]
    flat = jnp.concatenate([kernel[...].astype(f32), jnp.zeros((channels, LANES - own), f32)], axis=1)
    wide[...] = jnp.transpose(jnp.concatenate([flat, jnp.zeros((LANES - channels, LANES), f32)], axis=0))
    pieces = [one, two, m[feats : feats + 1]]
    share = (payload.shape[2] - 256) // channels
    for j in range(share):
        pieces.append(wide[pl.ds(mine[0, 0] * share + j, 1), :channels])
    row = jnp.concatenate(pieces, axis=1)
    payload[...] = jnp.broadcast_to(row[:, None, :], payload.shape)
    for s in range(scenes):
        copy_in(z, z_out, sems.at[1], s).wait()
        copy_in(winner, winner_out, sems.at[2], s).wait()


def vmem(count):
    return [pl.BlockSpec(memory_space=pltpu.VMEM)] * count


def smem(count):
    return [pl.BlockSpec(memory_space=pltpu.SMEM)] * count


def hbm(count):
    return [pl.BlockSpec(memory_space=pltpu.HBM)] * count


def near(x):
    return pltpu.with_memory_space_constraint(x, pltpu.VMEM)


scoped = pltpu.CompilerParams(vmem_limit_bytes=SCOPE)


def lift(mine, points, counts, pixels, weight, norm, kernel, peers, share):
    scenes, feats, depth, size = points.shape
    channels = weight.shape[1]
    full = (feats + 2) * PACK
    rows = (feats + 1) * PACK
    edge_rows = scenes // 2 * EDGE + 2 * scenes
    return pl.pallas_call(
        lift_body,
        in_specs=smem(1) + hbm(1) + vmem(5),
        out_specs=hbm(2) + vmem(3),
        out_shape=[
            jax.ShapeDtypeStruct((scenes, size, LANES), f32),
            jax.ShapeDtypeStruct((scenes, size, LANES), f32),
            jax.ShapeDtypeStruct((edge_rows, LANES), f32),
            jax.ShapeDtypeStruct((peers, 1, 256 + share), f32),
            jax.ShapeDtypeStruct((16, LANES), f32),
        ],
        scratch_shapes=[
            pltpu.VMEM((full, PACK * channels), bf16),
            pltpu.VMEM((rows, rows), f32),
            pltpu.VMEM((LANES, LANES), f32),
            pltpu.VMEM(points.shape, bf16),
            pltpu.VMEM((scenes, size, LANES), f32),
            pltpu.VMEM((size, LANES), f32),
            pltpu.VMEM((size, LANES), f32),
            pltpu.VMEM((scenes, size, LANES), f32),
            pltpu.SemaphoreType.DMA((3, scenes)),
        ],
        compiler_params=scoped,
        name="lift",
    )(mine, points, counts, pixels, weight, norm, kernel)


def gather_kernel(got, kern, devices, parts):
    channels = kern.shape[1]
    share = kern.shape[0] // devices // parts
    peers = got.shape[0]
    for j in range(share):
        rows = got[:, 0, 256 + j * channels : 256 + (j + 1) * channels]
        if parts > 1:
            kern[pl.ds(j, peers, stride=share), :] = rows
        else:
            for r in range(devices):
                at = r * (peers // devices)
                kern[r * share + j : r * share + j + 1, :] = rows[at : at + 1]


def tap(kern, a, b):
    channels = kern.shape[1]
    if a is None or b is None:
        return jnp.zeros((channels, channels), f32)
    return kern[(3 * a + b) * channels : (3 * a + b + 1) * channels, :]


def edge_rows_of(block, s, scenes, lower):
    spot = pl.ds(pl.multiple_of((s % (scenes // 2)) * EDGE, 8), EDGE)
    rows = jnp.where(lower == (s < scenes // 2), block[spot, :], 0.0)
    return rows + swap_halves(rows)


def conv_body(
    devices, parts, pix, far_pix, got, z_in, edge, norm, conv_out, pooled_out, sums, kernel,
    params, source, kern, taps, grid_a, grid_b, side, acc, z, conv, pooled, sems,
):
    scenes, size, _ = z.shape
    for s in range(scenes):
        copy_in(z_in, z, sems.at[0], s).start()
    channels = norm.shape[1]
    _, pairs, out_cols, _ = conv.shape
    cols = 2 * out_cols
    last_row = (4 * pairs - 1) * cols
    tot = jnp.sum(got[:, :, :256], axis=0)
    count = tot[:, 2 * channels + 9 : 2 * channels + 10]
    mean = tot[:, :channels] / count
    inv = lax.rsqrt(tot[:, channels : 2 * channels] / count - mean * mean + norm_eps)
    nw = norm[...].astype(f32)
    gain = nw[0:1]
    sign = jnp.where(gain > 0, 1.0, jnp.where(gain < 0, -1.0, 0.0))
    params[0:1] = twice(mean)
    params[1:2] = twice(inv)
    params[2:3] = twice(gain)
    params[3:4] = twice(nw[1:2])
    params[4:5] = twice(sign)
    gather_kernel(got, kern, devices, parts)
    kernel[...] = kern[...].astype(bf16)
    for w, (low, high) in enumerate(((0, None), (1, None), (2, 0), (None, 1), (None, 2))):
        none = tap(kern, None, None)
        top = jnp.concatenate([tap(kern, low, 1), tap(kern, high, 1), none, none], axis=1)
        end = jnp.concatenate([tap(kern, low, 2), tap(kern, high, 2), tap(kern, low, 0), tap(kern, high, 0)], axis=1)
        taps[w] = jnp.concatenate([top, end], axis=0).astype(bf16)
    grid_a[...] = jnp.zeros_like(grid_a)
    grid_b[...] = jnp.zeros_like(grid_b)
    side[...] = jnp.zeros_like(side)
    acc[...] = jnp.zeros_like(acc)

    def pool(x, ok):
        pre = params[2:3] * ((x * params[4:5] - params[0:1]) * params[1:2]) + params[3:4]
        return jnp.where(ok, jnp.maximum(pre, 0.0), 0.0).astype(bf16)

    own_at = 8 + cols
    far_at = 8 - last_row

    def fill(s):
        zs = z[s]
        own = pool(zs, zs > -0.5 * BIG)
        pooled[s, :size] = own
        source[:size] = own.astype(f32)
        far = edge_rows_of(edge, s, scenes, iota((EDGE, LANES), 1) < channels)
        flag = edge[edge.shape[0] - scenes : edge.shape[0] - scenes + 1, :]
        far = pool(far, (far > -0.5 * BIG) & (flag > 0.5))
        pooled[s, size:] = jnp.concatenate([far, jnp.zeros((LANES - EDGE, LANES), bf16)], axis=0)
        source[size : size + EDGE] = far.astype(f32)

    def place_far(dst, s):
        for p in range(EDGE):
            at = jnp.maximum(far_pix[s, p], last_row) + far_at
            dst[pl.ds(at, 1), :] = source[size + p : size + p + 1, :]

    def place(dst, s, j):
        rows = dst.at[pl.ds(own_at, 4 * pairs * cols), :]
        some = size // pairs
        line = s * pairs + j
        base = pl.multiple_of(j * some, 8)
        for p in range(some):
            rows[pl.ds(pix[line, 0, p], 1), :] = source[pl.ds(base + p, 1), :]

    left = iota((out_cols, LANES), 1) < channels

    def convolve_pair(src, s, j):
        out = None
        for w in range(5):
            base = 8 + (4 * j + w) * cols
            even = src[pl.ds(base, out_cols, stride=2), :]
            odd = src[pl.ds(base + 1, out_cols, stride=2), :]
            part = dot_nn(jnp.where(left, even, odd).astype(bf16), taps[w])
            out = part if out is None else out + part
        side[8:, :] = out[:, LANES:]
        value = out[:, :LANES] + side[7 : 7 + out_cols, :]
        conv[s, j] = value
        acc[0:8] += jnp.sum(value.reshape(out_cols // 8, 8, LANES), axis=0)
        acc[8:16] += jnp.sum((value * value).reshape(out_cols // 8, 8, LANES), axis=0)
        base = pl.multiple_of(8 + 4 * j * cols, 8)
        src[pl.ds(base, 4 * cols), :] = jnp.zeros((4 * cols, LANES), f32)

    def clear_last(src):
        src[8 + 4 * pairs * cols : 8 + (4 * pairs + 1) * cols, :] = jnp.zeros((cols, LANES), f32)

    copy_in(z_in, z, sems.at[0], 0).wait()
    fill(0)
    place_far(grid_a, 0)

    def start(j, _):
        place(grid_a, 0, j)
        return 0

    lax.fori_loop(0, pairs, start, 0)

    def two_scenes(i, _):
        for k, (src, dst) in enumerate(((grid_a, grid_b), (grid_b, grid_a))):
            s = 2 * i + k
            ahead = jnp.minimum(s + 1, scenes - 1)

            @pl.when(s + 1 < scenes)
            def _():
                copy_in(z_in, z, sems.at[0], s + 1).wait()

            fill(ahead)
            place_far(dst, ahead)

            def step(j, _):
                place(dst, ahead, j)
                convolve_pair(src, s, j)
                return 0

            lax.fori_loop(0, pairs, step, 0)
            clear_last(src)
            copy_in(conv, conv_out, sems.at[1], s).start()
            copy_in(pooled, pooled_out, sems.at[2], s).start()
        return 0

    lax.fori_loop(0, scenes // 2, two_scenes, 0)
    for s in range(scenes):
        copy_in(conv, conv_out, sems.at[1], s).wait()
        copy_in(pooled, pooled_out, sems.at[2], s).wait()
    sums[...] = jnp.broadcast_to(both_sums(acc, channels), sums.shape)


def both_sums(acc, channels):
    one = jnp.sum(acc[0:8], axis=0, keepdims=True)
    two = jnp.sum(acc[8:16], axis=0, keepdims=True)
    one = one + swap_halves(one)
    two = two + swap_halves(two)
    return jnp.where(iota((1, LANES), 1) < channels, one, two)


def convolve(devices, parts, pix, far_pix, got, z, edge, norm, pairs, out_cols):
    scenes, size, _ = z.shape
    peers = got.shape[0]
    channels = norm.shape[1]
    cells = 8 + (4 * pairs + 1) * 2 * out_cols + 8
    return pl.pallas_call(
        functools.partial(conv_body, devices, parts),
        in_specs=smem(2) + vmem(1) + hbm(1) + vmem(2),
        out_specs=hbm(2) + vmem(2),
        out_shape=[
            jax.ShapeDtypeStruct((scenes, pairs, out_cols, LANES), f32),
            jax.ShapeDtypeStruct((scenes, size + LANES, LANES), bf16),
            jax.ShapeDtypeStruct((peers, LANES), f32),
            jax.ShapeDtypeStruct((9 * channels, channels), bf16),
        ],
        scratch_shapes=[
            pltpu.VMEM((8, LANES), f32),
            pltpu.VMEM((size + LANES, LANES), f32),
            pltpu.VMEM((9 * channels, channels), f32),
            pltpu.VMEM((5, LANES, 2 * LANES), bf16),
            pltpu.VMEM((cells, LANES), f32),
            pltpu.VMEM((cells, LANES), f32),
            pltpu.VMEM((out_cols + 8, LANES), f32),
            pltpu.VMEM((16, LANES), f32),
            pltpu.VMEM((scenes, size, LANES), f32),
            pltpu.VMEM((scenes, pairs, out_cols, LANES), f32),
            pltpu.VMEM((scenes, size + LANES, LANES), bf16),
            pltpu.SemaphoreType.DMA((3, scenes)),
        ],
        compiler_params=scoped,
        name="convolve",
    )(pix, far_pix, got, z, edge, norm)


def split_sums(stats, channels):
    tot = jnp.sum(stats[...], axis=0)
    lower = iota((1, LANES), 1) < channels
    turned = swap_halves(tot)
    return jnp.where(lower, tot, turned), jnp.where(lower, turned, tot)


def conv_params(cells, stats, norm):
    one, two = split_sums(stats, norm.shape[1])
    mean = one / cells
    inv = lax.rsqrt(two / cells - mean * mean + norm_eps)
    nw = norm[...].astype(f32)
    return mean, inv, twice(nw[2:3]), twice(nw[3:4])


def turned_pair(block, j, k):
    _, _, channels, cols = block.shape
    return jnp.transpose(block[2 * j : 2 * j + 2, k].reshape(2 * channels, cols)).astype(f32)


def scene_copy(source, target, sems, s):
    return pltpu.make_async_copy(source.at[:, s], target.at[:, s], sems.at[s])


def norm_body(cells, stats, conv_in, cot_in, norm, result_out, sums, acc, conv, cot, result, sems):
    channels = norm.shape[1]
    scenes, pairs, out_cols, _ = conv.shape
    for s in range(scenes):
        copy_in(conv_in, conv, sems.at[0], s).start()
        scene_copy(cot_in, cot, sems.at[1], s).start()
    mean, inv, gain, bias = conv_params(cells, stats, norm)
    acc[...] = jnp.zeros_like(acc)

    def scene(k, _):
        copy_in(conv_in, conv, sems.at[0], k).wait()
        scene_copy(cot_in, cot, sems.at[1], k).wait()
        for j in range(pairs):
            xhat = (conv[k, j] - mean) * inv
            pre = gain * xhat + bias
            out = jnp.transpose(jnp.maximum(pre, 0.0).astype(bf16))
            result[2 * j : 2 * j + 2, k] = out.reshape(2, channels, out_cols)
            back = jnp.where(pre > 0, turned_pair(cot, j, k), 0.0)
            acc[0:8] += jnp.sum(back.reshape(out_cols // 8, 8, LANES), axis=0)
            acc[8:16] += jnp.sum((back * xhat).reshape(out_cols // 8, 8, LANES), axis=0)
        scene_copy(result, result_out, sems.at[2], k).start()
        return 0

    lax.fori_loop(0, scenes, scene, 0)
    sums[...] = jnp.broadcast_to(both_sums(acc, channels), sums.shape)
    for s in range(scenes):
        scene_copy(result, result_out, sems.at[2], s).wait()


def normalize(cells, stats, conv, cot, norm):
    peers = stats.shape[0]
    scenes = conv.shape[0]
    return pl.pallas_call(
        functools.partial(norm_body, cells),
        in_specs=vmem(1) + hbm(2) + vmem(1),
        out_specs=hbm(1) + vmem(1),
        out_shape=[
            jax.ShapeDtypeStruct(cot.shape, bf16),
            jax.ShapeDtypeStruct((peers, LANES), f32),
        ],
        scratch_shapes=[
            pltpu.VMEM((16, LANES), f32),
            pltpu.VMEM(conv.shape, f32),
            pltpu.VMEM(cot.shape, bf16),
            pltpu.VMEM(cot.shape, bf16),
            pltpu.SemaphoreType.DMA((3, scenes)),
        ],
        compiler_params=scoped,
        name="normalize",
    )(stats, conv, cot, norm)


def grad_body(
    cells, devices, parts, idx, stats, sums, conv_in, cot_in, norm, pooled_in, phase, kernel, slots_out, edge, far, kgrad,
    taps, field_a, field_b, taken_a, taken_b, turn, column, acc, rows_k, conv, cot, pooled, slots, exact, sems,
):
    scenes, pairs, out_cols, _ = conv.shape
    channels = norm.shape[1]
    size = slots.shape[1]
    strip = out_cols + 8
    some = idx.shape[2]
    for s in range(scenes):
        copy_in(conv_in, conv, sems.at[0], s).start()
        scene_copy(cot_in, cot, sems.at[1], s).start()
    for s in range(scenes):
        copy_in(pooled_in, pooled, sems.at[2], s).start()
    for hp in range(2):
        for up in range(2):
            line = []
            for dw in range(2):
                for dr in range(2):
                    a = ((1, None), (2, 0))[hp][dr]
                    b = ((1, None), (2, 0))[up][dw]
                    if a is None or b is None:
                        line.append(jnp.zeros((channels, channels), f32))
                    else:
                        at = (3 * a + b) * channels
                        line.append(kernel[at : at + channels, :].astype(f32))
            ph = 2 * hp + up
            taps[ph * channels : (ph + 1) * channels, :] = jnp.concatenate(line, axis=1).astype(bf16)
    for block in (field_a, field_b, taken_a, taken_b, acc):
        block[...] = jnp.zeros_like(block)

    def phases(s, _):
        for c in range(column.shape[1] // LANES):
            row = phase[s, :, c * LANES : (c + 1) * LANES]
            column[s, c * LANES : (c + 1) * LANES, :] = jnp.transpose(jnp.broadcast_to(row, (LANES, LANES)))
        return 0

    lax.fori_loop(0, scenes, phases, 0)
    mean, inv, gain, bias = conv_params(cells, stats, norm)
    bias_grad, gain_grad = split_sums(sums, channels)
    scale = gain * inv / cells
    left = iota((out_cols, LANES), 1) < channels
    half = (iota((some, LANES), 1) >= channels).astype(f32)

    def field(dst, s, j):
        xhat = (conv[s, j] - mean) * inv
        pre = gain * xhat + bias
        both = cot[pl.ds(2 * j, 2), s].reshape(2 * channels, out_cols)
        back = jnp.where(pre > 0, jnp.transpose(both).astype(f32), 0.0)
        grad = scale * (cells * back - bias_grad - xhat * gain_grad)
        grad = grad.astype(bf16).astype(f32)
        turned = swap_halves(grad)
        base = pl.multiple_of(2 * j * strip, 8)
        dst[pl.ds(base, out_cols), :] = jnp.where(left, turn[...], turned)
        dst[pl.ds(pl.multiple_of(base + strip, 8), out_cols), :] = grad
        turn[...] = turned

    def take(dst, src, s, j):
        line = s * pairs + j
        for p in range(some):
            dst[2 * p : 2 * p + 2, :] = src[pl.ds(idx[line, 0, p], 2), :]

    def product(src, s, j):
        at = pl.ds(pl.multiple_of(j * some, 16), some)
        part = jnp.concatenate([src[pl.ds(0, some, stride=2), :], src[pl.ds(1, some, stride=2), :]], axis=1).astype(bf16)
        out = dot_nt(part, taps[...])
        ph = column[s, at, :]
        is_even = ph == half
        is_odd = ph == half + 2.0
        value = jnp.where(is_even, out[:, :LANES], 0.0) + jnp.where(is_odd, out[:, LANES:], 0.0)
        value = value + swap_halves(value)
        pf = pooled[s, at, :].astype(f32)
        value = jnp.where(pf > 0, value, 0.0)
        exact[s, at, :] = value
        slots[s, at, :] = value.astype(bf16)
        split = jnp.concatenate([jnp.where(is_even, pf, 0.0), jnp.where(is_odd, pf, 0.0)], axis=1)
        acc[...] += dot_tn(split.astype(bf16), part)

    def walk(dst, src, s):
        before = jnp.clip(s - 1, 0, scenes - 1)
        older = jnp.clip(s - 2, 0, scenes - 1)

        def step(i, _):
            for k, (to, of) in enumerate(((taken_a, taken_b), (taken_b, taken_a))):
                j = 2 * i + k
                if dst is not None:
                    field(dst, s, j)
                take(to, src, before, j)
                last = jnp.where(j > 0, before, older)
                product(of, last, jnp.where(j > 0, j - 1, pairs - 1))
            return 0

        if dst is not None:
            copy_in(conv_in, conv, sems.at[0], s).wait()
            scene_copy(cot_in, cot, sems.at[1], s).wait()
            copy_in(pooled_in, pooled, sems.at[2], s).wait()
            turn[...] = jnp.zeros_like(turn)
        lax.fori_loop(0, pairs // 2, step, 0)
        if dst is not None:
            dst[2 * pairs * strip : 2 * pairs * strip + out_cols, :] = jnp.where(left, turn[...], 0.0)

    def two_scenes(i, _):
        walk(field_a, field_b, 2 * i)
        walk(field_b, field_a, 2 * i + 1)
        return 0

    lax.fori_loop(0, scenes // 2, two_scenes, 0)
    walk(None, field_b, scenes)
    product(taken_b, scenes - 1, pairs - 1)
    for s in range(scenes):
        copy_in(slots, slots_out, sems.at[0], s).start()
    far[...] = jnp.zeros_like(far)
    edge[...] = jnp.zeros_like(edge)

    def pick(s, _):
        half_store(edge, s, scenes, exact[s, :EDGE, :])
        half_store(far, s, scenes, exact[s, size - LANES : size - LANES + EDGE, :])
        return 0

    lax.fori_loop(0, scenes, pick, 0)
    for a in range(3):
        for b in range(3):
            hp, dr = ((1, 1), (0, 0), (1, 0))[a]
            up, dw = ((1, 1), (0, 0), (1, 0))[b]
            row, col = hp * 2 + up, dw * 2 + dr
            at = (3 * a + b) * channels
            rows_k[at : at + channels, :] = acc[
                row * channels : (row + 1) * channels, col * channels : (col + 1) * channels
            ]
    own = rows_k.shape[0] // devices
    share = own // parts
    for q in range(parts):
        for j in range(share):
            lanes = slice(j * channels, (j + 1) * channels)
            kgrad[q * devices : (q + 1) * devices, lanes] = rows_k[pl.ds(q * share + j, devices, stride=own), :]
    for s in range(scenes):
        copy_in(slots, slots_out, sems.at[0], s).wait()


def gradients(cells, devices, parts, idx, stats, sums, conv, cot, norm, pooled, phase, kernel):
    scenes, pairs, out_cols, _ = conv.shape
    channels = norm.shape[1]
    rows = pooled.shape[1]
    return pl.pallas_call(
        functools.partial(grad_body, cells, devices, parts),
        in_specs=smem(1) + vmem(2) + hbm(2) + vmem(1) + hbm(1) + vmem(2),
        out_specs=hbm(1) + vmem(3),
        out_shape=[
            jax.ShapeDtypeStruct((scenes, rows, LANES), bf16),
            jax.ShapeDtypeStruct((scenes // 2 * EDGE, LANES), f32),
            jax.ShapeDtypeStruct((scenes // 2 * EDGE, LANES), f32),
            jax.ShapeDtypeStruct((parts * devices, 9 * channels * channels // devices // parts), f32),
        ],
        scratch_shapes=[
            pltpu.VMEM((4 * channels, 4 * channels), bf16),
            pltpu.VMEM(((2 * pairs + 1) * (out_cols + 8), LANES), f32),
            pltpu.VMEM(((2 * pairs + 1) * (out_cols + 8), LANES), f32),
            pltpu.VMEM((2 * idx.shape[2], LANES), f32),
            pltpu.VMEM((2 * idx.shape[2], LANES), f32),
            pltpu.VMEM((out_cols, LANES), f32),
            pltpu.VMEM((scenes, rows, LANES), f32),
            pltpu.VMEM((4 * channels, 4 * channels), f32),
            pltpu.VMEM((9 * channels, channels), f32),
            pltpu.VMEM(conv.shape, f32),
            pltpu.VMEM(cot.shape, bf16),
            pltpu.VMEM(pooled.shape, bf16),
            pltpu.VMEM((scenes, rows, LANES), bf16),
            pltpu.VMEM((scenes, rows, LANES), f32),
            pltpu.SemaphoreType.DMA((3, scenes)),
        ],
        compiler_params=scoped,
        name="gradients",
    )(idx, stats, sums, conv, cot, norm, pooled, phase, kernel)


def unlift_body(
    points, counts, weight, norm, z, winner_in, slots_in, edge, far, moments, rest,
    table, acc, bias, pts, winner, slots, best, mult, sems,
):
    feats, channels = weight.shape
    scenes, _, depth, size = points.shape
    rows = feats * PACK
    tiles = size // TILE
    for s in range(scenes):
        copy_in(points, pts, sems.at[0], s).start()
        copy_in(winner_in, winner, sems.at[1], s).start()
        copy_in(slots_in, slots, sems.at[2], s).start()
    lift_table(weight, norm, table)
    acc[...] = jnp.zeros_like(acc)
    bias[...] = jnp.zeros_like(bias)
    second_half = (iota((1, LANES), 1) >= channels).astype(f32)
    slot = iota((rows, LANES), 0) % PACK
    upper = (iota((rows, LANES), 1) >= channels).astype(jnp.int32)

    def fold(q, prod):
        near_n = slot - 4 * q
        return jnp.where(near_n == upper, prod[:, :LANES], 0.0) + jnp.where(near_n == upper + 2, prod[:, LANES:], 0.0)

    def tile(u, _):
        s = u // tiles
        t = u % tiles
        at = pl.ds(pl.multiple_of(t * TILE, TILE), TILE)

        @pl.when(t == 0)
        def _():
            copy_in(points, pts, sems.at[0], s).wait()
            copy_in(winner_in, winner, sems.at[1], s).wait()
            copy_in(slots_in, slots, sems.at[2], s).wait()
            lower = iota((EDGE, LANES), 1) < channels
            whole = edge_rows_of(edge, s, scenes, lower) + edge_rows_of(far, s, scenes, lower)
            slots[s, :EDGE, :] = whole.astype(bf16)

        grad = slots[s, at, :].astype(f32)
        who = winner[s, at, :]
        bias[...] += jnp.sum(grad.reshape(TILE // 8, 8, LANES), axis=0)
        total = None
        for part in range(depth // PACK):
            x = pts[s, :, part * PACK : (part + 1) * PACK, at].reshape(rows, TILE)
            for q in range(PACK // 4):
                n_one = second_half + float(part * PACK + q * 4)
                value = jnp.concatenate(
                    [jnp.where(who == n_one, grad, 0.0), jnp.where(who == n_one + 2.0, grad, 0.0)], axis=1
                )
                prod = fold(q, dot_nn(x, value.astype(bf16)))
                total = prod if total is None else total + prod
        acc[...] += total

        @pl.when(jnp.min(who) < 0.0)
        def _():
            fetch = pltpu.make_async_copy(z.at[s, at], best, sems.at[0, 0])
            fetch.start()
            fetch.wait()
            best[...] = jnp.where(winner[s, at, :] < 0.0, best[...], BIG)
            mult[...] = jnp.zeros_like(mult)
            count = counts[pl.ds(s, 1), at]

            def lifted(part, q):
                xin = lift_inputs(pts[s, :, part * PACK : (part + 1) * PACK, at], count, part)
                l = dot_nn(jnp.transpose(xin), table[:, q * 256 : (q + 1) * 256])
                return xin, l[:, :LANES] == best[...], l[:, LANES:] == best[...]

            for part in range(depth // PACK):
                for q in range(PACK // 4):
                    _, one, two = lifted(part, q)
                    mult[...] += jnp.where(one, 1.0, 0.0) + jnp.where(two, 1.0, 0.0)
            many = jnp.maximum(mult[...] + swap_halves(mult[...]), 1.0)
            mult[...] = slots[s, at, :].astype(f32) / many
            for part in range(depth // PACK):
                for q in range(PACK // 4):
                    xin, one, two = lifted(part, q)
                    value = jnp.concatenate([jnp.where(one, mult[...], 0.0), jnp.where(two, mult[...], 0.0)], axis=1)
                    acc[...] += fold(q, exact_right(xin[:rows], value))

        return 0

    lax.fori_loop(0, scenes * tiles, tile, 0)
    out = exact_right(one_hot_cols(16, rows), acc[...])
    out = out + swap_halves(out)
    pieces = [out[i : i + 1, :channels] for i in range(feats)]
    pieces.append(jnp.sum(bias[...], axis=0, keepdims=True)[:, :channels])
    pieces += [moments[i : i + 1, :16] for i in range(feats + 1)]
    width = (feats + 1) * (channels + 16)
    pieces.append(jnp.zeros((1, rest.shape[1] - width), f32))
    rest[...] = jnp.concatenate(pieces, axis=1)


def unlift(points, counts, weight, norm, z, winner, slots, edge, far, moments):
    scenes, feats, depth, size = points.shape
    channels = weight.shape[1]
    full = (feats + 2) * PACK
    width = -(-(feats + 1) * (channels + 16) // LANES) * LANES
    return pl.pallas_call(
        unlift_body,
        in_specs=hbm(1) + vmem(3) + hbm(3) + vmem(3),
        out_specs=pl.BlockSpec(memory_space=pltpu.VMEM),
        out_shape=jax.ShapeDtypeStruct((1, width), f32),
        scratch_shapes=[
            pltpu.VMEM((full, PACK * channels), bf16),
            pltpu.VMEM((feats * PACK, LANES), f32),
            pltpu.VMEM((8, LANES), f32),
            pltpu.VMEM(points.shape, bf16),
            pltpu.VMEM((scenes, size, LANES), f32),
            pltpu.VMEM(slots.shape, bf16),
            pltpu.VMEM((TILE, LANES), f32),
            pltpu.VMEM((TILE, LANES), f32),
            pltpu.SemaphoreType.DMA((3, scenes)),
        ],
        compiler_params=scoped,
        name="unlift",
    )(points, counts, weight, norm, z, winner, slots, edge, far, moments)


def adam(fixes, w, states, grad, rate):
    moment = beta_one * states[0] + (1.0 - beta_one) * grad
    second = beta_two * states[1] + (1.0 - beta_two) * grad * grad
    new = w - rate * (moment / fixes[0] / (jnp.sqrt(second / fixes[1]) + adam_eps) + decay_rate * w)
    return new, moment, second, average_keep * states[2] + (1.0 - average_keep) * new


def step_body(devices, parts, fix, got, sums, weight, norm, pm, ps, nm, ns, km, ks, *refs):
    p_new, p_states, p_avg, p_copy, n_new, n_states, n_avg, n_copy, k_new, k_states, k_avg, k_copy, kgrad = refs
    feats, channels = weight.shape
    own = km.shape[1]
    share = own // parts
    peers = got.shape[0]
    scenes = peers // devices
    fixes = (fix[0], fix[1])

    width = share * channels
    kgrad[...] = jnp.zeros_like(kgrad)
    for q in range(parts):
        tot = got[q, :, :width]
        for r in range(1, devices):
            tot = tot + got[r * scenes + q, :, :width]
        for j in range(share):
            kgrad[q * share + j : q * share + j + 1, :channels] = tot[:, j * channels : (j + 1) * channels]
    grad = jnp.transpose(kgrad[...])[:channels, :own]
    new, moment, second, average = adam(fixes, km[...], (ks[0], ks[1], ks[2]), grad, rate_kernel)
    k_new[...] = new
    k_states[0] = moment
    k_states[1] = second
    k_avg[...] = average
    k_copy[...] = new.astype(bf16)

    row = jnp.sum(got[:, :, width:], axis=0)
    cross = jnp.concatenate([row[:, i * channels : (i + 1) * channels] for i in range(feats + 1)], axis=0)
    base = (feats + 1) * channels
    moments = jnp.concatenate([row[:, base + i * 16 : base + (i + 1) * 16] for i in range(feats + 1)], axis=0)
    w = weight[...].astype(f32)
    nw = norm[...].astype(f32)
    total = moments[feats : feats + 1, feats : feats + 1]
    firsts = moments[:feats, feats : feats + 1]
    mixed = None
    first_sum = None
    for i in range(feats):
        part = moments[:feats, i : i + 1] * w[i : i + 1]
        mixed = part if mixed is None else mixed + part
        part = moments[feats : feats + 1, i : i + 1] * w[i : i + 1]
        first_sum = part if first_sum is None else first_sum + part
    mean = first_sum / total
    inv = lax.rsqrt(jnp.sum(mixed * w, axis=0, keepdims=True) / total - mean * mean + norm_eps)
    bias_p = cross[feats : feats + 1]
    gain_p = inv * (jnp.sum(w * cross[:feats], axis=0, keepdims=True) - mean * bias_p)
    spread = inv * (mixed - firsts * mean)
    point_grad = (nw[0:1] * inv) * (cross[:feats] - (firsts * bias_p + spread * gain_p) / total)
    states = (ps[:, 0, :], ps[:, 1, :], ps[:, 2, :])
    new, moment, second, average = adam(fixes, pm[...], states, point_grad, rate_points)
    p_new[...] = new
    p_states[:, 0, :] = moment
    p_states[:, 1, :] = second
    p_avg[...] = average
    p_copy[...] = new.astype(bf16)

    both = jnp.sum(sums[...], axis=0)
    norm_grad = jnp.concatenate([gain_p, bias_p, both[:, channels:], both[:, :channels]], axis=0)
    new, moment, second, average = adam(fixes, nm[...], (ns[0], ns[1], ns[2]), norm_grad, rate_norms)
    n_new[...] = new
    n_states[0] = moment
    n_states[1] = second
    n_avg[...] = average
    n_copy[...] = new.astype(bf16)


def update(devices, parts, fix, got, sums, weight, norm, pm, ps, nm, ns, km, ks):
    feats, channels = weight.shape
    shapes = []
    for m, states in ((pm, (feats, 2, channels)), (nm, (2,) + nm.shape), (km, (2,) + km.shape)):
        shapes.append(jax.ShapeDtypeStruct(m.shape, f32))
        shapes.append(jax.ShapeDtypeStruct(states, f32))
        shapes.append(jax.ShapeDtypeStruct(m.shape, f32))
        shapes.append(jax.ShapeDtypeStruct(m.shape, bf16))
    return pl.pallas_call(
        functools.partial(step_body, devices, parts),
        in_specs=smem(1) + vmem(10),
        out_specs=vmem(12),
        out_shape=shapes,
        scratch_shapes=[pltpu.VMEM((LANES, LANES), f32)],
        compiler_params=scoped,
        name="update",
    )(fix, got, sums, weight, norm, pm, ps, nm, ns, km, ks)


def shifted(x, by):
    length = lax.axis_size("rows")
    pairs = [(i, i + by) for i in range(length) if 0 <= i + by < length]
    return lax.ppermute(x, "rows", pairs)


def exchange(x):
    return lax.all_to_all(x, ("rows", "scene"), 0, 0, tiled=True)


def body(
    points,
    pillar_counts,
    pillar_pixels,
    point_weight,
    point_master,
    point_states,
    norm_weight,
    norm_master,
    norm_states,
    kernel_weight,
    kernel_master,
    kernel_states,
    step_count,
    cotangent,
):
    size = points.shape[3]
    out_rows, scenes, channels, out_cols = cotangent.shape
    cols = 2 * out_cols
    devices = lax.axis_size("rows")
    scene_devices = lax.axis_size("scene")
    peers = devices * scene_devices
    cells = float(out_rows * scenes * out_cols * peers)
    own = kernel_weight.shape[0]
    parts = scene_devices if own % scene_devices == 0 else 1
    share = own // parts * channels
    mine = lax.axis_index("scene") if parts > 1 else jnp.int32(0)

    z, winner, edge, stats, moments = lift(
        mine.reshape(1, 1), points, pillar_counts, pillar_pixels, point_weight, norm_weight, kernel_weight.T, peers, share
    )
    edge = shifted(edge, 1)
    got = near(exchange(stats))
    held = scenes // 2 * EDGE
    far_pixels = edge[held : held + scenes].astype(jnp.int32)
    pairs = out_rows // 2
    own_pixels = pillar_pixels.reshape(scenes * pairs, 1, size // pairs)
    conv, pooled, sums, kernel = convolve(
        devices, parts, own_pixels, far_pixels, got, z, near(edge), norm_weight, pairs, out_cols
    )
    conv_stats = near(exchange(sums[:, None]))

    far_pixels = far_pixels[:, :EDGE]
    at = (pillar_pixels % cols) // 2
    own_at = (pillar_pixels // (2 * cols) + 1) * (out_cols + 8) + at
    take_at = jnp.concatenate([own_at, (far_pixels % cols) // 2], axis=1)
    take_at = jnp.pad(take_at, ((0, 0), (0, -(size + EDGE) % (16 * pairs))))
    take_at = take_at.reshape(scenes * pairs, 1, take_at.shape[1] // pairs)
    own_phase = (pillar_pixels // cols % 2) * 2 + pillar_pixels % 2
    phase = jnp.concatenate([own_phase, 2 + far_pixels % 2], axis=1)
    phase = jnp.pad(phase, ((0, 0), (0, LANES - EDGE))).astype(f32)[:, None]

    result, sums = normalize(cells, conv_stats, conv, cotangent, norm_weight)
    grad_sums = near(exchange(sums[:, None]))
    slots, own_edge, far, kgrad = gradients(
        cells, devices, parts, take_at, conv_stats, grad_sums, conv, cotangent, norm_weight, pooled, phase, kernel
    )
    far, kgrad = lax.optimization_barrier((shifted(far, -1), kgrad))
    if parts > 1:
        kgrad = lax.all_to_all(kgrad, "scene", 0, 0, tiled=True)
    else:
        kgrad = lax.psum(kgrad, "scene")
    rest = unlift(
        points, pillar_counts, point_weight, norm_weight, z, winner, slots, near(own_edge), near(far), near(moments)
    )
    if parts > 1:
        kgrad = jnp.sum(kgrad.reshape(scene_devices, devices, share), axis=0)
    kgrad = jnp.broadcast_to(kgrad[:, None], (devices, scene_devices, share)).reshape(peers, share)
    got = exchange(jnp.concatenate([kgrad, jnp.broadcast_to(rest, (peers, rest.shape[1]))], axis=1)[:, None])
    got = near(got)
    steps_done = step_count[0].astype(f32)
    fix = jnp.stack([1.0 - beta_one**steps_done, 1.0 - beta_two**steps_done])
    outs = update(
        devices,
        parts,
        fix,
        got,
        grad_sums,
        point_weight,
        norm_weight,
        point_master,
        jnp.transpose(point_states, (1, 0, 2)),
        norm_master,
        norm_states,
        kernel_master.T,
        jnp.transpose(kernel_states, (0, 2, 1)),
    )
    outs = list(outs)
    outs[1] = jnp.transpose(outs[1], (1, 0, 2))
    outs[8], outs[10], outs[11] = outs[8].T, outs[10].T, outs[11].T
    outs[9] = jnp.transpose(outs[9], (0, 2, 1))
    return (result, *outs)


def solution(mesh):
    placed = (
        P("scene", None, None, "rows"),
        P("scene", "rows"),
        P("scene", "rows"),
        P(),
        P(),
        P(),
        P(),
        P(),
        P(),
        P("rows", None),
        P("rows", None),
        P(None, "rows", None),
        P(),
        P("rows", "scene", None, None),
    )
    return jax.shard_map(
        body,
        mesh=mesh,
        in_specs=placed,
        out_specs=(
            P("rows", "scene", None, None),
            P(),
            P(),
            P(),
            P(),
            P(),
            P(),
            P(),
            P(),
            P("rows", None),
            P(None, "rows", None),
            P("rows", None),
            P("rows", None),
        ),
        check_vma=False,
    )
```

time: 163 us -> 205 us (1.26); the launches traced: 164 us -> 202 us
  local copies, waits for them, and re-layouts: 17.4 us -> 46.4 us
  Pallas kernels: 81.6 us -> 90.9 us
  starting transfers between devices: 27.1 us -> 24.7 us
    unnamed x29 -> x100, local copies, waits for them, and re-layouts: 14.1 us -> 44 us
    pallas_call x6, Pallas kernels: 81.6 us -> 90.9 us  [the longest x1 27.4 us: convolve(): pl.pallas_call(functools.partial(conv_body, devices, parts), in_specs=sme...]
    all_to_all x4, starting transfers between devices: 17.4 us -> 14.4 us  [exchange(): return lax.all_to_all(x, ('rows', 'scene'), 0, 0, tiled=True)]
    all_to_all x2 -> x0, local copies, waits for them, and re-layouts: 2.65 us -> none  [exchange(): return lax.all_to_all(x, ('rows', 'scene'), 0, 0, tiled=True)]
  transfers between devices with their start and end apart: 7 -> 7, of which waited for: 5 -> 5; matrix products, arithmetic and copies ran while one was open for 4% -> 1% of each run, Pallas kernels for 15% -> 7%
where the time goes in v3:
time: 205 us; the launch traced here: 202 us
  Pallas kernels  90.9 us (44%)
  local copies, waits for them, and re-layouts  46.4 us (23%)
  waiting for transfers between devices  35.6 us (17%)
  starting transfers between devices  24.7 us (12%)
  other arithmetic  2.45 us (1%)
    unnamed x100, local copies, waits for them, and re-layouts  44 us
    all_to_all x4, waiting for transfers between devices, exchange(): return lax.all_to_all(x, ('rows', 'scene'), 0, 0, tiled=True)  30.4 us
    pallas_call x1, Pallas kernels, convolve(): pl.pallas_call(functools.partial(conv_body, devices, parts), in_specs=sme...  27.4 us
    pallas_call x1, Pallas kernels, lift(): pl.pallas_call(lift_body, in_specs=smem(1) + hbm(1) + vmem(5), out_specs=...  21.8 us
    pallas_call x1, Pallas kernels, gradients(): pl.pallas_call(functools.partial(grad_body, cells, devices, parts), in_sp...  21.3 us
    pallas_call x1, Pallas kernels, unlift(): pl.pallas_call(unlift_body, in_specs=hbm(1) + vmem(3) + hbm(3) + vmem(3),...  15 us
    all_to_all x4, starting transfers between devices, exchange(): return lax.all_to_all(x, ('rows', 'scene'), 0, 0, tiled=True)  14.4 us
    ppermute x2, starting transfers between devices, shifted(): return lax.ppermute(x, 'rows', pairs)  6.13 us
  transfers between devices with their start and end apart: 7, of which 5 were waited for; matrix products, arithmetic and copies ran while one was open for 1% of the time, Pallas kernels for 7%

profile of v3, /device:TPU:0, one launch (start us, length us, event | category | flops | bytes accessed | tf_op | source)
XLA Modules:
  0.0 202.0 jit_solution(11310732927648108730)
XLA Ops:
  0.7 2.0 copy-done.3
  6.2 21.8 %lift.1 = (f32[8,768,128]{2,1,0:T(8,128)S(1)}, f32[8,768,128]{2,1,0:T(8,128)S(1)}, f32[208,128]{1,0:T(8,128)}, f32[32,1,1408]{2,1,0:T(1,128)}, f32[16,128]{1,0:T(8,128)S(1)}) custom-call(s32[1,1]{1,0:T(1,128)} %bitcast.mine, bf16[8,9,32,768]{3,2,1,0:T(8,128)(2,1)S(1)} %copy-done.3, s32[8,768]{1,0:T(8,128)S(1)} %copy-done.30, s32[8,768]{1,0:T(8,128)S(1)} %copy-done.15, ...), custom_call_target="tpu_custom_call" | custom-call | tf_op jit(solution)/shard_map/lift/pallas_call | solution.py:221
  28.0 1.6 copy-done.9
  30.3 4.8 %collective-permute-start = (f32[208,128]{1,0:T(8,128)}, f32[208,128]{1,0:T(8,128)S(1)}, u32[]{:S(2)}, u32[]{:S(2)}) collective-permute-start(f32[208,128]{1,0:T(8,128)} %get-tuple-element.42), channel_id=1, source_target_pairs={{0,4},{4,8},{8,12},{12,16},{16,20},{20,24},{24,28},{1,5},{5,9},{9,... | collective-permute-start | bytes 319496 | tf_op jit(solution)/shard_map/ppermute | solution.py:905
  35.1 4.9 %all-to-all-start = ((f32[32,1,1408]{2,1,0:T(1,128)}), f32[32,1,1408]{2,1,0:T(1,128)S(1)}, u32[]{:S(2)}, u32[]{:S(2)}) async-start(f32[32,1,1408]{2,1,0:T(1,128)} %get-tuple-element.43), calls=%async_computation | async-start | bytes 360448 | tf_op jit(solution)/shard_map/all_to_all | solution.py:909
  40.9 7.9 %all-to-all-done.got = f32[32,1,1408]{2,1,0:T(1,128)S(1)} async-done(((f32[32,1,1408]{2,1,0:T(1,128)}), f32[32,1,1408]{2,1,0:T(1,128)S(1)}, u32[]{:S(2)}, u32[]{:S(2)}) %all-to-all-start) | async-done | bytes 180256 | tf_op jit(solution)/shard_map/all_to_all | solution.py:909
  48.8 27.4 %convolve.1 = (f32[8,4,256,128]{3,2,1,0:T(8,128)S(1)}, bf16[8,896,128]{2,1,0:T(8,128)(2,1)S(1)}, f32[32,128]{1,0:T(8,128)}, bf16[576,64]{1,0:T(8,128)(2,1)S(1)}) custom-call(s32[32,1,192]{2,1,0:T(1,128)S(1)} %reshape.54.pix, s32[8,128]{1,0:T(8,128)S(1)} %slice_convert_fusion.far_pix, f32[32,1,1408]{2,1,0:T(1,128)S(1)} %all-to-all-done.got, ...), custom_call_target="tpu_custom_call" | custom-call | tf_op jit(solution)/shard_map/convolve/pallas_call | solution.py:415
  76.2 2.0 copy-done
  80.1 2.5 %all-to-all-start.1 = ((f32[32,1,128]{2,1,0:T(1,128)}), f32[32,1,128]{2,1,0:T(1,128)S(1)}, u32[]{:S(2)}, u32[]{:S(2)}) async-start(f32[32,1,128]{2,1,0:T(1,128)} %bitcast.2), calls=%async_computation.1 | async-start | bytes 32768 | tf_op jit(solution)/shard_map/all_to_all | solution.py:909
  82.7 7.1 %all-to-all-done.1.stats = f32[32,1,128]{2,1,0:T(1,128)S(1)} async-done(((f32[32,1,128]{2,1,0:T(1,128)}), f32[32,1,128]{2,1,0:T(1,128)S(1)}, u32[]{:S(2)}, u32[]{:S(2)}) %all-to-all-start.1) | async-done | bytes 16416 | tf_op jit(solution)/shard_map/all_to_all | solution.py:909
  89.8 2.2 %copy-done.1 = f32[8,4,256,128]{3,2,1,0:T(8,128)S(1)} copy-done((f32[8,4,256,128]{3,2,1,0:T(8,128)S(1)}, f32[8,4,256,128]{3,2,1,0:T(8,128)}, u32[]{:S(2)}) %copy-start.1) | copy-done | bytes 4194328
  91.9 1.6 copy-done.7
  93.5 4.0 %normalize.1 = (bf16[8,8,64,256]{3,2,1,0:T(8,128)(2,1)}, f32[32,128]{1,0:T(8,128)}) custom-call(f32[32,1,128]{2,1,0:T(1,128)S(1)} %all-to-all-done.1.stats, f32[8,4,256,128]{3,2,1,0:T(8,128)S(1)} %copy-done.1, bf16[8,8,64,256]{3,2,1,0:T(8,128)(2,1)S(1)} %copy-done.7, bf16[4,64]{1,0:T(4,128)(2,1)S(1)} %copy-done.36), custom_call_target="tpu_custom_call" | custom-call | tf_op jit(solution)/shard_map/normalize/pallas_call | solution.py:500
  97.5 2.6 %all-to-all-start.2 = ((f32[32,1,128]{2,1,0:T(1,128)}), f32[32,1,128]{2,1,0:T(1,128)S(1)}, u32[]{:S(2)}, u32[]{:S(2)}) async-start(f32[32,1,128]{2,1,0:T(1,128)} %bitcast.3), calls=%async_computation.2 | async-start | bytes 32768 | tf_op jit(solution)/shard_map/all_to_all | solution.py:909
  101.5 5.7 %all-to-all-done.2.sums = f32[32,1,128]{2,1,0:T(1,128)S(1)} async-done(((f32[32,1,128]{2,1,0:T(1,128)}), f32[32,1,128]{2,1,0:T(1,128)S(1)}, u32[]{:S(2)}, u32[]{:S(2)}) %all-to-all-start.2) | async-done | bytes 16416 | tf_op jit(solution)/shard_map/all_to_all | solution.py:909
  107.8 2.2 %copy-done.2 = f32[8,4,256,128]{3,2,1,0:T(8,128)S(1)} copy-done((f32[8,4,256,128]{3,2,1,0:T(8,128)S(1)}, f32[8,4,256,128]{3,2,1,0:T(8,128)}, u32[]{:S(2)}) %copy-start.2) | copy-done | bytes 4194328
  116.9 21.3 %gradients.1 = (bf16[8,896,128]{2,1,0:T(8,128)(2,1)S(1)}, f32[192,128]{1,0:T(8,128)S(1)}, f32[192,128]{1,0:T(8,128)S(1)}, f32[32,1152]{1,0:T(8,128)S(1)}) custom-call(s32[32,1,208]{2,1,0:T(1,128)S(1)} %copy-done.23, f32[32,1,128]{2,1,0:T(1,128)S(1)} %all-to-all-done.1.stats, f32[32,1,128]{2,1,0:T(1,128)S(1)} %copy-done.18, f32[8,4,256,128]{3,2,1,0:T(8,128)S(1)} %copy-done.2, ...), custom_call_target="tpu_custom_call" | custom-call | tf_op jit(solution)/shard_map/gradients/pallas_call | solution.py:663
  141.3 5.2 %collective-permute-done.1.far = f32[192,128]{1,0:T(8,128)S(1)} collective-permute-done((f32[192,128]{1,0:T(8,128)S(1)}, f32[192,128]{1,0:T(8,128)S(1)}, u32[]{:S(2)}, u32[]{:S(2)}) %collective-permute-start.1) | collective-permute-done | bytes 98336 | tf_op jit(solution)/shard_map/ppermute | solution.py:905
  147.2 4.1 %all-to-all-start.3 = ((f32[4,8,1152]{2,1,0:T(8,128)}), f32[4,8,1152]{2,1,0:T(8,128)}, u32[]{:S(2)}, u32[]{:S(2)}) async-start(f32[4,8,1152]{2,1,0:T(8,128)} %bitcast.13), calls=%async_computation.3 | async-start | bytes 294912 | tf_op jit(solution)/shard_map/all_to_all | solution.py:971
  151.3 1.9 copy-done.6
  153.2 1.9 copy-done.10
  161.2 15.0 %unlift.1 = f32[1,896]{1,0:T(1,128)S(1)} custom-call(bf16[8,9,32,768]{3,2,1,0:T(8,128)(2,1)S(1)} %copy-done.4, s32[8,768]{1,0:T(8,128)S(1)} %copy-done.31, bf16[9,64]{1,0:T(8,128)(2,1)S(1)} %copy-done.33, bf16[4,64]{1,0:T(4,128)(2,1)S(1)} %copy-done.38, f32[8,768,128]{2,1,0:T(8,128)S(1)} %copy-done.6, f32[8,768,128]{2,1,0:T(8,128)S(1)} %copy-done.10, ...), custom_call_target="tpu_custom_call" | custom-call | tf_op jit(solution)/shard_map/unlift/pallas_call | solution.py:791
  179.5 4.4 %all-to-all-start.4 = ((f32[32,1,2048]{2,1,0:T(1,128)}), f32[32,1,2048]{2,1,0:T(1,128)S(1)}, u32[]{:S(2)}, u32[]{:S(2)}) async-start(f32[32,1,2048]{2,1,0:T(1,128)} %broadcast_in_dim.31), calls=%async_computation.4 | async-start | bytes 524288 | tf_op jit(solution)/shard_map/all_to_all | solution.py:909
  184.7 9.8 %all-to-all-done.4.got = f32[32,1,2048]{2,1,0:T(1,128)S(1)} async-done(((f32[32,1,2048]{2,1,0:T(1,128)}), f32[32,1,2048]{2,1,0:T(1,128)S(1)}, u32[]{:S(2)}, u32[]{:S(2)}) %all-to-all-start.4) | async-done | bytes 262176 | tf_op jit(solution)/shard_map/all_to_all | solution.py:909
  (115 shorter events, 36.3 us)
Async XLA Ops:
  0.6 48.1 %copy-start.36 = (bf16[4,64]{1,0:T(4,128)(2,1)S(1)}, bf16[4,64]{1,0:T(4,128)(2,1)}, u32[]{:S(2)}) copy-start(bf16[4,64]{1,0:T(4,128)(2,1)} %norm.11) | copy-start | bytes 1540
  0.7 2.0 copy-start.3
  6.2 33.8 %copy-start.16 = (s32[8,768]{1,0:T(8,128)S(1)}, s32[8,768]{1,0:T(8,128)}, u32[]{:S(2)}) copy-start(s32[8,768]{1,0:T(8,128)} %pixels.1) | copy-start | bytes 73732
  28.0 1.7 copy-start.9
  30.3 67.3 %copy-start.5 = (f32[8,768,128]{2,1,0:T(8,128)}, f32[8,768,128]{2,1,0:T(8,128)S(1)}, u32[]{:S(2)}) copy-start(f32[8,768,128]{2,1,0:T(8,128)S(1)} %get-tuple-element.44.z_in.z) | copy-start | bytes 9437188
  30.3 10.6 %collective-permute-start = (f32[208,128]{1,0:T(8,128)}, f32[208,128]{1,0:T(8,128)S(1)}, u32[]{:S(2)}, u32[]{:S(2)}) collective-permute-start(f32[208,128]{1,0:T(8,128)} %get-tuple-element.42), channel_id=1, source_target_pairs={{0,4},{4,8},{8,12},{12,16},{16,20},{20,24},{24,28},{1,5},{5,9},{9,... | collective-permute-start | bytes 319496 | tf_op jit(solution)/shard_map/ppermute | solution.py:905
  35.1 13.7 %all-to-all-start = ((f32[32,1,1408]{2,1,0:T(1,128)}), f32[32,1,1408]{2,1,0:T(1,128)S(1)}, u32[]{:S(2)}, u32[]{:S(2)}) async-start(f32[32,1,1408]{2,1,0:T(1,128)} %get-tuple-element.43), calls=%async_computation | async-start | bytes 360448 | tf_op jit(solution)/shard_map/all_to_all | solution.py:909
  76.1 2.0 copy-start
  80.1 9.6 %all-to-all-start.1 = ((f32[32,1,128]{2,1,0:T(1,128)}), f32[32,1,128]{2,1,0:T(1,128)S(1)}, u32[]{:S(2)}, u32[]{:S(2)}) async-start(f32[32,1,128]{2,1,0:T(1,128)} %bitcast.2), calls=%async_computation.1 | async-start | bytes 32768 | tf_op jit(solution)/shard_map/all_to_all | solution.py:909
  89.8 2.2 %copy-start.1 = (f32[8,4,256,128]{3,2,1,0:T(8,128)S(1)}, f32[8,4,256,128]{3,2,1,0:T(8,128)}, u32[]{:S(2)}) copy-start(f32[8,4,256,128]{3,2,1,0:T(8,128)} %copy-done) | copy-start | bytes 12582916
  91.9 1.6 copy-start.7
  93.5 6.6 %copy-start.49 = (s32[8,768]{1,0:T(8,128)S(1)}, s32[8,768]{1,0:T(8,128)}, u32[]{:S(2)}) copy-start(s32[8,768]{1,0:T(8,128)} %get-tuple-element.74) | copy-start | bytes 73732
  97.5 9.6 %all-to-all-start.2 = ((f32[32,1,128]{2,1,0:T(1,128)}), f32[32,1,128]{2,1,0:T(1,128)S(1)}, u32[]{:S(2)}, u32[]{:S(2)}) async-start(f32[32,1,128]{2,1,0:T(1,128)} %bitcast.3), calls=%async_computation.2 | async-start | bytes 32768 | tf_op jit(solution)/shard_map/all_to_all | solution.py:909
  107.8 2.2 %copy-start.2 = (f32[8,4,256,128]{3,2,1,0:T(8,128)S(1)}, f32[8,4,256,128]{3,2,1,0:T(8,128)}, u32[]{:S(2)}) copy-start(f32[8,4,256,128]{3,2,1,0:T(8,128)} %copy-done) | copy-start | bytes 12582916
  110.0 1.6 copy-start.8
  111.6 1.5 copy-start.12
  116.9 34.5 %copy-start.4 = (bf16[8,9,32,768]{3,2,1,0:T(8,128)(2,1)S(1)}, bf16[8,9,32,768]{3,2,1,0:T(8,128)(2,1)}, u32[]{:S(2)}) copy-start(bf16[8,9,32,768]{3,2,1,0:T(8,128)(2,1)} %points.3) | copy-start | bytes 10616836
  140.0 7.1 %copy-start.20 = (f32[32,1152]{1,0:T(8,128)}, f32[32,1152]{1,0:T(8,128)S(1)}, u32[]{:S(2)}) copy-start(f32[32,1152]{1,0:T(8,128)S(1)} %get-tuple-element.53) | copy-start | bytes 442372
  140.0 6.5 %collective-permute-start.1 = (f32[192,128]{1,0:T(8,128)S(1)}, f32[192,128]{1,0:T(8,128)S(1)}, u32[]{:S(2)}, u32[]{:S(2)}) collective-permute-start(f32[192,128]{1,0:T(8,128)S(1)} %get-tuple-element.51), channel_id=1, source_target_pairs={{4,0},{8,4},{12,8},{16,12},{20,16},{24,20},{28,24},{5,1},{9,5},{13... | collective-permute-start | bytes 294920 | tf_op jit(solution)/shard_map/ppermute | solution.py:905
  147.2 30.4 %all-to-all-start.3 = ((f32[4,8,1152]{2,1,0:T(8,128)}), f32[4,8,1152]{2,1,0:T(8,128)}, u32[]{:S(2)}, u32[]{:S(2)}) async-start(f32[4,8,1152]{2,1,0:T(8,128)} %bitcast.13), calls=%async_computation.3 | async-start | bytes 294912 | tf_op jit(solution)/shard_map/all_to_all | solution.py:971
  151.3 1.9 copy-start.6
  153.2 1.9 copy-start.10
  161.2 33.3 %copy-start.19 = (f32[32,1,128]{2,1,0:T(1,128)S(1)}, f32[32,1,128]{2,1,0:T(1,128)}, u32[]{:S(2)}) copy-start(f32[32,1,128]{2,1,0:T(1,128)} %copy-done.17) | copy-start | bytes 49156
  179.5 15.0 %all-to-all-start.4 = ((f32[32,1,2048]{2,1,0:T(1,128)}), f32[32,1,2048]{2,1,0:T(1,128)S(1)}, u32[]{:S(2)}, u32[]{:S(2)}) async-start(f32[32,1,2048]{2,1,0:T(1,128)} %broadcast_in_dim.31), calls=%async_computation.4 | async-start | bytes 524288 | tf_op jit(solution)/shard_map/all_to_all | solution.py:909
  (33 other events, 25.5 us)

commit v4 on v3

--- a/solution.py
+++ b/solution.py
@@ -21,7 +21,6 @@
 BIG = 1e30
 PACK = 8
 TILE = 256
-SCOPE = 40 << 20
 LANES = 128
 f32 = jnp.float32
 bf16 = jnp.bfloat16
@@ -205,13 +204,6 @@
     return [pl.BlockSpec(memory_space=pltpu.HBM)] * count
 
 
-def near(x):
-    return pltpu.with_memory_space_constraint(x, pltpu.VMEM)
-
-
-scoped = pltpu.CompilerParams(vmem_limit_bytes=SCOPE)
-
-
 def lift(mine, points, counts, pixels, weight, norm, kernel, peers, share):
     scenes, feats, depth, size = points.shape
     channels = weight.shape[1]
@@ -240,7 +232,6 @@
             pltpu.VMEM((scenes, size, LANES), f32),
             pltpu.SemaphoreType.DMA((3, scenes)),
         ],
-        compiler_params=scoped,
         name="lift",
     )(mine, points, counts, pixels, weight, norm, kernel)
 
@@ -382,8 +373,8 @@
             place_far(dst, ahead)
 
             def step(j, _):
+                convolve_pair(src, s, j)
                 place(dst, ahead, j)
-                convolve_pair(src, s, j)
                 return 0
 
             lax.fori_loop(0, pairs, step, 0)
@@ -436,7 +427,6 @@
             pltpu.VMEM((scenes, size + LANES, LANES), bf16),
             pltpu.SemaphoreType.DMA((3, scenes)),
         ],
-        compiler_params=scoped,
         name="convolve",
     )(pix, far_pix, got, z, edge, norm)
 
@@ -512,7 +502,6 @@
             pltpu.VMEM(cot.shape, bf16),
             pltpu.SemaphoreType.DMA((3, scenes)),
         ],
-        compiler_params=scoped,
         name="normalize",
     )(stats, conv, cot, norm)
 
@@ -687,7 +676,6 @@
             pltpu.VMEM((scenes, rows, LANES), f32),
             pltpu.SemaphoreType.DMA((3, scenes)),
         ],
-        compiler_params=scoped,
         name="gradients",
     )(idx, stats, sums, conv, cot, norm, pooled, phase, kernel)
 
@@ -804,7 +792,6 @@
             pltpu.VMEM((TILE, LANES), f32),
             pltpu.SemaphoreType.DMA((3, scenes)),
         ],
-        compiler_params=scoped,
         name="unlift",
     )(points, counts, weight, norm, z, winner, slots, edge, far, moments)
 
@@ -894,7 +881,6 @@
         out_specs=vmem(12),
         out_shape=shapes,
         scratch_shapes=[pltpu.VMEM((LANES, LANES), f32)],
-        compiler_params=scoped,
         name="update",
     )(fix, got, sums, weight, norm, pm, ps, nm, ns, km, ks)
 
@@ -941,15 +927,15 @@
         mine.reshape(1, 1), points, pillar_counts, pillar_pixels, point_weight, norm_weight, kernel_weight.T, peers, share
     )
     edge = shifted(edge, 1)
-    got = near(exchange(stats))
+    got = exchange(stats)
     held = scenes // 2 * EDGE
     far_pixels = edge[held : held + scenes].astype(jnp.int32)
     pairs = out_rows // 2
     own_pixels = pillar_pixels.reshape(scenes * pairs, 1, size // pairs)
     conv, pooled, sums, kernel = convolve(
-        devices, parts, own_pixels, far_pixels, got, z, near(edge), norm_weight, pairs, out_cols
+        devices, parts, own_pixels, far_pixels, got, z, edge, norm_weight, pairs, out_cols
     )
-    conv_stats = near(exchange(sums[:, None]))
+    conv_stats = exchange(sums[:, None])
 
     far_pixels = far_pixels[:, :EDGE]
     at = (pillar_pixels % cols) // 2
@@ -962,7 +948,7 @@
     phase = jnp.pad(phase, ((0, 0), (0, LANES - EDGE))).astype(f32)[:, None]
 
     result, sums = normalize(cells, conv_stats, conv, cotangent, norm_weight)
-    grad_sums = near(exchange(sums[:, None]))
+    grad_sums = exchange(sums[:, None])
     slots, own_edge, far, kgrad = gradients(
         cells, devices, parts, take_at, conv_stats, grad_sums, conv, cotangent, norm_weight, pooled, phase, kernel
     )
@@ -972,13 +958,13 @@
     else:
         kgrad = lax.psum(kgrad, "scene")
     rest = unlift(
-        points, pillar_counts, point_weight, norm_weight, z, winner, slots, near(own_edge), near(far), near(moments)
+        points, pillar_counts, point_weight, norm_weight, z, winner, slots, own_edge, far, moments
     )
     if parts > 1:
         kgrad = jnp.sum(kgrad.reshape(scene_devices, devices, share), axis=0)
     kgrad = jnp.broadcast_to(kgrad[:, None], (devices, scene_devices, share)).reshape(peers, share)
     got = exchange(jnp.concatenate([kgrad, jnp.broadcast_to(rest, (peers, rest.shape[1]))], axis=1)[:, None])
-    got = near(got)
+    got = got
     steps_done = step_count[0].astype(f32)
     fix = jnp.stack([1.0 - beta_one**steps_done, 1.0 - beta_two**steps_done])
     outs = update(

time: 205 us -> 146 us (0.71)
  local copies, waits for them, and re-layouts: 46.4 us -> 5.62 us
  Pallas kernels: 90.9 us -> 76.8 us
    unnamed x100 -> x16, local copies, waits for them, and re-layouts: 44 us -> 2.58 us
    pallas_call x1, Pallas kernels: 27.4 us -> 19.8 us  [convolve(): pl.pallas_call(functools.partial(conv_body, devices, parts), in_specs=sme...]
    pallas_call x1, Pallas kernels: 15 us -> 11.8 us  [unlift(): pl.pallas_call(unlift_body, in_specs=hbm(1) + vmem(3) + hbm(3) + vmem(3),...]
    pallas_call x1, Pallas kernels: 21.8 us -> 18.7 us  [lift(): pl.pallas_call(lift_body, in_specs=smem(1) + hbm(1) + vmem(5), out_specs=...]
    pallas_call x1, Pallas kernels: 21.3 us -> 19 us  [gradients(): pl.pallas_call(functools.partial(grad_body, cells, devices, parts), in_sp...]
  transfers between devices with their start and end apart: 7 -> 7, of which waited for: 5 -> 5; matrix products, arithmetic and copies ran while one was open for 1% -> 2% of each run, Pallas kernels for 7% -> 8%
where the time goes in v4:
time: 146 us; the launch traced here: 144 us
  Pallas kernels  76.8 us (53%)
  waiting for transfers between devices  35.2 us (24%)
  starting transfers between devices  22.8 us (16%)
  local copies, waits for them, and re-layouts  5.62 us (4%)
  between operations  1.61 us (1%)
  other arithmetic  1.51 us (1%)
    all_to_all x4, waiting for transfers between devices, exchange(): return lax.all_to_all(x, ('rows', 'scene'), 0, 0, tiled=True)  29.8 us
    pallas_call x1, Pallas kernels, convolve(): pl.pallas_call(functools.partial(conv_body, devices, parts), in_specs=sme...  19.8 us
    pallas_call x1, Pallas kernels, gradients(): pl.pallas_call(functools.partial(grad_body, cells, devices, parts), in_sp...  19 us
    pallas_call x1, Pallas kernels, lift(): pl.pallas_call(lift_body, in_specs=smem(1) + hbm(1) + vmem(5), out_specs=...  18.7 us
    all_to_all x4, starting transfers between devices, exchange(): return lax.all_to_all(x, ('rows', 'scene'), 0, 0, tiled=True)  13.3 us
    pallas_call x1, Pallas kernels, unlift(): pl.pallas_call(unlift_body, in_specs=hbm(1) + vmem(3) + hbm(3) + vmem(3),...  11.8 us
    ppermute x2, starting transfers between devices, shifted(): return lax.ppermute(x, 'rows', pairs)  6.15 us
    pallas_call x1, Pallas kernels, normalize(): pl.pallas_call(functools.partial(norm_body, cells), in_specs=vmem(1) + hb...  5.61 us
  transfers between devices with their start and end apart: 7, of which 5 were waited for; matrix products, arithmetic and copies ran while one was open for 2% of the time, Pallas kernels for 8%

profile of v4, /device:TPU:0, one launch (start us, length us, event | category | flops | bytes accessed | tf_op | source)
XLA Modules:
  0.0 143.6 jit_solution(7850374806724388225)
XLA Ops:
  0.7 18.7 %lift.1 = (f32[8,768,128]{2,1,0:T(8,128)}, f32[8,768,128]{2,1,0:T(8,128)}, f32[208,128]{1,0:T(8,128)}, f32[32,1,1408]{2,1,0:T(1,128)}, f32[16,128]{1,0:T(8,128)}) custom-call(s32[1,1]{1,0:T(1,128)} %bitcast.mine, bf16[8,9,32,768]{3,2,1,0:T(8,128)(2,1)} %points.3, s32[8,768]{1,0:T(8,128)} %counts.3, s32[8,768]{1,0:T(8,128)} %pixels.1, bf16[9,64]{1,0:T(8,128)(2,1)} %weight.5, ...), custom_call_target="tpu_custom_call" | custom-call | tf_op jit(solution)/shard_map/lift/pallas_call | solution.py:213
  19.3 4.9 %collective-permute-start = (f32[208,128]{1,0:T(8,128)}, f32[208,128]{1,0:T(8,128)S(1)}, u32[]{:S(2)}, u32[]{:S(2)}) collective-permute-start(f32[208,128]{1,0:T(8,128)} %get-tuple-element.42), channel_id=1, source_target_pairs={{0,4},{4,8},{8,12},{12,16},{16,20},{20,24},{24,28},{1,5},{5,9},{9,... | collective-permute-start | bytes 319496 | tf_op jit(solution)/shard_map/ppermute | solution.py:891
  24.2 4.9 %all-to-all-start = ((f32[32,1,1408]{2,1,0:T(1,128)}), f32[32,1,1408]{2,1,0:T(1,128)S(1)}, u32[]{:S(2)}, u32[]{:S(2)}) async-start(f32[32,1,1408]{2,1,0:T(1,128)} %get-tuple-element.43), calls=%async_computation | async-start | bytes 360448 | tf_op jit(solution)/shard_map/all_to_all | solution.py:895
  29.2 0.7 reshape.54.pix
  30.0 7.9 %all-to-all-done.got = f32[32,1,1408]{2,1,0:T(1,128)S(1)} async-done(((f32[32,1,1408]{2,1,0:T(1,128)}), f32[32,1,1408]{2,1,0:T(1,128)S(1)}, u32[]{:S(2)}, u32[]{:S(2)}) %all-to-all-start) | async-done | bytes 180256 | tf_op jit(solution)/shard_map/all_to_all | solution.py:895
  37.9 0.7 copy-done.1
  38.5 19.8 %convolve.1 = (f32[8,4,256,128]{3,2,1,0:T(8,128)}, bf16[8,896,128]{2,1,0:T(8,128)(2,1)}, f32[32,128]{1,0:T(8,128)}, bf16[576,64]{1,0:T(8,128)(2,1)}) custom-call(s32[32,1,192]{2,1,0:T(1,128)} %reshape.54.pix, s32[8,128]{1,0:T(8,128)} %copy-done.7, f32[32,1,1408]{2,1,0:T(1,128)} %copy-done.1, f32[8,768,128]{2,1,0:T(8,128)} %get-tuple-element.44.z_in.z, ...), custom_call_target="tpu_custom_call" | custom-call | tf_op jit(solution)/shard_map/convolve/pallas_call | solution.py:406
  58.3 2.6 %all-to-all-start.1 = ((f32[32,1,128]{2,1,0:T(1,128)}), f32[32,1,128]{2,1,0:T(1,128)S(1)}, u32[]{:S(2)}, u32[]{:S(2)}) async-start(f32[32,1,128]{2,1,0:T(1,128)} %bitcast.19), calls=%async_computation.1 | async-start | bytes 32768 | tf_op jit(solution)/shard_map/all_to_all | solution.py:895
  60.9 7.1 %all-to-all-done.1.stats = f32[32,1,128]{2,1,0:T(1,128)S(1)} async-done(((f32[32,1,128]{2,1,0:T(1,128)}), f32[32,1,128]{2,1,0:T(1,128)S(1)}, u32[]{:S(2)}, u32[]{:S(2)}) %all-to-all-start.1) | async-done | bytes 16416 | tf_op jit(solution)/shard_map/all_to_all | solution.py:895
  68.6 5.6 %normalize.1 = (bf16[8,8,64,256]{3,2,1,0:T(8,128)(2,1)}, f32[32,128]{1,0:T(8,128)}) custom-call(f32[32,1,128]{2,1,0:T(1,128)} %copy-done.3, f32[8,4,256,128]{3,2,1,0:T(8,128)} %get-tuple-element.46.conv_in, bf16[8,8,64,256]{3,2,1,0:T(8,128)(2,1)} %cot_in.3, bf16[4,64]{1,0:T(4,128)(2,1)} %norm.11), custom_call_target="tpu_custom_call" | custom-call | tf_op jit(solution)/shard_map/normalize/pallas_call | solution.py:490
  74.2 2.6 %all-to-all-start.2 = ((f32[32,1,128]{2,1,0:T(1,128)}), f32[32,1,128]{2,1,0:T(1,128)S(1)}, u32[]{:S(2)}, u32[]{:S(2)}) async-start(f32[32,1,128]{2,1,0:T(1,128)} %bitcast.18), calls=%async_computation.2 | async-start | bytes 32768 | tf_op jit(solution)/shard_map/all_to_all | solution.py:895
  76.8 0.7 reshape.58.idx
  78.1 5.7 %all-to-all-done.2.sums = f32[32,1,128]{2,1,0:T(1,128)S(1)} async-done(((f32[32,1,128]{2,1,0:T(1,128)}), f32[32,1,128]{2,1,0:T(1,128)S(1)}, u32[]{:S(2)}, u32[]{:S(2)}) %all-to-all-start.2) | async-done | bytes 16416 | tf_op jit(solution)/shard_map/all_to_all | solution.py:895
  84.4 19.0 %gradients.1 = (bf16[8,896,128]{2,1,0:T(8,128)(2,1)}, f32[192,128]{1,0:T(8,128)}, f32[192,128]{1,0:T(8,128)}, f32[32,1152]{1,0:T(8,128)}) custom-call(s32[32,1,208]{2,1,0:T(1,128)} %reshape.58.idx, f32[32,1,128]{2,1,0:T(1,128)} %copy-done.3, f32[32,1,128]{2,1,0:T(1,128)} %copy-done.4, f32[8,4,256,128]{3,2,1,0:T(8,128)} %get-tuple-element.46.conv_in, ...), custom_call_target="tpu_custom_call" | custom-call | tf_op jit(solution)/shard_map/gradients/pallas_call | solution.py:652
  103.4 1.3 collective-permute-start.1
  104.7 5.4 %collective-permute-done.1.far = f32[192,128]{1,0:T(8,128)S(1)} collective-permute-done((f32[192,128]{1,0:T(8,128)}, f32[192,128]{1,0:T(8,128)S(1)}, u32[]{:S(2)}, u32[]{:S(2)}) %collective-permute-start.1) | collective-permute-done | bytes 98336 | tf_op jit(solution)/shard_map/ppermute | solution.py:891
  110.1 3.3 %all-to-all-start.3 = ((f32[4,8,1152]{2,1,0:T(8,128)}), f32[4,8,1152]{2,1,0:T(8,128)S(1)}, u32[]{:S(2)}, u32[]{:S(2)}) async-start(f32[4,8,1152]{2,1,0:T(8,128)} %bitcast.13), calls=%async_computation.3 | async-start | bytes 294912 | tf_op jit(solution)/shard_map/all_to_all | solution.py:957
  113.5 11.8 %unlift.1 = f32[1,896]{1,0:T(1,128)} custom-call(bf16[8,9,32,768]{3,2,1,0:T(8,128)(2,1)} %points.3, s32[8,768]{1,0:T(8,128)} %counts.3, bf16[9,64]{1,0:T(8,128)(2,1)} %weight.5, bf16[4,64]{1,0:T(4,128)(2,1)} %norm.11, f32[8,768,128]{2,1,0:T(8,128)} %get-tuple-element.44.z_in.z, f32[8,768,128]{2,1,0:T(8,128)} %get-tuple-element.54.winner_in, ...), custom_call_target="tpu_custom_call" | custom-call | tf_op jit(solution)/shard_map/unlift/pallas_call | solution.py:779
  125.2 0.7 reduce.1
  126.1 0.9 broadcast_in_dim.31
  127.0 3.3 %all-to-all-start.4 = ((f32[32,1,2048]{2,1,0:T(1,128)}), f32[32,1,2048]{2,1,0:T(1,128)S(1)}, u32[]{:S(2)}, u32[]{:S(2)}) async-start(f32[32,1,2048]{2,1,0:T(1,128)} %broadcast_in_dim.31), calls=%async_computation.4 | async-start | bytes 524288 | tf_op jit(solution)/shard_map/all_to_all | solution.py:895
  131.6 9.2 %all-to-all-done.4.got = f32[32,1,2048]{2,1,0:T(1,128)S(1)} async-done(((f32[32,1,2048]{2,1,0:T(1,128)}), f32[32,1,2048]{2,1,0:T(1,128)S(1)}, u32[]{:S(2)}, u32[]{:S(2)}) %all-to-all-start.4) | async-done | bytes 262176 | tf_op jit(solution)/shard_map/all_to_all | solution.py:895
  140.9 0.7 copy-done
  141.6 2.1 %update.1 = (f32[9,64]{1,0:T(8,128)}, f32[9,2,64]{2,1,0:T(2,128)}, f32[9,64]{1,0:T(8,128)}, bf16[9,64]{1,0:T(8,128)(2,1)}, f32[4,64]{1,0:T(4,128)}, /*index=5*/f...) custom-call(f32[2]{0:T(128)} %pad_maximum_fusion.1.fix, ...), custom_call_target="tpu_custom_call" | custom-call | tf_op jit(solution)/shard_map/update/pallas_call | solution.py:878
  (31 shorter events, 2.8 us)
Async XLA Ops:
  0.6 28.5 %copy-start.2 = (s32[8,768]{1,0:T(8,128)S(1)}, s32[8,768]{1,0:T(8,128)}, u32[]{:S(2)}) copy-start(s32[8,768]{1,0:T(8,128)} %pixels.1) | copy-start | bytes 73732
  19.3 10.6 %collective-permute-start = (f32[208,128]{1,0:T(8,128)}, f32[208,128]{1,0:T(8,128)S(1)}, u32[]{:S(2)}, u32[]{:S(2)}) collective-permute-start(f32[208,128]{1,0:T(8,128)} %get-tuple-element.42), channel_id=1, source_target_pairs={{0,4},{4,8},{8,12},{12,16},{16,20},{20,24},{24,28},{1,5},{5,9},{9,... | collective-permute-start | bytes 319496 | tf_op jit(solution)/shard_map/ppermute | solution.py:891
  24.2 13.7 %all-to-all-start = ((f32[32,1,1408]{2,1,0:T(1,128)}), f32[32,1,1408]{2,1,0:T(1,128)S(1)}, u32[]{:S(2)}, u32[]{:S(2)}) async-start(f32[32,1,1408]{2,1,0:T(1,128)} %get-tuple-element.43), calls=%async_computation | async-start | bytes 360448 | tf_op jit(solution)/shard_map/all_to_all | solution.py:895
  29.9 7.9 %copy-start.5 = (f32[208,128]{1,0:T(8,128)}, f32[208,128]{1,0:T(8,128)S(1)}, u32[]{:S(2)}) copy-start(f32[208,128]{1,0:T(8,128)S(1)} %collective-permute-done.edge) | copy-start | bytes 319492
  29.9 7.9 %copy-start.7 = (s32[8,128]{1,0:T(8,128)}, s32[8,128]{1,0:T(8,128)S(1)}, u32[]{:S(2)}) copy-start(s32[8,128]{1,0:T(8,128)S(1)} %slice_convert_fusion.far_pix) | copy-start | bytes 12292
  37.9 0.7 copy-start.1
  58.3 9.6 %all-to-all-start.1 = ((f32[32,1,128]{2,1,0:T(1,128)}), f32[32,1,128]{2,1,0:T(1,128)S(1)}, u32[]{:S(2)}, u32[]{:S(2)}) async-start(f32[32,1,128]{2,1,0:T(1,128)} %bitcast.19), calls=%async_computation.1 | async-start | bytes 32768 | tf_op jit(solution)/shard_map/all_to_all | solution.py:895
  68.0 0.6 copy-start.3
  74.2 9.6 %all-to-all-start.2 = ((f32[32,1,128]{2,1,0:T(1,128)}), f32[32,1,128]{2,1,0:T(1,128)S(1)}, u32[]{:S(2)}, u32[]{:S(2)}) async-start(f32[32,1,128]{2,1,0:T(1,128)} %bitcast.18), calls=%async_computation.2 | async-start | bytes 32768 | tf_op jit(solution)/shard_map/all_to_all | solution.py:895
  83.8 0.6 copy-start.4
  103.4 6.7 %collective-permute-start.1 = (f32[192,128]{1,0:T(8,128)}, f32[192,128]{1,0:T(8,128)S(1)}, u32[]{:S(2)}, u32[]{:S(2)}) collective-permute-start(f32[192,128]{1,0:T(8,128)} %get-tuple-element.51), channel_id=1, source_target_pairs={{4,0},{8,4},{12,8},{16,12},{20,16},{24,20},{28,24},{5,1},{9,5},{13... | collective-permute-start | bytes 294920 | tf_op jit(solution)/shard_map/ppermute | solution.py:891
  110.1 3.3 %copy-start.6 = (f32[192,128]{1,0:T(8,128)}, f32[192,128]{1,0:T(8,128)S(1)}, u32[]{:S(2)}) copy-start(f32[192,128]{1,0:T(8,128)S(1)} %collective-permute-done.1.far) | copy-start | bytes 294916
  110.1 15.8 %all-to-all-start.3 = ((f32[4,8,1152]{2,1,0:T(8,128)}), f32[4,8,1152]{2,1,0:T(8,128)S(1)}, u32[]{:S(2)}, u32[]{:S(2)}) async-start(f32[4,8,1152]{2,1,0:T(8,128)} %bitcast.13), calls=%async_computation.3 | async-start | bytes 294912 | tf_op jit(solution)/shard_map/all_to_all | solution.py:957
  127.0 13.9 %all-to-all-start.4 = ((f32[32,1,2048]{2,1,0:T(1,128)}), f32[32,1,2048]{2,1,0:T(1,128)S(1)}, u32[]{:S(2)}, u32[]{:S(2)}) async-start(f32[32,1,2048]{2,1,0:T(1,128)} %broadcast_in_dim.31), calls=%async_computation.4 | async-start | bytes 524288 | tf_op jit(solution)/shard_map/all_to_all | solution.py:895
  140.9 0.7 copy-start

commit v5 on v4

--- a/solution.py
+++ b/solution.py
@@ -121,7 +121,6 @@
     lift_table(weight, norm, table)
     gram[...] = jnp.zeros_like(gram)
     edge[...] = jnp.zeros_like(edge)
-    second_half = (iota((1, LANES), 1) >= channels).astype(f32)
 
     def scene(s, _):
         copy_in(points, pts, sems.at[0], s).wait()
@@ -137,8 +136,7 @@
                 for q in range(PACK // 4):
                     l = dot_nn(turned, table[:, q * 256 : (q + 1) * 256])
                     one, two = l[:, :LANES], l[:, LANES:]
-                    n_one = second_half + float(part * PACK + q * 4)
-                    n_two = n_one + 2.0
+                    n_one, n_two = float(part * PACK + q * 4), float(part * PACK + q * 4 + 2)
                     m = jnp.maximum(one, two)
                     first = jnp.where(two > one, n_two, n_one)
                     last = jnp.where(two >= one, n_two, n_one)
@@ -148,6 +146,8 @@
                         last = jnp.where(m >= old, last, high[at, :])
                         m = jnp.maximum(old, m)
                     if part == depth // PACK - 1 and q == PACK // 4 - 1:
+                        upper = (iota((TILE, LANES), 1) >= channels).astype(f32)
+                        first, last = first + upper, last + upper
                         other = swap_halves(m)
                         first = jnp.where(other > m, swap_halves(first), first)
                         last = jnp.where(other >= m, swap_halves(last), last)
@@ -294,7 +294,6 @@
         end = jnp.concatenate([tap(kern, low, 2), tap(kern, high, 2), tap(kern, low, 0), tap(kern, high, 0)], axis=1)
         taps[w] = jnp.concatenate([top, end], axis=0).astype(bf16)
     grid_a[...] = jnp.zeros_like(grid_a)
-    grid_b[...] = jnp.zeros_like(grid_b)
     side[...] = jnp.zeros_like(side)
     acc[...] = jnp.zeros_like(acc)
 
@@ -304,30 +303,33 @@
 
     own_at = 8 + cols
     far_at = 8 - last_row
-
-    def fill(s):
-        zs = z[s]
+    some = size // pairs
+
+    def part_of(j):
+        return pl.ds(j * some if isinstance(j, int) else pl.multiple_of(j * some, 16), some)
+
+    def fill(s, j):
+        zs = z[s, part_of(j), :]
         own = pool(zs, zs > -0.5 * BIG)
-        pooled[s, :size] = own
-        source[:size] = own.astype(f32)
+        pooled[s, part_of(j), :] = own
+        source[part_of(j), :] = own.astype(f32)
+
+    def fill_far(dst, s):
         far = edge_rows_of(edge, s, scenes, iota((EDGE, LANES), 1) < channels)
         flag = edge[edge.shape[0] - scenes : edge.shape[0] - scenes + 1, :]
         far = pool(far, (far > -0.5 * BIG) & (flag > 0.5))
         pooled[s, size:] = jnp.concatenate([far, jnp.zeros((LANES - EDGE, LANES), bf16)], axis=0)
         source[size : size + EDGE] = far.astype(f32)
-
-    def place_far(dst, s):
         for p in range(EDGE):
             at = jnp.maximum(far_pix[s, p], last_row) + far_at
             dst[pl.ds(at, 1), :] = source[size + p : size + p + 1, :]
 
     def place(dst, s, j):
         rows = dst.at[pl.ds(own_at, 4 * pairs * cols), :]
-        some = size // pairs
-        line = s * pairs + j
-        base = pl.multiple_of(j * some, 8)
+        line = pix.at[s * pairs + j]
+        values = source.at[part_of(j), :]
         for p in range(some):
-            rows[pl.ds(pix[line, 0, p], 1), :] = source[pl.ds(base + p, 1), :]
+            rows[pl.ds(line[0, p], 1), :] = values[p : p + 1, :]
 
     left = iota((out_cols, LANES), 1) < channels
 
@@ -344,17 +346,18 @@
         conv[s, j] = value
         acc[0:8] += jnp.sum(value.reshape(out_cols // 8, 8, LANES), axis=0)
         acc[8:16] += jnp.sum((value * value).reshape(out_cols // 8, 8, LANES), axis=0)
-        base = pl.multiple_of(8 + 4 * j * cols, 8)
-        src[pl.ds(base, 4 * cols), :] = jnp.zeros((4 * cols, LANES), f32)
-
-    def clear_last(src):
-        src[8 + 4 * pairs * cols : 8 + (4 * pairs + 1) * cols, :] = jnp.zeros((cols, LANES), f32)
+        used = (5 if j == pairs - 1 else 4) * cols
+        base = 8 + 4 * j * cols
+        src[base : base + used, :] = jnp.zeros((used, LANES), f32)
 
     copy_in(z_in, z, sems.at[0], 0).wait()
-    fill(0)
-    place_far(grid_a, 0)
+    fill_far(grid_a, 0)
+    grid_b[:8, :] = jnp.zeros((8, LANES), f32)
+    grid_b[8 + 4 * pairs * cols :, :] = jnp.zeros((grid_b.shape[0] - 8 - 4 * pairs * cols, LANES), f32)
 
     def start(j, _):
+        grid_b[pl.ds(pl.multiple_of(8 + 4 * j * cols, 8), 4 * cols), :] = jnp.zeros((4 * cols, LANES), f32)
+        fill(0, j)
         place(grid_a, 0, j)
         return 0
 
@@ -369,16 +372,12 @@
             def _():
                 copy_in(z_in, z, sems.at[0], s + 1).wait()
 
-            fill(ahead)
-            place_far(dst, ahead)
-
-            def step(j, _):
+            fill_far(dst, ahead)
+            for j in range(pairs):
+                fill(ahead, j)
+                place(dst, ahead, j)
                 convolve_pair(src, s, j)
-                place(dst, ahead, j)
-                return 0
-
-            lax.fori_loop(0, pairs, step, 0)
-            clear_last(src)
+
             copy_in(conv, conv_out, sems.at[1], s).start()
             copy_in(pooled, pooled_out, sems.at[2], s).start()
         return 0
@@ -508,17 +507,17 @@
 
 def grad_body(
     cells, devices, parts, idx, stats, sums, conv_in, cot_in, norm, pooled_in, phase, kernel, slots_out, edge, far, kgrad,
-    taps, field_a, field_b, taken_a, taken_b, turn, column, acc, rows_k, conv, cot, pooled, slots, exact, sems,
+    taps, field_a, field_b, taken_a, taken_b, turn, column_a, column_b, acc, rows_k, conv, cot, pooled, slots_a, slots_b, exact_a, exact_b, sems,
 ):
     scenes, pairs, out_cols, _ = conv.shape
     channels = norm.shape[1]
-    size = slots.shape[1]
+    size = slots_a.shape[0]
     strip = out_cols + 8
     some = idx.shape[2]
+    columns, slots, exact = (column_a, column_b), (slots_a, slots_b), (exact_a, exact_b)
     for s in range(scenes):
         copy_in(conv_in, conv, sems.at[0], s).start()
         scene_copy(cot_in, cot, sems.at[1], s).start()
-    for s in range(scenes):
         copy_in(pooled_in, pooled, sems.at[2], s).start()
     for hp in range(2):
         for up in range(2):
@@ -537,13 +536,12 @@
     for block in (field_a, field_b, taken_a, taken_b, acc):
         block[...] = jnp.zeros_like(block)
 
-    def phases(s, _):
-        for c in range(column.shape[1] // LANES):
+    def phases(column, s, j):
+        chunks = column.shape[0] // LANES
+        for c in range(j * chunks // pairs, (j + 1) * chunks // pairs):
             row = phase[s, :, c * LANES : (c + 1) * LANES]
-            column[s, c * LANES : (c + 1) * LANES, :] = jnp.transpose(jnp.broadcast_to(row, (LANES, LANES)))
-        return 0
-
-    lax.fori_loop(0, scenes, phases, 0)
+            column[c * LANES : (c + 1) * LANES, :] = jnp.transpose(jnp.broadcast_to(row, (LANES, LANES)))
+
     mean, inv, gain, bias = conv_params(cells, stats, norm)
     bias_grad, gain_grad = split_sums(sums, channels)
     scale = gain * inv / cells
@@ -553,79 +551,93 @@
     def field(dst, s, j):
         xhat = (conv[s, j] - mean) * inv
         pre = gain * xhat + bias
-        both = cot[pl.ds(2 * j, 2), s].reshape(2 * channels, out_cols)
+        both = cot[2 * j : 2 * j + 2, s].reshape(2 * channels, out_cols)
         back = jnp.where(pre > 0, jnp.transpose(both).astype(f32), 0.0)
         grad = scale * (cells * back - bias_grad - xhat * gain_grad)
         grad = grad.astype(bf16).astype(f32)
         turned = swap_halves(grad)
-        base = pl.multiple_of(2 * j * strip, 8)
-        dst[pl.ds(base, out_cols), :] = jnp.where(left, turn[...], turned)
-        dst[pl.ds(pl.multiple_of(base + strip, 8), out_cols), :] = grad
+        base = 2 * j * strip
+        dst[base : base + out_cols, :] = jnp.where(left, turn[...], turned)
+        dst[base + strip : base + strip + out_cols, :] = grad
         turn[...] = turned
 
     def take(dst, src, s, j):
-        line = s * pairs + j
+        line = idx.at[s * pairs + j]
         for p in range(some):
-            dst[2 * p : 2 * p + 2, :] = src[pl.ds(idx[line, 0, p], 2), :]
-
-    def product(src, s, j):
-        at = pl.ds(pl.multiple_of(j * some, 16), some)
+            dst[2 * p : 2 * p + 2, :] = src[pl.ds(line[0, p], 2), :]
+
+    def product(src, k, s, j):
+        at = slice(j * some, (j + 1) * some)
         part = jnp.concatenate([src[pl.ds(0, some, stride=2), :], src[pl.ds(1, some, stride=2), :]], axis=1).astype(bf16)
         out = dot_nt(part, taps[...])
-        ph = column[s, at, :]
+        ph = columns[k][at, :]
         is_even = ph == half
         is_odd = ph == half + 2.0
         value = jnp.where(is_even, out[:, :LANES], 0.0) + jnp.where(is_odd, out[:, LANES:], 0.0)
         value = value + swap_halves(value)
         pf = pooled[s, at, :].astype(f32)
         value = jnp.where(pf > 0, value, 0.0)
-        exact[s, at, :] = value
-        slots[s, at, :] = value.astype(bf16)
+        exact[k][at, :] = value
+        slots[k][at, :] = value.astype(bf16)
         split = jnp.concatenate([jnp.where(is_even, pf, 0.0), jnp.where(is_odd, pf, 0.0)], axis=1)
         acc[...] += dot_tn(split.astype(bf16), part)
 
-    def walk(dst, src, s):
+    def copy_out(k, s):
+        return pltpu.make_async_copy(slots[k], slots_out.at[s], sems.at[3, k])
+
+    def done(k, s):
+        half_store(edge, s, scenes, exact[k][:EDGE, :])
+        half_store(far, s, scenes, exact[k][size - LANES : size - LANES + EDGE, :])
+        slots[k][:EDGE, :] = jnp.zeros((EDGE, LANES), bf16)
+        copy_out(k, s).start()
+
+    def walk(dst, src, k, s):
         before = jnp.clip(s - 1, 0, scenes - 1)
-        older = jnp.clip(s - 2, 0, scenes - 1)
-
-        def step(i, _):
-            for k, (to, of) in enumerate(((taken_a, taken_b), (taken_b, taken_a))):
-                j = 2 * i + k
-                if dst is not None:
-                    field(dst, s, j)
-                take(to, src, before, j)
-                last = jnp.where(j > 0, before, older)
-                product(of, last, jnp.where(j > 0, j - 1, pairs - 1))
-            return 0
-
+        held = jnp.where(s > 0, s - 1, scenes)
+        older = jnp.where(s > 1, s - 2, scenes)
         if dst is not None:
             copy_in(conv_in, conv, sems.at[0], s).wait()
             scene_copy(cot_in, cot, sems.at[1], s).wait()
-            copy_in(pooled_in, pooled, sems.at[2], s).wait()
             turn[...] = jnp.zeros_like(turn)
-        lax.fori_loop(0, pairs // 2, step, 0)
+
+        @pl.when(s > 0)
+        def _():
+            copy_in(pooled_in, pooled, sems.at[2], before).wait()
+
+
+        @pl.when(s >= 3)
+        def _():
+            copy_out(1 - k, s - 3).wait()
+
+        for j in range(pairs):
+            to, of = ((taken_a, taken_b), (taken_b, taken_a))[j % 2]
+            if dst is not None:
+                phases(columns[k], s, j)
+                field(dst, s, j)
+            take(to, src, before, j)
+            product(of, k if j == 0 else 1 - k, held if j > 0 else older, (j - 1) % pairs)
+
+        @pl.when(s >= 2)
+        def _():
+            done(k, s - 2)
+
         if dst is not None:
             dst[2 * pairs * strip : 2 * pairs * strip + out_cols, :] = jnp.where(left, turn[...], 0.0)
 
     def two_scenes(i, _):
-        walk(field_a, field_b, 2 * i)
-        walk(field_b, field_a, 2 * i + 1)
+        walk(field_a, field_b, 0, 2 * i)
+        walk(field_b, field_a, 1, 2 * i + 1)
         return 0
 
-    lax.fori_loop(0, scenes // 2, two_scenes, 0)
-    walk(None, field_b, scenes)
-    product(taken_b, scenes - 1, pairs - 1)
-    for s in range(scenes):
-        copy_in(slots, slots_out, sems.at[0], s).start()
     far[...] = jnp.zeros_like(far)
     edge[...] = jnp.zeros_like(edge)
-
-    def pick(s, _):
-        half_store(edge, s, scenes, exact[s, :EDGE, :])
-        half_store(far, s, scenes, exact[s, size - LANES : size - LANES + EDGE, :])
-        return 0
-
-    lax.fori_loop(0, scenes, pick, 0)
+    for block in (column_a, column_b):
+        block[...] = jnp.zeros_like(block)
+    pooled[scenes] = jnp.zeros_like(pooled[scenes])
+    lax.fori_loop(0, scenes // 2, two_scenes, 0)
+    walk(None, field_b, 0, scenes)
+    product(taken_b, 1, scenes - 1, pairs - 1)
+    done(1, scenes - 1)
     for a in range(3):
         for b in range(3):
             hp, dr = ((1, 1), (0, 0), (1, 0))[a]
@@ -641,8 +653,8 @@
         for j in range(share):
             lanes = slice(j * channels, (j + 1) * channels)
             kgrad[q * devices : (q + 1) * devices, lanes] = rows_k[pl.ds(q * share + j, devices, stride=own), :]
-    for s in range(scenes):
-        copy_in(slots, slots_out, sems.at[0], s).wait()
+    copy_out(0, scenes - 2).wait()
+    copy_out(1, scenes - 1).wait()
 
 
 def gradients(cells, devices, parts, idx, stats, sums, conv, cot, norm, pooled, phase, kernel):
@@ -666,23 +678,68 @@
             pltpu.VMEM((2 * idx.shape[2], LANES), f32),
             pltpu.VMEM((2 * idx.shape[2], LANES), f32),
             pltpu.VMEM((out_cols, LANES), f32),
-            pltpu.VMEM((scenes, rows, LANES), f32),
+            pltpu.VMEM((rows, LANES), f32),
+            pltpu.VMEM((rows, LANES), f32),
             pltpu.VMEM((4 * channels, 4 * channels), f32),
             pltpu.VMEM((9 * channels, channels), f32),
             pltpu.VMEM(conv.shape, f32),
             pltpu.VMEM(cot.shape, bf16),
-            pltpu.VMEM(pooled.shape, bf16),
-            pltpu.VMEM((scenes, rows, LANES), bf16),
-            pltpu.VMEM((scenes, rows, LANES), f32),
-            pltpu.SemaphoreType.DMA((3, scenes)),
+            pltpu.VMEM((scenes + 1, rows, LANES), bf16),
+            pltpu.VMEM((rows, LANES), bf16),
+            pltpu.VMEM((rows, LANES), bf16),
+            pltpu.VMEM((rows, LANES), f32),
+            pltpu.VMEM((rows, LANES), f32),
+            pltpu.SemaphoreType.DMA((4, scenes)),
         ],
         name="gradients",
     )(idx, stats, sums, conv, cot, norm, pooled, phase, kernel)
 
 
+def fold(q, prod, channels):
+    shape = (prod.shape[0], LANES)
+    slot = iota(shape, 0) % PACK - 4 * q
+    upper = (iota(shape, 1) >= channels).astype(jnp.int32)
+    return jnp.where(slot == upper, prod[:, :LANES], 0.0) + jnp.where(slot == upper + 2, prod[:, LANES:], 0.0)
+
+
+def single_winners(pts, who, grad, channels):
+    size = who.shape[0]
+    who = who - (iota((size, LANES), 1) >= channels).astype(f32)
+    total = None
+    for part, x in enumerate(pts):
+        for q in range(PACK // 4):
+            n = part * PACK + q * 4
+            one = jnp.where(who == float(n), grad, 0.0)
+            two = jnp.where(who == float(n + 2), grad, 0.0)
+            prod = fold(q, dot_nn(x, jnp.concatenate([one, two], axis=1).astype(bf16)), channels)
+            total = prod if total is None else total + prod
+    return total
+
+
+def shared_winners(pts, count, table, best, grad, mult, acc, depth, channels):
+    feats = pts.shape[0]
+
+    def lifted(part, q):
+        xin = lift_inputs(pts[:, part * PACK : (part + 1) * PACK, :], count, part)
+        l = dot_nn(jnp.transpose(xin), table[:, q * 256 : (q + 1) * 256])
+        return xin, l[:, :LANES] == best[...], l[:, LANES:] == best[...]
+
+    mult[...] = jnp.zeros_like(mult)
+    for part in range(depth // PACK):
+        for q in range(PACK // 4):
+            _, one, two = lifted(part, q)
+            mult[...] += jnp.where(one, 1.0, 0.0) + jnp.where(two, 1.0, 0.0)
+    many = jnp.maximum(mult[...] + swap_halves(mult[...]), 1.0)
+    mult[...] = grad / many
+    for part in range(depth // PACK):
+        for q in range(PACK // 4):
+            xin, one, two = lifted(part, q)
+            value = jnp.concatenate([jnp.where(one, mult[...], 0.0), jnp.where(two, mult[...], 0.0)], axis=1)
+            acc[...] += fold(q, exact_right(xin[: feats * PACK], value), channels)
+
+
 def unlift_body(
-    points, counts, weight, norm, z, winner_in, slots_in, edge, far, moments, rest,
-    table, acc, bias, pts, winner, slots, best, mult, sems,
+    points, counts, weight, norm, z, winner_in, slots_in, acc, bias, table, pts, winner, slots, best, mult, sems
 ):
     feats, channels = weight.shape
     scenes, _, depth, size = points.shape
@@ -695,96 +752,62 @@
     lift_table(weight, norm, table)
     acc[...] = jnp.zeros_like(acc)
     bias[...] = jnp.zeros_like(bias)
-    second_half = (iota((1, LANES), 1) >= channels).astype(f32)
-    slot = iota((rows, LANES), 0) % PACK
-    upper = (iota((rows, LANES), 1) >= channels).astype(jnp.int32)
-
-    def fold(q, prod):
-        near_n = slot - 4 * q
-        return jnp.where(near_n == upper, prod[:, :LANES], 0.0) + jnp.where(near_n == upper + 2, prod[:, LANES:], 0.0)
-
-    def tile(u, _):
-        s = u // tiles
-        t = u % tiles
-        at = pl.ds(pl.multiple_of(t * TILE, TILE), TILE)
-
-        @pl.when(t == 0)
+
+    def scene(s, _):
+        copy_in(points, pts, sems.at[0], s).wait()
+        copy_in(winner_in, winner, sems.at[1], s).wait()
+        copy_in(slots_in, slots, sems.at[2], s).wait()
+        total = None
+        sums = None
+        for t in range(tiles):
+            at = slice(t * TILE, (t + 1) * TILE)
+            grad = slots[s, at, :].astype(f32)
+            one = jnp.sum(grad.reshape(TILE // 8, 8, LANES), axis=0)
+            sums = one if sums is None else sums + one
+            x = [pts[s, :, part * PACK : (part + 1) * PACK, at].reshape(rows, TILE) for part in range(depth // PACK)]
+            one = single_winners(x, winner[s, at, :], grad, channels)
+            total = one if total is None else total + one
+        acc[...] += total
+        bias[...] += sums
+
+        @pl.when(jnp.min(winner[s]) < 0.0)
         def _():
-            copy_in(points, pts, sems.at[0], s).wait()
-            copy_in(winner_in, winner, sems.at[1], s).wait()
-            copy_in(slots_in, slots, sems.at[2], s).wait()
-            lower = iota((EDGE, LANES), 1) < channels
-            whole = edge_rows_of(edge, s, scenes, lower) + edge_rows_of(far, s, scenes, lower)
-            slots[s, :EDGE, :] = whole.astype(bf16)
-
-        grad = slots[s, at, :].astype(f32)
-        who = winner[s, at, :]
-        bias[...] += jnp.sum(grad.reshape(TILE // 8, 8, LANES), axis=0)
-        total = None
-        for part in range(depth // PACK):
-            x = pts[s, :, part * PACK : (part + 1) * PACK, at].reshape(rows, TILE)
-            for q in range(PACK // 4):
-                n_one = second_half + float(part * PACK + q * 4)
-                value = jnp.concatenate(
-                    [jnp.where(who == n_one, grad, 0.0), jnp.where(who == n_one + 2.0, grad, 0.0)], axis=1
-                )
-                prod = fold(q, dot_nn(x, value.astype(bf16)))
-                total = prod if total is None else total + prod
-        acc[...] += total
-
-        @pl.when(jnp.min(who) < 0.0)
-        def _():
-            fetch = pltpu.make_async_copy(z.at[s, at], best, sems.at[0, 0])
-            fetch.start()
-            fetch.wait()
-            best[...] = jnp.where(winner[s, at, :] < 0.0, best[...], BIG)
-            mult[...] = jnp.zeros_like(mult)
-            count = counts[pl.ds(s, 1), at]
-
-            def lifted(part, q):
-                xin = lift_inputs(pts[s, :, part * PACK : (part + 1) * PACK, at], count, part)
-                l = dot_nn(jnp.transpose(xin), table[:, q * 256 : (q + 1) * 256])
-                return xin, l[:, :LANES] == best[...], l[:, LANES:] == best[...]
-
-            for part in range(depth // PACK):
-                for q in range(PACK // 4):
-                    _, one, two = lifted(part, q)
-                    mult[...] += jnp.where(one, 1.0, 0.0) + jnp.where(two, 1.0, 0.0)
-            many = jnp.maximum(mult[...] + swap_halves(mult[...]), 1.0)
-            mult[...] = slots[s, at, :].astype(f32) / many
-            for part in range(depth // PACK):
-                for q in range(PACK // 4):
-                    xin, one, two = lifted(part, q)
-                    value = jnp.concatenate([jnp.where(one, mult[...], 0.0), jnp.where(two, mult[...], 0.0)], axis=1)
-                    acc[...] += fold(q, exact_right(xin[:rows], value))
+            def tile(t, _):
+                at = pl.ds(pl.multiple_of(t * TILE, TILE), TILE)
+
+                @pl.when(jnp.min(winner[s, at, :]) < 0.0)
+                def _():
+                    fetch = pltpu.make_async_copy(z.at[s, at], best, sems.at[0, 0])
+                    fetch.start()
+                    fetch.wait()
+                    best[...] = jnp.where(winner[s, at, :] < 0.0, best[...], BIG)
+                    grad = slots[s, at, :].astype(f32)
+                    count = counts[pl.ds(s, 1), at]
+                    shared_winners(pts.at[s, :, :, at], count, table, best, grad, mult, acc, depth, channels)
+
+                return 0
+
+            lax.fori_loop(0, tiles, tile, 0)
 
         return 0
 
-    lax.fori_loop(0, scenes * tiles, tile, 0)
-    out = exact_right(one_hot_cols(16, rows), acc[...])
-    out = out + swap_halves(out)
-    pieces = [out[i : i + 1, :channels] for i in range(feats)]
-    pieces.append(jnp.sum(bias[...], axis=0, keepdims=True)[:, :channels])
-    pieces += [moments[i : i + 1, :16] for i in range(feats + 1)]
-    width = (feats + 1) * (channels + 16)
-    pieces.append(jnp.zeros((1, rest.shape[1] - width), f32))
-    rest[...] = jnp.concatenate(pieces, axis=1)
-
-
-def unlift(points, counts, weight, norm, z, winner, slots, edge, far, moments):
+    lax.fori_loop(0, scenes, scene, 0)
+
+
+def unlift(points, counts, weight, norm, z, winner, slots):
     scenes, feats, depth, size = points.shape
     channels = weight.shape[1]
     full = (feats + 2) * PACK
-    width = -(-(feats + 1) * (channels + 16) // LANES) * LANES
     return pl.pallas_call(
         unlift_body,
-        in_specs=hbm(1) + vmem(3) + hbm(3) + vmem(3),
-        out_specs=pl.BlockSpec(memory_space=pltpu.VMEM),
-        out_shape=jax.ShapeDtypeStruct((1, width), f32),
+        in_specs=hbm(1) + vmem(3) + hbm(3),
+        out_specs=vmem(2),
+        out_shape=[
+            jax.ShapeDtypeStruct((feats * PACK, LANES), f32),
+            jax.ShapeDtypeStruct((8, LANES), f32),
+        ],
         scratch_shapes=[
             pltpu.VMEM((full, PACK * channels), bf16),
-            pltpu.VMEM((feats * PACK, LANES), f32),
-            pltpu.VMEM((8, LANES), f32),
             pltpu.VMEM(points.shape, bf16),
             pltpu.VMEM((scenes, size, LANES), f32),
             pltpu.VMEM(slots.shape, bf16),
@@ -792,8 +815,92 @@
             pltpu.VMEM((TILE, LANES), f32),
             pltpu.SemaphoreType.DMA((3, scenes)),
         ],
+        cost_estimate=pl.CostEstimate(flops=40_000_000_000, bytes_accessed=16_000_000, transcendentals=0),
         name="unlift",
-    )(points, counts, weight, norm, z, winner, slots, edge, far, moments)
+    )(points, counts, weight, norm, z, winner, slots)
+
+
+def edges_body(
+    devices, parts, pts, counts, weight, norm, z, winner, edge, far, moments, inner, inner_bias, kgrad, payload,
+    table, acc, bias, best, mult, sem,
+):
+    feats, channels = weight.shape
+    scenes, _, depth, _ = pts.shape
+    rows = feats * PACK
+    size = pts.shape[3]
+    lift_table(weight, norm, table)
+    acc[...] = inner[...]
+    bias[...] = inner_bias[...]
+    peers = payload.shape[0]
+    share = kgrad.shape[1]
+    for r in range(devices):
+        row = kgrad[r : r + 1, :]
+        for q in range(1, parts):
+            row = row + kgrad[q * devices + r : q * devices + r + 1, :]
+        each = peers // devices
+        payload[r * each : (r + 1) * each, :, :share] = jnp.broadcast_to(row[:, None, :], (each, 1, share))
+
+    def scene(s, _):
+        lower = iota((EDGE, LANES), 1) < channels
+        whole = edge_rows_of(edge, s, scenes, lower) + edge_rows_of(far, s, scenes, lower)
+        whole = whole.astype(bf16).astype(f32)
+        grad = jnp.concatenate([whole, jnp.zeros((size - EDGE, LANES), f32)], axis=0)
+        bias[...] += jnp.sum(whole.reshape(EDGE // 8, 8, LANES), axis=0)
+        x = [pts[s, :, part * PACK : (part + 1) * PACK, :].reshape(rows, size) for part in range(depth // PACK)]
+        acc[...] += single_winners(x, winner[s], grad, channels)
+
+        @pl.when(jnp.min(winner[s, :EDGE, :]) < 0.0)
+        def _():
+            fetch = pltpu.make_async_copy(z.at[s, :size], best, sem)
+            fetch.start()
+            fetch.wait()
+            best[...] = jnp.where(winner[s] < 0.0, best[...], BIG)
+            count = counts[pl.ds(s, 1), :][:, :size]
+            shared_winners(pts.at[s], count, table, best, grad, mult, acc, depth, channels)
+
+        return 0
+
+    lax.fori_loop(0, scenes, scene, 0)
+    out = exact_right(one_hot_cols(16, rows), acc[...])
+    out = out + swap_halves(out)
+    pieces = [out[i : i + 1, :channels] for i in range(feats)]
+    pieces.append(jnp.sum(bias[...], axis=0, keepdims=True)[:, :channels])
+    pieces += [moments[i : i + 1, :16] for i in range(feats + 1)]
+    width = (feats + 1) * (channels + 16)
+    pieces.append(jnp.zeros((1, payload.shape[2] - share - width), f32))
+    row = jnp.concatenate(pieces, axis=1)
+    payload[:, :, share:] = jnp.broadcast_to(row[:, None, :], (peers, 1, row.shape[1]))
+
+
+def unlift_edges(devices, parts, peers, points, counts, weight, norm, z, winner, edge, far, moments, inner, bias, kgrad):
+    scenes, feats, depth, _ = points.shape
+    channels = weight.shape[1]
+    full = (feats + 2) * PACK
+    width = -(-(feats + 1) * (channels + 16) // LANES) * LANES
+    return pl.pallas_call(
+        functools.partial(edges_body, devices, parts),
+        grid=(1,),
+        in_specs=[
+            pl.BlockSpec((scenes, feats, depth, LANES), lambda i: (0, 0, 0, 0)),
+            pl.BlockSpec(counts.shape, lambda i: (0, 0)),
+            pl.BlockSpec(weight.shape, lambda i: (0, 0)),
+            pl.BlockSpec(norm.shape, lambda i: (0, 0)),
+            pl.BlockSpec(memory_space=pltpu.HBM),
+            pl.BlockSpec((scenes, LANES, LANES), lambda i: (0, 0, 0)),
+        ]
+        + [pl.BlockSpec(x.shape, lambda i: (0, 0)) for x in (edge, far, moments, inner, bias, kgrad)],
+        out_specs=pl.BlockSpec((peers, 1, kgrad.shape[1] + width), lambda i: (0, 0, 0)),
+        out_shape=jax.ShapeDtypeStruct((peers, 1, kgrad.shape[1] + width), f32),
+        scratch_shapes=[
+            pltpu.VMEM((full, PACK * channels), bf16),
+            pltpu.VMEM((feats * PACK, LANES), f32),
+            pltpu.VMEM((8, LANES), f32),
+            pltpu.VMEM((LANES, LANES), f32),
+            pltpu.VMEM((LANES, LANES), f32),
+            pltpu.SemaphoreType.DMA,
+        ],
+        name="edges",
+    )(points, counts, weight, norm, z, winner, edge, far, moments, inner, bias, kgrad)
 
 
 def adam(fixes, w, states, grad, rate):
@@ -952,19 +1059,17 @@
     slots, own_edge, far, kgrad = gradients(
         cells, devices, parts, take_at, conv_stats, grad_sums, conv, cotangent, norm_weight, pooled, phase, kernel
     )
-    far, kgrad = lax.optimization_barrier((shifted(far, -1), kgrad))
+    far = shifted(far, -1)
     if parts > 1:
         kgrad = lax.all_to_all(kgrad, "scene", 0, 0, tiled=True)
     else:
         kgrad = lax.psum(kgrad, "scene")
-    rest = unlift(
-        points, pillar_counts, point_weight, norm_weight, z, winner, slots, own_edge, far, moments
+    inner, bias = unlift(points, pillar_counts, point_weight, norm_weight, z, winner, slots)
+    far, kgrad, inner, bias = lax.optimization_barrier((far, kgrad, inner, bias))
+    payload = unlift_edges(
+        devices, parts, peers, points, pillar_counts, point_weight, norm_weight, z, winner, own_edge, far, moments, inner, bias, kgrad
     )
-    if parts > 1:
-        kgrad = jnp.sum(kgrad.reshape(scene_devices, devices, share), axis=0)
-    kgrad = jnp.broadcast_to(kgrad[:, None], (devices, scene_devices, share)).reshape(peers, share)
-    got = exchange(jnp.concatenate([kgrad, jnp.broadcast_to(rest, (peers, rest.shape[1]))], axis=1)[:, None])
-    got = got
+    got = exchange(payload)
     steps_done = step_count[0].astype(f32)
     fix = jnp.stack([1.0 - beta_one**steps_done, 1.0 - beta_two**steps_done])
     outs = update(

time: 146 us -> 138 us (0.945)
  waiting for transfers between devices: 35.2 us -> 29.9 us
  Pallas kernels: 76.8 us -> 73.6 us
    ppermute x2, waiting for transfers between devices: 5.42 us -> 0.01 us  [shifted(): return lax.ppermute(x, 'rows', pairs)]
    pallas_call x1, Pallas kernels: 19.8 us -> 16.1 us  [convolve(): pl.pallas_call(functools.partial(conv_body, devices, parts), in_specs=sme...]
    pallas_call x1 -> x2, Pallas kernels: 11.8 us -> 13.9 us  [the longest x1 8.84 us: unlift(): pl.pallas_call(unlift_body, in_specs=hbm(1) + vmem(3) + hbm(3), out_specs...]
    unnamed x16 -> x18, local copies, waits for them, and re-layouts: 2.58 us -> 3.26 us
  transfers between devices with their start and end apart: 7 -> 7, of which waited for: 5 -> 4; matrix products, arithmetic and copies ran while one was open for 2% -> 2% of each run, Pallas kernels for 8% -> 7%
where the time goes in v5:
time: 138 us; the launch traced here: 135 us
  Pallas kernels  73.6 us (53%)
  waiting for transfers between devices  29.9 us (22%)
  starting transfers between devices  24 us (17%)
  local copies, waits for them, and re-layouts  5.34 us (4%)
  between operations  1.75 us (1%)
    all_to_all x4, waiting for transfers between devices, exchange(): return lax.all_to_all(x, ('rows', 'scene'), 0, 0, tiled=True)  29.9 us
    pallas_call x1, Pallas kernels, gradients(): pl.pallas_call(functools.partial(grad_body, cells, devices, parts), in_sp...  18.6 us
    pallas_call x1, Pallas kernels, lift(): pl.pallas_call(lift_body, in_specs=smem(1) + hbm(1) + vmem(5), out_specs=...  17.3 us
    pallas_call x1, Pallas kernels, convolve(): pl.pallas_call(functools.partial(conv_body, devices, parts), in_specs=sme...  16.1 us
    all_to_all x4, starting transfers between devices, exchange(): return lax.all_to_all(x, ('rows', 'scene'), 0, 0, tiled=True)  14.3 us
    pallas_call x1, Pallas kernels, unlift(): pl.pallas_call(unlift_body, in_specs=hbm(1) + vmem(3) + hbm(3), out_specs...  8.84 us
    ppermute x2, starting transfers between devices, shifted(): return lax.ppermute(x, 'rows', pairs)  6.15 us
    pallas_call x1, Pallas kernels, normalize(): pl.pallas_call(functools.partial(norm_body, cells), in_specs=vmem(1) + hb...  5.61 us
  transfers between devices with their start and end apart: 7, of which 4 were waited for; matrix products, arithmetic and copies ran while one was open for 2% of the time, Pallas kernels for 7%

profile of v5, /device:TPU:0, one launch (start us, length us, event | category | flops | bytes accessed | tf_op | source)
XLA Modules:
  0.0 135.3 jit_solution(17987415572397295763)
XLA Ops:
  0.7 17.3 %lift.1 = (f32[8,768,128]{2,1,0:T(8,128)}, f32[8,768,128]{2,1,0:T(8,128)}, f32[208,128]{1,0:T(8,128)}, f32[32,1,1408]{2,1,0:T(1,128)}, f32[16,128]{1,0:T(8,128)}) custom-call(s32[1,1]{1,0:T(1,128)} %bitcast.mine, bf16[8,9,32,768]{3,2,1,0:T(8,128)(2,1)} %pts.1, s32[8,768]{1,0:T(8,128)} %counts.5, s32[8,768]{1,0:T(8,128)} %pixels.1, bf16[9,64]{1,0:T(8,128)(2,1)} %weight.7, ...), custom_call_target="tpu_custom_call" | custom-call | tf_op jit(solution)/shard_map/lift/pallas_call | solution.py:213
  17.9 4.9 %collective-permute-start = (f32[208,128]{1,0:T(8,128)}, f32[208,128]{1,0:T(8,128)S(1)}, u32[]{:S(2)}, u32[]{:S(2)}) collective-permute-start(f32[208,128]{1,0:T(8,128)} %get-tuple-element.46), channel_id=1, source_target_pairs={{0,4},{4,8},{8,12},{12,16},{16,20},{20,24},{24,28},{1,5},{5,9},{9,... | collective-permute-start | bytes 319496 | tf_op jit(solution)/shard_map/ppermute | solution.py:998
  22.8 4.9 %all-to-all-start = ((f32[32,1,1408]{2,1,0:T(1,128)}), f32[32,1,1408]{2,1,0:T(1,128)S(1)}, u32[]{:S(2)}, u32[]{:S(2)}) async-start(f32[32,1,1408]{2,1,0:T(1,128)} %get-tuple-element.47), calls=%async_computation | async-start | bytes 360448 | tf_op jit(solution)/shard_map/all_to_all | solution.py:1002
  27.8 0.7 reshape.48.pix
  28.6 7.9 %all-to-all-done.got = f32[32,1,1408]{2,1,0:T(1,128)S(1)} async-done(((f32[32,1,1408]{2,1,0:T(1,128)}), f32[32,1,1408]{2,1,0:T(1,128)S(1)}, u32[]{:S(2)}, u32[]{:S(2)}) %all-to-all-start) | async-done | bytes 180256 | tf_op jit(solution)/shard_map/all_to_all | solution.py:1002
  36.5 0.7 copy-done.1
  37.1 16.1 %convolve.1 = (f32[8,4,256,128]{3,2,1,0:T(8,128)}, bf16[8,896,128]{2,1,0:T(8,128)(2,1)}, f32[32,128]{1,0:T(8,128)}, bf16[576,64]{1,0:T(8,128)(2,1)}) custom-call(s32[32,1,192]{2,1,0:T(1,128)} %reshape.48.pix, s32[8,128]{1,0:T(8,128)} %copy-done.8, f32[32,1,1408]{2,1,0:T(1,128)} %copy-done.1, f32[8,768,128]{2,1,0:T(8,128)} %get-tuple-element.48.z_in.z, ...), custom_call_target="tpu_custom_call" | custom-call | tf_op jit(solution)/shard_map/convolve/pallas_call | solution.py:405
  53.2 2.6 %all-to-all-start.1 = ((f32[32,1,128]{2,1,0:T(1,128)}), f32[32,1,128]{2,1,0:T(1,128)S(1)}, u32[]{:S(2)}, u32[]{:S(2)}) async-start(f32[32,1,128]{2,1,0:T(1,128)} %bitcast.21), calls=%async_computation.1 | async-start | bytes 32768 | tf_op jit(solution)/shard_map/all_to_all | solution.py:1002
  55.8 7.1 %all-to-all-done.1.stats = f32[32,1,128]{2,1,0:T(1,128)S(1)} async-done(((f32[32,1,128]{2,1,0:T(1,128)}), f32[32,1,128]{2,1,0:T(1,128)S(1)}, u32[]{:S(2)}, u32[]{:S(2)}) %all-to-all-start.1) | async-done | bytes 16416 | tf_op jit(solution)/shard_map/all_to_all | solution.py:1002
  62.9 0.6 copy-done.4
  63.5 5.6 %normalize.1 = (bf16[8,8,64,256]{3,2,1,0:T(8,128)(2,1)}, f32[32,128]{1,0:T(8,128)}) custom-call(f32[32,1,128]{2,1,0:T(1,128)} %copy-done.4, f32[8,4,256,128]{3,2,1,0:T(8,128)} %get-tuple-element.50.conv_in, bf16[8,8,64,256]{3,2,1,0:T(8,128)(2,1)} %cot_in.3, bf16[4,64]{1,0:T(4,128)(2,1)} %norm.13), custom_call_target="tpu_custom_call" | custom-call | tf_op jit(solution)/shard_map/normalize/pallas_call | solution.py:489
  69.1 2.6 %all-to-all-start.2 = ((f32[32,1,128]{2,1,0:T(1,128)}), f32[32,1,128]{2,1,0:T(1,128)S(1)}, u32[]{:S(2)}, u32[]{:S(2)}) async-start(f32[32,1,128]{2,1,0:T(1,128)} %bitcast.20), calls=%async_computation.2 | async-start | bytes 32768 | tf_op jit(solution)/shard_map/all_to_all | solution.py:1002
  71.7 0.7 reshape.51.idx
  72.4 0.6 broadcast_in_dim.11.phase
  73.1 5.7 %all-to-all-done.2.sums = f32[32,1,128]{2,1,0:T(1,128)S(1)} async-done(((f32[32,1,128]{2,1,0:T(1,128)}), f32[32,1,128]{2,1,0:T(1,128)S(1)}, u32[]{:S(2)}, u32[]{:S(2)}) %all-to-all-start.2) | async-done | bytes 16416 | tf_op jit(solution)/shard_map/all_to_all | solution.py:1002
  79.3 18.6 %gradients.1 = (bf16[8,896,128]{2,1,0:T(8,128)(2,1)}, f32[192,128]{1,0:T(8,128)}, f32[192,128]{1,0:T(8,128)}, f32[32,1152]{1,0:T(8,128)}) custom-call(s32[32,1,208]{2,1,0:T(1,128)} %reshape.51.idx, f32[32,1,128]{2,1,0:T(1,128)} %copy-done.4, f32[32,1,128]{2,1,0:T(1,128)} %copy-done.5, f32[8,4,256,128]{3,2,1,0:T(8,128)} %get-tuple-element.50.conv_in, ...), custom_call_target="tpu_custom_call" | custom-call | tf_op jit(solution)/shard_map/gradients/pallas_call | solution.py:664
  98.0 1.3 collective-permute-start.1
  99.3 3.5 %all-to-all-start.3 = ((f32[4,8,1152]{2,1,0:T(8,128)}), f32[4,8,1152]{2,1,0:T(8,128)S(1)}, u32[]{:S(2)}, u32[]{:S(2)}) async-start(f32[4,8,1152]{2,1,0:T(8,128)} %bitcast.15), calls=%async_computation.3 | async-start | bytes 294912 | tf_op jit(solution)/shard_map/all_to_all | solution.py:1064
  102.8 8.8 %unlift.1 = (f32[72,128]{1,0:T(8,128)}, f32[8,128]{1,0:T(8,128)}) custom-call(bf16[8,9,32,768]{3,2,1,0:T(8,128)(2,1)} %pts.1, s32[8,768]{1,0:T(8,128)} %counts.5, bf16[9,64]{1,0:T(8,128)(2,1)} %weight.7, bf16[4,64]{1,0:T(4,128)(2,1)} %norm.13, f32[8,768,128]{2,1,0:T(8,128)} %get-tuple-element.48.z_in.z, f32[8,768,128]{2,1,0:T(8,128)} %get-tuple-element.52.winner_in.winner, ...), custom_call_target="tpu_custom_call" | custom-call | flops 40000000000 | bytes 16000000 | tf_op jit(solution)/shard_map/unlift/pallas_call | solution.py:801
  112.3 5.1 %edges.1 = f32[32,1,2048]{2,1,0:T(1,128)} custom-call(bf16[8,9,32,768]{3,2,1,0:T(8,128)(2,1)} %pts.1, s32[8,768]{1,0:T(8,128)} %counts.5, bf16[9,64]{1,0:T(8,128)(2,1)} %weight.7, bf16[4,64]{1,0:T(4,128)(2,1)} %norm.13, f32[8,768,128]{2,1,0:T(8,128)} %get-tuple-element.48.z_in.z, f32[8,768,128]{2,1,0:T(8,128)} %get-tuple-element.52.winner_in.winner, ...), custom_call_target="tpu_custom_call" | custom-call | tf_op jit(solution)/shard_map/edges/pallas_call | solution.py:880
  117.5 4.3 %all-to-all-start.4 = ((f32[32,1,2048]{2,1,0:T(1,128)}), f32[32,1,2048]{2,1,0:T(1,128)S(1)}, u32[]{:S(2)}, u32[]{:S(2)}) async-start(f32[32,1,2048]{2,1,0:T(1,128)} %edges.1), calls=%async_computation.4 | async-start | bytes 524288 | tf_op jit(solution)/shard_map/all_to_all | solution.py:1002
  123.1 9.3 %all-to-all-done.4.got = f32[32,1,2048]{2,1,0:T(1,128)S(1)} async-done(((f32[32,1,2048]{2,1,0:T(1,128)}), f32[32,1,2048]{2,1,0:T(1,128)S(1)}, u32[]{:S(2)}, u32[]{:S(2)}) %all-to-all-start.4) | async-done | bytes 262176 | tf_op jit(solution)/shard_map/all_to_all | solution.py:1002
  132.4 0.7 copy-done
  133.1 2.1 %update.1 = (f32[9,64]{1,0:T(8,128)}, f32[9,2,64]{2,1,0:T(2,128)}, f32[9,64]{1,0:T(8,128)}, bf16[9,64]{1,0:T(8,128)(2,1)}, f32[4,64]{1,0:T(4,128)}, /*index=5*/f...) custom-call(f32[2]{0:T(128)} %pad_maximum_fusion.fix, ...), custom_call_target="tpu_custom_call" | custom-call | tf_op jit(solution)/shard_map/update/pallas_call | solution.py:985
  (27 shorter events, 2.0 us)
Async XLA Ops:
  0.6 27.1 %copy-start.3 = (s32[8,768]{1,0:T(8,128)S(1)}, s32[8,768]{1,0:T(8,128)}, u32[]{:S(2)}) copy-start(s32[8,768]{1,0:T(8,128)} %pixels.1) | copy-start | bytes 73732
  17.9 10.6 %collective-permute-start = (f32[208,128]{1,0:T(8,128)}, f32[208,128]{1,0:T(8,128)S(1)}, u32[]{:S(2)}, u32[]{:S(2)}) collective-permute-start(f32[208,128]{1,0:T(8,128)} %get-tuple-element.46), channel_id=1, source_target_pairs={{0,4},{4,8},{8,12},{12,16},{16,20},{20,24},{24,28},{1,5},{5,9},{9,... | collective-permute-start | bytes 319496 | tf_op jit(solution)/shard_map/ppermute | solution.py:998
  22.8 13.7 %all-to-all-start = ((f32[32,1,1408]{2,1,0:T(1,128)}), f32[32,1,1408]{2,1,0:T(1,128)S(1)}, u32[]{:S(2)}, u32[]{:S(2)}) async-start(f32[32,1,1408]{2,1,0:T(1,128)} %get-tuple-element.47), calls=%async_computation | async-start | bytes 360448 | tf_op jit(solution)/shard_map/all_to_all | solution.py:1002
  28.5 7.9 %copy-start.6 = (f32[208,128]{1,0:T(8,128)}, f32[208,128]{1,0:T(8,128)S(1)}, u32[]{:S(2)}) copy-start(f32[208,128]{1,0:T(8,128)S(1)} %collective-permute-done.edge) | copy-start | bytes 319492
  28.5 7.9 %copy-start.8 = (s32[8,128]{1,0:T(8,128)}, s32[8,128]{1,0:T(8,128)S(1)}, u32[]{:S(2)}) copy-start(s32[8,128]{1,0:T(8,128)S(1)} %slice_convert_fusion.far_pix) | copy-start | bytes 12292
  36.5 0.7 copy-start.1
  53.2 9.6 %all-to-all-start.1 = ((f32[32,1,128]{2,1,0:T(1,128)}), f32[32,1,128]{2,1,0:T(1,128)S(1)}, u32[]{:S(2)}, u32[]{:S(2)}) async-start(f32[32,1,128]{2,1,0:T(1,128)} %bitcast.21), calls=%async_computation.1 | async-start | bytes 32768 | tf_op jit(solution)/shard_map/all_to_all | solution.py:1002
  62.9 0.6 copy-start.4
  69.1 9.6 %all-to-all-start.2 = ((f32[32,1,128]{2,1,0:T(1,128)}), f32[32,1,128]{2,1,0:T(1,128)S(1)}, u32[]{:S(2)}, u32[]{:S(2)}) async-start(f32[32,1,128]{2,1,0:T(1,128)} %bitcast.20), calls=%async_computation.2 | async-start | bytes 32768 | tf_op jit(solution)/shard_map/all_to_all | solution.py:1002
  78.7 0.6 copy-start.5
  98.0 13.7 %collective-permute-start.1 = (f32[192,128]{1,0:T(8,128)}, f32[192,128]{1,0:T(8,128)S(1)}, u32[]{:S(2)}, u32[]{:S(2)}) collective-permute-start(f32[192,128]{1,0:T(8,128)} %get-tuple-element.57), channel_id=1, source_target_pairs={{4,0},{8,4},{12,8},{16,12},{20,16},{24,20},{28,24},{5,1},{9,5},{13... | collective-permute-start | bytes 294920 | tf_op jit(solution)/shard_map/ppermute | solution.py:998
  99.3 12.4 %all-to-all-start.3 = ((f32[4,8,1152]{2,1,0:T(8,128)}), f32[4,8,1152]{2,1,0:T(8,128)S(1)}, u32[]{:S(2)}, u32[]{:S(2)}) async-start(f32[4,8,1152]{2,1,0:T(8,128)} %bitcast.15), calls=%async_computation.3 | async-start | bytes 294912 | tf_op jit(solution)/shard_map/all_to_all | solution.py:1064
  111.7 0.6 copy-start.7
  111.7 0.7 copy-start.2
  117.5 14.9 %all-to-all-start.4 = ((f32[32,1,2048]{2,1,0:T(1,128)}), f32[32,1,2048]{2,1,0:T(1,128)S(1)}, u32[]{:S(2)}, u32[]{:S(2)}) async-start(f32[32,1,2048]{2,1,0:T(1,128)} %edges.1), calls=%async_computation.4 | async-start | bytes 524288 | tf_op jit(solution)/shard_map/all_to_all | solution.py:1002
  132.4 0.7 copy-start

commit v6 on v5

--- a/solution.py
+++ b/solution.py
@@ -20,6 +20,7 @@
 EDGE = 48
 BIG = 1e30
 PACK = 8
+ROWS = 128
 TILE = 256
 LANES = 128
 f32 = jnp.float32
@@ -94,8 +95,11 @@
 def lift_inputs(pts, count, part):
     feats, _, size = pts.shape
     live = (iota((PACK, size), 0) + part * PACK < count).astype(f32)
-    kept = (pts.astype(f32) * live[None]).reshape(feats * PACK, size)
-    return jnp.concatenate([kept, live, (live - 1.0) * BIG], axis=0).astype(bf16)
+    low = live.astype(bf16)
+    dead = ((live - 1.0) * BIG).astype(bf16)
+    full = jnp.concatenate([pts.reshape(feats * PACK, size), low, dead], axis=0)
+    kept = jnp.concatenate([(pts * low[None]).reshape(feats * PACK, size), low], axis=0)
+    return full, kept
 
 
 def copy_in(source, target, sems, s):
@@ -111,7 +115,7 @@
 
 def lift_body(
     mine, points, counts, pixels, weight, norm, kernel, z_out, winner_out, edge, payload, moments,
-    table, gram, wide, pts, z, low, high, winner, sems,
+    table, gram, wide, pts, z, winner, sems,
 ):
     feats, channels = weight.shape
     scenes, _, depth, size = points.shape
@@ -126,38 +130,41 @@
         copy_in(points, pts, sems.at[0], s).wait()
         count = counts[pl.ds(s, 1), :]
         total = None
+        inputs = []
         for part in range(depth // PACK):
-            xin = lift_inputs(pts[s, :, part * PACK : (part + 1) * PACK, :], count, part)
-            prod = dot_nt(xin[:rows], xin[:rows])
+            xin, kept = lift_inputs(pts[s, :, part * PACK : (part + 1) * PACK, :], count, part)
+            prod = dot_nt(kept, xin[:rows])
             total = prod if total is None else total + prod
-            for t in range(size // TILE):
-                at = slice(t * TILE, (t + 1) * TILE)
-                turned = jnp.transpose(xin[:, at])
-                for q in range(PACK // 4):
-                    l = dot_nn(turned, table[:, q * 256 : (q + 1) * 256])
-                    one, two = l[:, :LANES], l[:, LANES:]
-                    n_one, n_two = float(part * PACK + q * 4), float(part * PACK + q * 4 + 2)
-                    m = jnp.maximum(one, two)
-                    first = jnp.where(two > one, n_two, n_one)
-                    last = jnp.where(two >= one, n_two, n_one)
-                    if part > 0 or q > 0:
-                        old = z[s, at, :]
-                        first = jnp.where(m > old, first, low[at, :])
-                        last = jnp.where(m >= old, last, high[at, :])
-                        m = jnp.maximum(old, m)
-                    if part == depth // PACK - 1 and q == PACK // 4 - 1:
-                        upper = (iota((TILE, LANES), 1) >= channels).astype(f32)
-                        first, last = first + upper, last + upper
-                        other = swap_halves(m)
-                        first = jnp.where(other > m, swap_halves(first), first)
-                        last = jnp.where(other >= m, swap_halves(last), last)
-                        m = jnp.maximum(m, other)
-                        only = jnp.where(first == last, first, -1.0)
-                        winner[s, at, :] = jnp.where(m > -0.5 * BIG, only, 99.0)
-                    else:
-                        low[at, :] = first
-                        high[at, :] = last
-                    z[s, at, :] = m
+            inputs.append(xin)
+        for t in range(size // LANES):
+            turned = [jnp.transpose(x[:, t * LANES : (t + 1) * LANES]) for x in inputs]
+            for h in range(LANES // ROWS):
+                best = None
+                for part in range(depth // PACK):
+                    lhs = turned[part][h * ROWS : (h + 1) * ROWS]
+                    for q in range(PACK // 4):
+                        l = dot_nn(lhs, table[:, q * 256 : (q + 1) * 256])
+                        one, two = l[:, :LANES], l[:, LANES:]
+                        n_one, n_two = float(part * PACK + q * 4), float(part * PACK + q * 4 + 2)
+                        m = jnp.maximum(one, two)
+                        low = jnp.where(two > one, n_two, n_one)
+                        high = jnp.where(two >= one, n_two, n_one)
+                        if best is None:
+                            best, first, last = m, low, high
+                        else:
+                            first = jnp.where(m > best, low, first)
+                            last = jnp.where(m >= best, high, last)
+                            best = jnp.maximum(best, m)
+                at = slice(t * LANES + h * ROWS, t * LANES + (h + 1) * ROWS)
+                upper = (iota((ROWS, LANES), 1) >= channels).astype(f32)
+                first, last = first + upper, last + upper
+                other = swap_halves(best)
+                first = jnp.where(other > best, swap_halves(first), first)
+                last = jnp.where(other >= best, swap_halves(last), last)
+                best = jnp.maximum(best, other)
+                only = jnp.where(first == last, first, -1.0)
+                winner[s, at, :] = jnp.where(best > -0.5 * BIG, only, 99.0).astype(bf16)
+                z[s, at, :] = best
         gram[...] += total
         copy_in(z, z_out, sems.at[1], s).start()
         copy_in(winner, winner_out, sems.at[2], s).start()
@@ -216,7 +223,7 @@
         out_specs=hbm(2) + vmem(3),
         out_shape=[
             jax.ShapeDtypeStruct((scenes, size, LANES), f32),
-            jax.ShapeDtypeStruct((scenes, size, LANES), f32),
+            jax.ShapeDtypeStruct((scenes, size, LANES), bf16),
             jax.ShapeDtypeStruct((edge_rows, LANES), f32),
             jax.ShapeDtypeStruct((peers, 1, 256 + share), f32),
             jax.ShapeDtypeStruct((16, LANES), f32),
@@ -227,9 +234,7 @@
             pltpu.VMEM((LANES, LANES), f32),
             pltpu.VMEM(points.shape, bf16),
             pltpu.VMEM((scenes, size, LANES), f32),
-            pltpu.VMEM((size, LANES), f32),
-            pltpu.VMEM((size, LANES), f32),
-            pltpu.VMEM((scenes, size, LANES), f32),
+            pltpu.VMEM((scenes, size, LANES), bf16),
             pltpu.SemaphoreType.DMA((3, scenes)),
         ],
         name="lift",
@@ -258,7 +263,8 @@
 
 
 def edge_rows_of(block, s, scenes, lower):
-    spot = pl.ds(pl.multiple_of((s % (scenes // 2)) * EDGE, 8), EDGE)
+    base = (s % (scenes // 2)) * EDGE
+    spot = pl.ds(base if isinstance(base, int) else pl.multiple_of(base, 8), EDGE)
     rows = jnp.where(lower == (s < scenes // 2), block[spot, :], 0.0)
     return rows + swap_halves(rows)
 
@@ -507,7 +513,7 @@
 
 def grad_body(
     cells, devices, parts, idx, stats, sums, conv_in, cot_in, norm, pooled_in, phase, kernel, slots_out, edge, far, kgrad,
-    taps, field_a, field_b, taken_a, taken_b, turn, column_a, column_b, acc, rows_k, conv, cot, pooled, slots_a, slots_b, exact_a, exact_b, sems,
+    taps, field_a, field_b, taken_a, taken_b, turn, column_a, column_b, acc, rows_k, conv, cot, pooled, slots_a, slots_b, exact_a, exact_b, staged, sems,
 ):
     scenes, pairs, out_cols, _ = conv.shape
     channels = norm.shape[1]
@@ -582,14 +588,15 @@
         split = jnp.concatenate([jnp.where(is_even, pf, 0.0), jnp.where(is_odd, pf, 0.0)], axis=1)
         acc[...] += dot_tn(split.astype(bf16), part)
 
-    def copy_out(k, s):
-        return pltpu.make_async_copy(slots[k], slots_out.at[s], sems.at[3, k])
+    def copy_out(s):
+        return copy_in(staged, slots_out, sems.at[3], s)
 
     def done(k, s):
         half_store(edge, s, scenes, exact[k][:EDGE, :])
         half_store(far, s, scenes, exact[k][size - LANES : size - LANES + EDGE, :])
-        slots[k][:EDGE, :] = jnp.zeros((EDGE, LANES), bf16)
-        copy_out(k, s).start()
+        staged[s, :EDGE, :] = jnp.zeros((EDGE, LANES), bf16)
+        staged[s, EDGE:, :] = slots[k][EDGE:, :]
+        copy_out(s).start()
 
     def walk(dst, src, k, s):
         before = jnp.clip(s - 1, 0, scenes - 1)
@@ -604,10 +611,6 @@
         def _():
             copy_in(pooled_in, pooled, sems.at[2], before).wait()
 
-
-        @pl.when(s >= 3)
-        def _():
-            copy_out(1 - k, s - 3).wait()
 
         for j in range(pairs):
             to, of = ((taken_a, taken_b), (taken_b, taken_a))[j % 2]
@@ -653,8 +656,8 @@
         for j in range(share):
             lanes = slice(j * channels, (j + 1) * channels)
             kgrad[q * devices : (q + 1) * devices, lanes] = rows_k[pl.ds(q * share + j, devices, stride=own), :]
-    copy_out(0, scenes - 2).wait()
-    copy_out(1, scenes - 1).wait()
+    for s in range(scenes):
+        copy_out(s).wait()
 
 
 def gradients(cells, devices, parts, idx, stats, sums, conv, cot, norm, pooled, phase, kernel):
@@ -689,6 +692,7 @@
             pltpu.VMEM((rows, LANES), bf16),
             pltpu.VMEM((rows, LANES), f32),
             pltpu.VMEM((rows, LANES), f32),
+            pltpu.VMEM((scenes, rows, LANES), bf16),
             pltpu.SemaphoreType.DMA((4, scenes)),
         ],
         name="gradients",
@@ -704,7 +708,7 @@
 
 def single_winners(pts, who, grad, channels):
     size = who.shape[0]
-    who = who - (iota((size, LANES), 1) >= channels).astype(f32)
+    who = who.astype(f32) - (iota((size, LANES), 1) >= channels).astype(f32)
     total = None
     for part, x in enumerate(pts):
         for q in range(PACK // 4):
@@ -720,7 +724,7 @@
     feats = pts.shape[0]
 
     def lifted(part, q):
-        xin = lift_inputs(pts[:, part * PACK : (part + 1) * PACK, :], count, part)
+        xin, _ = lift_inputs(pts[:, part * PACK : (part + 1) * PACK, :], count, part)
         l = dot_nn(jnp.transpose(xin), table[:, q * 256 : (q + 1) * 256])
         return xin, l[:, :LANES] == best[...], l[:, LANES:] == best[...]
 
@@ -739,7 +743,8 @@
 
 
 def unlift_body(
-    points, counts, weight, norm, z, winner_in, slots_in, acc, bias, table, pts, winner, slots, best, mult, sems
+    points, counts_in, weight_in, norm_in, z, winner_in, slots_in, acc, bias,
+    table, pts, winner, slots, best, mult, counts, weight, norm, sems,
 ):
     feats, channels = weight.shape
     scenes, _, depth, size = points.shape
@@ -749,7 +754,6 @@
         copy_in(points, pts, sems.at[0], s).start()
         copy_in(winner_in, winner, sems.at[1], s).start()
         copy_in(slots_in, slots, sems.at[2], s).start()
-    lift_table(weight, norm, table)
     acc[...] = jnp.zeros_like(acc)
     bias[...] = jnp.zeros_like(bias)
 
@@ -770,24 +774,31 @@
         acc[...] += total
         bias[...] += sums
 
-        @pl.when(jnp.min(winner[s]) < 0.0)
+        @pl.when(jnp.min(winner[s].astype(f32)) < 0.0)
         def _():
+            for i, (of, to) in enumerate(((counts_in, counts), (weight_in, weight), (norm_in, norm))):
+                fetch = pltpu.make_async_copy(of, to, sems.at[3, i])
+                fetch.start()
+                fetch.wait()
+            lift_table(weight, norm, table)
+
             def tile(t, _):
-                at = pl.ds(pl.multiple_of(t * TILE, TILE), TILE)
-
-                @pl.when(jnp.min(winner[s, at, :]) < 0.0)
+                at = pl.ds(pl.multiple_of(t * LANES, LANES), LANES)
+
+                @pl.when(jnp.min(winner[s, at, :].astype(f32)) < 0.0)
                 def _():
                     fetch = pltpu.make_async_copy(z.at[s, at], best, sems.at[0, 0])
                     fetch.start()
                     fetch.wait()
-                    best[...] = jnp.where(winner[s, at, :] < 0.0, best[...], BIG)
+                    best[...] = jnp.where(winner[s, at, :].astype(f32) < 0.0, best[...], BIG)
                     grad = slots[s, at, :].astype(f32)
-                    count = counts[pl.ds(s, 1), at]
+                    count = counts[:, at]
+                    count = jnp.sum(jnp.where(iota(count.shape, 0) == s, count, 0), axis=0, keepdims=True)
                     shared_winners(pts.at[s, :, :, at], count, table, best, grad, mult, acc, depth, channels)
 
                 return 0
 
-            lax.fori_loop(0, tiles, tile, 0)
+            lax.fori_loop(0, size // LANES, tile, 0)
 
         return 0
 
@@ -800,7 +811,7 @@
     full = (feats + 2) * PACK
     return pl.pallas_call(
         unlift_body,
-        in_specs=hbm(1) + vmem(3) + hbm(3),
+        in_specs=hbm(7),
         out_specs=vmem(2),
         out_shape=[
             jax.ShapeDtypeStruct((feats * PACK, LANES), f32),
@@ -809,11 +820,14 @@
         scratch_shapes=[
             pltpu.VMEM((full, PACK * channels), bf16),
             pltpu.VMEM(points.shape, bf16),
-            pltpu.VMEM((scenes, size, LANES), f32),
+            pltpu.VMEM((scenes, size, LANES), bf16),
             pltpu.VMEM(slots.shape, bf16),
-            pltpu.VMEM((TILE, LANES), f32),
-            pltpu.VMEM((TILE, LANES), f32),
-            pltpu.SemaphoreType.DMA((3, scenes)),
+            pltpu.VMEM((LANES, LANES), f32),
+            pltpu.VMEM((LANES, LANES), f32),
+            pltpu.VMEM(counts.shape, jnp.int32),
+            pltpu.VMEM(weight.shape, bf16),
+            pltpu.VMEM(norm.shape, bf16),
+            pltpu.SemaphoreType.DMA((4, scenes)),
         ],
         cost_estimate=pl.CostEstimate(flops=40_000_000_000, bytes_accessed=16_000_000, transcendentals=0),
         name="unlift",
@@ -828,9 +842,6 @@
     scenes, _, depth, _ = pts.shape
     rows = feats * PACK
     size = pts.shape[3]
-    lift_table(weight, norm, table)
-    acc[...] = inner[...]
-    bias[...] = inner_bias[...]
     peers = payload.shape[0]
     share = kgrad.shape[1]
     for r in range(devices):
@@ -840,27 +851,42 @@
         each = peers // devices
         payload[r * each : (r + 1) * each, :, :share] = jnp.broadcast_to(row[:, None, :], (each, 1, share))
 
-    def scene(s, _):
-        lower = iota((EDGE, LANES), 1) < channels
-        whole = edge_rows_of(edge, s, scenes, lower) + edge_rows_of(far, s, scenes, lower)
-        whole = whole.astype(bf16).astype(f32)
-        grad = jnp.concatenate([whole, jnp.zeros((size - EDGE, LANES), f32)], axis=0)
-        bias[...] += jnp.sum(whole.reshape(EDGE // 8, 8, LANES), axis=0)
+    lower = iota((EDGE, LANES), 1) < channels
+
+    def whole(s):
+        rows_of = edge_rows_of(edge, s, scenes, lower) + edge_rows_of(far, s, scenes, lower)
+        return rows_of.astype(bf16).astype(f32)
+
+    def padded(grad):
+        return jnp.concatenate([grad, jnp.zeros((size - EDGE, LANES), f32)], axis=0)
+
+    total, sums = inner[...], inner_bias[...]
+    for s in range(scenes):
+        grad = whole(s)
+        sums = sums + jnp.sum(grad.reshape(EDGE // 8, 8, LANES), axis=0)
         x = [pts[s, :, part * PACK : (part + 1) * PACK, :].reshape(rows, size) for part in range(depth // PACK)]
-        acc[...] += single_winners(x, winner[s], grad, channels)
-
-        @pl.when(jnp.min(winner[s, :EDGE, :]) < 0.0)
-        def _():
-            fetch = pltpu.make_async_copy(z.at[s, :size], best, sem)
-            fetch.start()
-            fetch.wait()
-            best[...] = jnp.where(winner[s] < 0.0, best[...], BIG)
-            count = counts[pl.ds(s, 1), :][:, :size]
-            shared_winners(pts.at[s], count, table, best, grad, mult, acc, depth, channels)
-
-        return 0
-
-    lax.fori_loop(0, scenes, scene, 0)
+        total = total + single_winners(x, winner[s], padded(grad), channels)
+    acc[...] = total
+    bias[...] = sums
+
+    @pl.when(jnp.min(winner[:, :EDGE, :].astype(f32)) < 0.0)
+    def _():
+        lift_table(weight, norm, table)
+
+        def scene(s, _):
+            @pl.when(jnp.min(winner[s, :EDGE, :].astype(f32)) < 0.0)
+            def _():
+                fetch = pltpu.make_async_copy(z.at[s, :size], best, sem)
+                fetch.start()
+                fetch.wait()
+                best[...] = jnp.where(winner[s].astype(f32) < 0.0, best[...], BIG)
+                count = counts[pl.ds(s, 1), :][:, :size]
+                shared_winners(pts.at[s], count, table, best, padded(whole(s)), mult, acc, depth, channels)
+
+            return 0
+
+        lax.fori_loop(0, scenes, scene, 0)
+
     out = exact_right(one_hot_cols(16, rows), acc[...])
     out = out + swap_halves(out)
     pieces = [out[i : i + 1, :channels] for i in range(feats)]

time: 138 us -> 134 us (0.971); the launches traced: 135 us -> 134 us
  Pallas kernels: 73.6 us -> 67.2 us
  starting transfers between devices: 24 us -> 29.4 us
    all_to_all x4, starting transfers between devices: 14.3 us -> 19.7 us  [exchange(): return lax.all_to_all(x, ('rows', 'scene'), 0, 0, tiled=True)]
    pallas_call x1, Pallas kernels: 18.6 us -> 14.9 us  [gradients(): pl.pallas_call(functools.partial(grad_body, cells, devices, parts), in_sp...]
    pallas_call x1, Pallas kernels: 5.11 us -> 3.3 us  [unlift_edges(): pl.pallas_call(functools.partial(edges_body, devices, parts), grid=(1,),...]
  transfers between devices with their start and end apart: 7 -> 7, of which waited for: 4 -> 4; matrix products, arithmetic and copies ran while one was open for 2% -> 2% of each run, Pallas kernels for 7% -> 6%
where the time goes in v6:
time: 134 us
  Pallas kernels  67.2 us (50%)
  waiting for transfers between devices  29.8 us (22%)
  starting transfers between devices  29.4 us (22%)
  local copies, waits for them, and re-layouts  5.38 us (4%)
  between operations  1.75 us (1%)
    all_to_all x4, waiting for transfers between devices, exchange(): return lax.all_to_all(x, ('rows', 'scene'), 0, 0, tiled=True)  29.8 us
    all_to_all x4, starting transfers between devices, exchange(): return lax.all_to_all(x, ('rows', 'scene'), 0, 0, tiled=True)  19.7 us
    pallas_call x1, Pallas kernels, lift(): pl.pallas_call(lift_body, in_specs=smem(1) + hbm(1) + vmem(5), out_specs=...  16.9 us
    pallas_call x1, Pallas kernels, convolve(): pl.pallas_call(functools.partial(conv_body, devices, parts), in_specs=sme...  16.1 us
    pallas_call x1, Pallas kernels, gradients(): pl.pallas_call(functools.partial(grad_body, cells, devices, parts), in_sp...  14.9 us
    pallas_call x1, Pallas kernels, unlift(): pl.pallas_call(unlift_body, in_specs=hbm(7), out_specs=vmem(2), out_shape...  8.31 us
    ppermute x2, starting transfers between devices, shifted(): return lax.ppermute(x, 'rows', pairs)  6.13 us
    pallas_call x1, Pallas kernels, normalize(): pl.pallas_call(functools.partial(norm_body, cells), in_specs=vmem(1) + hb...  5.61 us
  transfers between devices with their start and end apart: 7, of which 4 were waited for; matrix products, arithmetic and copies ran while one was open for 2% of the time, Pallas kernels for 6%

profile of v6, /device:TPU:0, one launch (start us, length us, event | category | flops | bytes accessed | tf_op | source)
XLA Modules:
  0.0 134.2 jit_solution(7559861584789703171)
XLA Ops:
  0.7 16.9 %lift.1 = (f32[8,768,128]{2,1,0:T(8,128)}, bf16[8,768,128]{2,1,0:T(8,128)(2,1)}, f32[208,128]{1,0:T(8,128)}, f32[32,1,1408]{2,1,0:T(1,128)}, f32[16,128]{1,0:T(8,128)}) custom-call(s32[1,1]{1,0:T(1,128)} %bitcast.mine, bf16[8,9,32,768]{3,2,1,0:T(8,128)(2,1)} %pts.1, s32[8,768]{1,0:T(8,128)} %counts.3, s32[8,768]{1,0:T(8,128)} %pixels.1, ...), custom_call_target="tpu_custom_call" | custom-call | tf_op jit(solution)/shard_map/lift/pallas_call | solution.py:220
  17.6 4.8 %collective-permute-start = (f32[208,128]{1,0:T(8,128)}, f32[208,128]{1,0:T(8,128)S(1)}, u32[]{:S(2)}, u32[]{:S(2)}) collective-permute-start(f32[208,128]{1,0:T(8,128)} %get-tuple-element.46), channel_id=1, source_target_pairs={{0,4},{4,8},{8,12},{12,16},{16,20},{20,24},{24,28},{1,5},{5,9},{9,... | collective-permute-start | bytes 319496 | tf_op jit(solution)/shard_map/ppermute | solution.py:1024
  22.4 4.9 %all-to-all-start = ((f32[32,1,1408]{2,1,0:T(1,128)}), f32[32,1,1408]{2,1,0:T(1,128)S(1)}, u32[]{:S(2)}, u32[]{:S(2)}) async-start(f32[32,1,1408]{2,1,0:T(1,128)} %get-tuple-element.47), calls=%async_computation | async-start | bytes 360448 | tf_op jit(solution)/shard_map/all_to_all | solution.py:1028
  27.4 0.7 reshape.48.pix
  28.2 7.9 %all-to-all-done.got = f32[32,1,1408]{2,1,0:T(1,128)S(1)} async-done(((f32[32,1,1408]{2,1,0:T(1,128)}), f32[32,1,1408]{2,1,0:T(1,128)S(1)}, u32[]{:S(2)}, u32[]{:S(2)}) %all-to-all-start) | async-done | bytes 180256 | tf_op jit(solution)/shard_map/all_to_all | solution.py:1028
  36.1 0.7 copy-done.1
  36.7 16.1 %convolve.1 = (f32[8,4,256,128]{3,2,1,0:T(8,128)}, bf16[8,896,128]{2,1,0:T(8,128)(2,1)}, f32[32,128]{1,0:T(8,128)}, bf16[576,64]{1,0:T(8,128)(2,1)}) custom-call(s32[32,1,192]{2,1,0:T(1,128)} %reshape.48.pix, s32[8,128]{1,0:T(8,128)} %copy-done.8, f32[32,1,1408]{2,1,0:T(1,128)} %copy-done.1, f32[8,768,128]{2,1,0:T(8,128)} %get-tuple-element.48.z_in.z, ...), custom_call_target="tpu_custom_call" | custom-call | tf_op jit(solution)/shard_map/convolve/pallas_call | solution.py:411
  52.8 2.6 %all-to-all-start.1 = ((f32[32,1,128]{2,1,0:T(1,128)}), f32[32,1,128]{2,1,0:T(1,128)S(1)}, u32[]{:S(2)}, u32[]{:S(2)}) async-start(f32[32,1,128]{2,1,0:T(1,128)} %bitcast.21), calls=%async_computation.1 | async-start | bytes 32768 | tf_op jit(solution)/shard_map/all_to_all | solution.py:1028
  55.4 7.1 %all-to-all-done.1.stats = f32[32,1,128]{2,1,0:T(1,128)S(1)} async-done(((f32[32,1,128]{2,1,0:T(1,128)}), f32[32,1,128]{2,1,0:T(1,128)S(1)}, u32[]{:S(2)}, u32[]{:S(2)}) %all-to-all-start.1) | async-done | bytes 16416 | tf_op jit(solution)/shard_map/all_to_all | solution.py:1028
  63.1 5.6 %normalize.1 = (bf16[8,8,64,256]{3,2,1,0:T(8,128)(2,1)}, f32[32,128]{1,0:T(8,128)}) custom-call(f32[32,1,128]{2,1,0:T(1,128)} %copy-done.4, f32[8,4,256,128]{3,2,1,0:T(8,128)} %get-tuple-element.50.conv_in, bf16[8,8,64,256]{3,2,1,0:T(8,128)(2,1)} %cot_in.3, bf16[4,64]{1,0:T(4,128)(2,1)} %norm.11), custom_call_target="tpu_custom_call" | custom-call | tf_op jit(solution)/shard_map/normalize/pallas_call | solution.py:495
  68.7 2.6 %all-to-all-start.2 = ((f32[32,1,128]{2,1,0:T(1,128)}), f32[32,1,128]{2,1,0:T(1,128)S(1)}, u32[]{:S(2)}, u32[]{:S(2)}) async-start(f32[32,1,128]{2,1,0:T(1,128)} %bitcast.20), calls=%async_computation.2 | async-start | bytes 32768 | tf_op jit(solution)/shard_map/all_to_all | solution.py:1028
  71.3 0.7 reshape.51.idx
  72.0 0.6 broadcast_in_dim.11.phase
  72.7 5.7 %all-to-all-done.2.sums = f32[32,1,128]{2,1,0:T(1,128)S(1)} async-done(((f32[32,1,128]{2,1,0:T(1,128)}), f32[32,1,128]{2,1,0:T(1,128)S(1)}, u32[]{:S(2)}, u32[]{:S(2)}) %all-to-all-start.2) | async-done | bytes 16416 | tf_op jit(solution)/shard_map/all_to_all | solution.py:1028
  79.0 14.9 %gradients.1 = (bf16[8,896,128]{2,1,0:T(8,128)(2,1)}, f32[192,128]{1,0:T(8,128)}, f32[192,128]{1,0:T(8,128)}, f32[32,1152]{1,0:T(8,128)}) custom-call(s32[32,1,208]{2,1,0:T(1,128)} %reshape.51.idx, f32[32,1,128]{2,1,0:T(1,128)} %copy-done.4, f32[32,1,128]{2,1,0:T(1,128)} %copy-done.5, f32[8,4,256,128]{3,2,1,0:T(8,128)} %get-tuple-element.50.conv_in, ...), custom_call_target="tpu_custom_call" | custom-call | tf_op jit(solution)/shard_map/gradients/pallas_call | solution.py:667
  93.9 1.3 collective-permute-start.1
  95.2 3.5 %all-to-all-start.3 = ((f32[4,8,1152]{2,1,0:T(8,128)}), f32[4,8,1152]{2,1,0:T(8,128)S(1)}, u32[]{:S(2)}, u32[]{:S(2)}) async-start(f32[4,8,1152]{2,1,0:T(8,128)} %bitcast.15), calls=%async_computation.3 | async-start | bytes 294912 | tf_op jit(solution)/shard_map/all_to_all | solution.py:1090
  98.7 8.3 %unlift.1 = (f32[72,128]{1,0:T(8,128)}, f32[8,128]{1,0:T(8,128)}) custom-call(bf16[8,9,32,768]{3,2,1,0:T(8,128)(2,1)} %pts.1, s32[8,768]{1,0:T(8,128)} %counts.3, bf16[9,64]{1,0:T(8,128)(2,1)} %weight.5, bf16[4,64]{1,0:T(4,128)(2,1)} %norm.11, f32[8,768,128]{2,1,0:T(8,128)} %get-tuple-element.48.z_in.z, ...), custom_call_target="tpu_custom_call" | custom-call | flops 40000000000 | bytes 16000000 | tf_op jit(solution)/shard_map/unlift/pallas_call | solution.py:812
  107.7 3.3 %edges.1 = f32[32,1,2048]{2,1,0:T(1,128)} custom-call(bf16[8,9,32,768]{3,2,1,0:T(8,128)(2,1)} %pts.1, s32[8,768]{1,0:T(8,128)} %counts.3, bf16[9,64]{1,0:T(8,128)(2,1)} %weight.5, bf16[4,64]{1,0:T(4,128)(2,1)} %norm.11, f32[8,768,128]{2,1,0:T(8,128)} %get-tuple-element.48.z_in.z, bf16[8,768,128]{2,1,0:T(8,128)(2,1)} %get-tuple-element.52.winner_in.winner, ...), custom_call_target="tpu_custom_call" | custom-call | tf_op jit(solution)/shard_map/edges/pallas_call | solution.py:906
  111.0 9.7 %all-to-all-start.4 = ((f32[32,1,2048]{2,1,0:T(1,128)}), f32[32,1,2048]{2,1,0:T(1,128)S(1)}, u32[]{:S(2)}, u32[]{:S(2)}) async-start(f32[32,1,2048]{2,1,0:T(1,128)} %edges.1), calls=%async_computation.4 | async-start | bytes 524288 | tf_op jit(solution)/shard_map/all_to_all | solution.py:1028
  121.4 0.7 pad_maximum_fusion.fix
  122.1 9.2 %all-to-all-done.4.got = f32[32,1,2048]{2,1,0:T(1,128)S(1)} async-done(((f32[32,1,2048]{2,1,0:T(1,128)}), f32[32,1,2048]{2,1,0:T(1,128)S(1)}, u32[]{:S(2)}, u32[]{:S(2)}) %all-to-all-start.4) | async-done | bytes 262176 | tf_op jit(solution)/shard_map/all_to_all | solution.py:1028
  131.3 0.7 copy-done
  132.0 2.1 %update.1 = (f32[9,64]{1,0:T(8,128)}, f32[9,2,64]{2,1,0:T(2,128)}, f32[9,64]{1,0:T(8,128)}, bf16[9,64]{1,0:T(8,128)(2,1)}, f32[4,64]{1,0:T(4,128)}, /*index=5*/f...) custom-call(f32[2]{0:T(128)} %pad_maximum_fusion.fix, ...), custom_call_target="tpu_custom_call" | custom-call | tf_op jit(solution)/shard_map/update/pallas_call | solution.py:1011
  (27 shorter events, 2.1 us)
Async XLA Ops:
  0.6 26.7 %copy-start.3 = (s32[8,768]{1,0:T(8,128)S(1)}, s32[8,768]{1,0:T(8,128)}, u32[]{:S(2)}) copy-start(s32[8,768]{1,0:T(8,128)} %pixels.1) | copy-start | bytes 73732
  17.6 10.6 %collective-permute-start = (f32[208,128]{1,0:T(8,128)}, f32[208,128]{1,0:T(8,128)S(1)}, u32[]{:S(2)}, u32[]{:S(2)}) collective-permute-start(f32[208,128]{1,0:T(8,128)} %get-tuple-element.46), channel_id=1, source_target_pairs={{0,4},{4,8},{8,12},{12,16},{16,20},{20,24},{24,28},{1,5},{5,9},{9,... | collective-permute-start | bytes 319496 | tf_op jit(solution)/shard_map/ppermute | solution.py:1024
  22.4 13.7 %all-to-all-start = ((f32[32,1,1408]{2,1,0:T(1,128)}), f32[32,1,1408]{2,1,0:T(1,128)S(1)}, u32[]{:S(2)}, u32[]{:S(2)}) async-start(f32[32,1,1408]{2,1,0:T(1,128)} %get-tuple-element.47), calls=%async_computation | async-start | bytes 360448 | tf_op jit(solution)/shard_map/all_to_all | solution.py:1028
  28.1 7.9 %copy-start.6 = (f32[208,128]{1,0:T(8,128)}, f32[208,128]{1,0:T(8,128)S(1)}, u32[]{:S(2)}) copy-start(f32[208,128]{1,0:T(8,128)S(1)} %collective-permute-done.edge) | copy-start | bytes 319492
  28.2 7.9 %copy-start.8 = (s32[8,128]{1,0:T(8,128)}, s32[8,128]{1,0:T(8,128)S(1)}, u32[]{:S(2)}) copy-start(s32[8,128]{1,0:T(8,128)S(1)} %slice_convert_fusion.far_pix) | copy-start | bytes 12292
  36.1 0.7 copy-start.1
  52.8 9.6 %all-to-all-start.1 = ((f32[32,1,128]{2,1,0:T(1,128)}), f32[32,1,128]{2,1,0:T(1,128)S(1)}, u32[]{:S(2)}, u32[]{:S(2)}) async-start(f32[32,1,128]{2,1,0:T(1,128)} %bitcast.21), calls=%async_computation.1 | async-start | bytes 32768 | tf_op jit(solution)/shard_map/all_to_all | solution.py:1028
  62.5 0.6 copy-start.4
  68.7 9.6 %all-to-all-start.2 = ((f32[32,1,128]{2,1,0:T(1,128)}), f32[32,1,128]{2,1,0:T(1,128)S(1)}, u32[]{:S(2)}, u32[]{:S(2)}) async-start(f32[32,1,128]{2,1,0:T(1,128)} %bitcast.20), calls=%async_computation.2 | async-start | bytes 32768 | tf_op jit(solution)/shard_map/all_to_all | solution.py:1028
  78.4 0.6 copy-start.5
  93.9 13.2 %collective-permute-start.1 = (f32[192,128]{1,0:T(8,128)}, f32[192,128]{1,0:T(8,128)S(1)}, u32[]{:S(2)}, u32[]{:S(2)}) collective-permute-start(f32[192,128]{1,0:T(8,128)} %get-tuple-element.57), channel_id=1, source_target_pairs={{4,0},{8,4},{12,8},{16,12},{20,16},{24,20},{28,24},{5,1},{9,5},{13... | collective-permute-start | bytes 294920 | tf_op jit(solution)/shard_map/ppermute | solution.py:1024
  95.2 11.9 %all-to-all-start.3 = ((f32[4,8,1152]{2,1,0:T(8,128)}), f32[4,8,1152]{2,1,0:T(8,128)S(1)}, u32[]{:S(2)}, u32[]{:S(2)}) async-start(f32[4,8,1152]{2,1,0:T(8,128)} %bitcast.15), calls=%async_computation.3 | async-start | bytes 294912 | tf_op jit(solution)/shard_map/all_to_all | solution.py:1090
  107.0 0.7 copy-start.7
  107.0 0.7 copy-start.2
  111.0 20.3 %all-to-all-start.4 = ((f32[32,1,2048]{2,1,0:T(1,128)}), f32[32,1,2048]{2,1,0:T(1,128)S(1)}, u32[]{:S(2)}, u32[]{:S(2)}) async-start(f32[32,1,2048]{2,1,0:T(1,128)} %edges.1), calls=%async_computation.4 | async-start | bytes 524288 | tf_op jit(solution)/shard_map/all_to_all | solution.py:1028
  131.3 0.7 copy-start

commit v7 on v6

--- a/solution.py
+++ b/solution.py
@@ -207,6 +207,29 @@
     return [pl.BlockSpec(memory_space=pltpu.SMEM)] * count
 
 
+def own_copies(body, small, *refs):
+    refs = list(refs)
+    count = len(small)
+    places, sems = refs[-count - 1 : -1], refs[-1]
+    refs = refs[: -count - 1]
+    copies = []
+    for i, (at, place) in enumerate(zip(small, places)):
+        copies.append(pltpu.make_async_copy(refs[at], place, sems.at[i]))
+        refs[at] = place
+    for copy in copies:
+        copy.start()
+
+    def ready():
+        for copy in copies:
+            copy.wait()
+
+    body(ready, *refs)
+
+
+def places_of(inputs, small):
+    return [pltpu.VMEM(inputs[at].shape, inputs[at].dtype) for at in small] + [pltpu.SemaphoreType.DMA((len(small),))]
+
+
 def hbm(count):
     return [pl.BlockSpec(memory_space=pltpu.HBM)] * count
 
@@ -720,31 +743,52 @@
     return total
 
 
-def shared_winners(pts, count, table, best, grad, mult, acc, depth, channels):
+def shared_winners(pts, count, table, who, grad, share, acc, depth, channels):
     feats = pts.shape[0]
+    size = who.shape[0]
 
     def lifted(part, q):
         xin, _ = lift_inputs(pts[:, part * PACK : (part + 1) * PACK, :], count, part)
         l = dot_nn(jnp.transpose(xin), table[:, q * 256 : (q + 1) * 256])
-        return xin, l[:, :LANES] == best[...], l[:, LANES:] == best[...]
-
-    mult[...] = jnp.zeros_like(mult)
+        return xin[: feats * PACK], l[:, :LANES], l[:, LANES:]
+
+    best = jnp.full((size, LANES), -3.0 * BIG, f32)
+    times = jnp.zeros((size, LANES), f32)
     for part in range(depth // PACK):
         for q in range(PACK // 4):
             _, one, two = lifted(part, q)
-            mult[...] += jnp.where(one, 1.0, 0.0) + jnp.where(two, 1.0, 0.0)
-    many = jnp.maximum(mult[...] + swap_halves(mult[...]), 1.0)
-    mult[...] = grad / many
-    for part in range(depth // PACK):
-        for q in range(PACK // 4):
-            xin, one, two = lifted(part, q)
-            value = jnp.concatenate([jnp.where(one, mult[...], 0.0), jnp.where(two, mult[...], 0.0)], axis=1)
-            acc[...] += fold(q, exact_right(xin[: feats * PACK], value), channels)
+            for l in (one, two):
+                times = jnp.where(l > best, 1.0, jnp.where(l == best, times + 1.0, times))
+                best = jnp.maximum(best, l)
+    other, more = swap_halves(best), swap_halves(times)
+    times = jnp.where(other > best, more, jnp.where(other == best, times + more, times))
+    best = jnp.where(who < 0.0, jnp.maximum(best, other), BIG)
+    share[...] = grad / times
+
+    def add(of):
+        total = None
+        for part in range(depth // PACK):
+            for q in range(PACK // 4):
+                x, one, two = lifted(part, q)
+                value = of(share[...])
+                value = jnp.concatenate([jnp.where(one == best, value, 0.0), jnp.where(two == best, value, 0.0)], axis=1)
+                part_sum = fold(q, dot_nn(x, value.astype(bf16)), channels)
+                total = part_sum if total is None else total + part_sum
+        acc[...] += total
+
+    def rest(x):
+        return x - x.astype(bf16).astype(f32)
+
+    add(lambda x: x)
+
+    @pl.when(jnp.max(jnp.where(who < 0.0, jnp.abs(rest(share[...])), 0.0)) > 0.0)
+    def _():
+        add(rest)
+        add(lambda x: rest(rest(x)))
 
 
 def unlift_body(
-    points, counts_in, weight_in, norm_in, z, winner_in, slots_in, acc, bias,
-    table, pts, winner, slots, best, mult, counts, weight, norm, sems,
+    ready, points, counts, weight, norm, winner_in, slots_in, acc, bias, table, pts, winner, slots, share, seen, sems
 ):
     feats, channels = weight.shape
     scenes, _, depth, size = points.shape
@@ -763,55 +807,62 @@
         copy_in(slots_in, slots, sems.at[2], s).wait()
         total = None
         sums = None
+        least = None
         for t in range(tiles):
             at = slice(t * TILE, (t + 1) * TILE)
             grad = slots[s, at, :].astype(f32)
+            who = winner[s, at, :].astype(f32)
             one = jnp.sum(grad.reshape(TILE // 8, 8, LANES), axis=0)
             sums = one if sums is None else sums + one
+            one = jnp.min(who.reshape(TILE // 8, 8, LANES), axis=0)
+            least = one if least is None else jnp.minimum(least, one)
             x = [pts[s, :, part * PACK : (part + 1) * PACK, at].reshape(rows, TILE) for part in range(depth // PACK)]
-            one = single_winners(x, winner[s, at, :], grad, channels)
+            one = single_winners(x, who, grad, channels)
             total = one if total is None else total + one
         acc[...] += total
         bias[...] += sums
-
-        @pl.when(jnp.min(winner[s].astype(f32)) < 0.0)
-        def _():
-            for i, (of, to) in enumerate(((counts_in, counts), (weight_in, weight), (norm_in, norm))):
-                fetch = pltpu.make_async_copy(of, to, sems.at[3, i])
-                fetch.start()
-                fetch.wait()
-            lift_table(weight, norm, table)
-
-            def tile(t, _):
-                at = pl.ds(pl.multiple_of(t * LANES, LANES), LANES)
-
-                @pl.when(jnp.min(winner[s, at, :].astype(f32)) < 0.0)
-                def _():
-                    fetch = pltpu.make_async_copy(z.at[s, at], best, sems.at[0, 0])
-                    fetch.start()
-                    fetch.wait()
-                    best[...] = jnp.where(winner[s, at, :].astype(f32) < 0.0, best[...], BIG)
-                    grad = slots[s, at, :].astype(f32)
-                    count = counts[:, at]
-                    count = jnp.sum(jnp.where(iota(count.shape, 0) == s, count, 0), axis=0, keepdims=True)
-                    shared_winners(pts.at[s, :, :, at], count, table, best, grad, mult, acc, depth, channels)
-
-                return 0
-
-            lax.fori_loop(0, size // LANES, tile, 0)
-
+        seen[s] = least
         return 0
 
     lax.fori_loop(0, scenes, scene, 0)
-
-
-def unlift(points, counts, weight, norm, z, winner, slots):
+    ready()
+
+    @pl.when(jnp.min(seen[...]) < 0.0)
+    def _():
+        lift_table(weight, norm, table)
+
+        def search(s, _):
+            @pl.when(jnp.min(seen[s]) < 0.0)
+            def _():
+                def tile(t, _):
+                    at = pl.ds(pl.multiple_of(t * LANES, LANES), LANES)
+                    who = winner[s, at, :].astype(f32)
+
+                    @pl.when(jnp.min(who) < 0.0)
+                    def _():
+                        count = counts[:, at]
+                        count = jnp.sum(jnp.where(iota(count.shape, 0) == s, count, 0), axis=0, keepdims=True)
+                        grad = slots[s, at, :].astype(f32)
+                        shared_winners(pts.at[s, :, :, at], count, table, who, grad, share, acc, depth, channels)
+
+                    return 0
+
+                lax.fori_loop(0, size // LANES, tile, 0)
+
+            return 0
+
+        lax.fori_loop(0, scenes, search, 0)
+
+
+def unlift(points, counts, weight, norm, winner, slots):
     scenes, feats, depth, size = points.shape
     channels = weight.shape[1]
     full = (feats + 2) * PACK
+    inputs = (points, counts, weight, norm, winner, slots)
+    small = (1, 2, 3)
     return pl.pallas_call(
-        unlift_body,
-        in_specs=hbm(7),
+        functools.partial(own_copies, unlift_body, small),
+        in_specs=hbm(6),
         out_specs=vmem(2),
         out_shape=[
             jax.ShapeDtypeStruct((feats * PACK, LANES), f32),
@@ -823,20 +874,18 @@
             pltpu.VMEM((scenes, size, LANES), bf16),
             pltpu.VMEM(slots.shape, bf16),
             pltpu.VMEM((LANES, LANES), f32),
-            pltpu.VMEM((LANES, LANES), f32),
-            pltpu.VMEM(counts.shape, jnp.int32),
-            pltpu.VMEM(weight.shape, bf16),
-            pltpu.VMEM(norm.shape, bf16),
-            pltpu.SemaphoreType.DMA((4, scenes)),
-        ],
+            pltpu.VMEM((scenes, 8, LANES), f32),
+            pltpu.SemaphoreType.DMA((3, scenes)),
+        ]
+        + places_of(inputs, small),
         cost_estimate=pl.CostEstimate(flops=40_000_000_000, bytes_accessed=16_000_000, transcendentals=0),
         name="unlift",
-    )(points, counts, weight, norm, z, winner, slots)
+    )(*inputs)
 
 
 def edges_body(
-    devices, parts, pts, counts, weight, norm, z, winner, edge, far, moments, inner, inner_bias, kgrad, payload,
-    table, acc, bias, best, mult, sem,
+    devices, parts, pts, counts, weight, norm, winner, edge, far, moments, inner, inner_bias, kgrad, payload,
+    table, acc, bias, share_of,
 ):
     feats, channels = weight.shape
     scenes, _, depth, _ = pts.shape
@@ -876,12 +925,10 @@
         def scene(s, _):
             @pl.when(jnp.min(winner[s, :EDGE, :].astype(f32)) < 0.0)
             def _():
-                fetch = pltpu.make_async_copy(z.at[s, :size], best, sem)
-                fetch.start()
-                fetch.wait()
-                best[...] = jnp.where(winner[s].astype(f32) < 0.0, best[...], BIG)
                 count = counts[pl.ds(s, 1), :][:, :size]
-                shared_winners(pts.at[s], count, table, best, padded(whole(s)), mult, acc, depth, channels)
+                who = winner[s].astype(f32)
+                grad = padded(whole(s))
+                shared_winners(pts.at[s], count, table, who, grad, share_of, acc, depth, channels)
 
             return 0
 
@@ -898,7 +945,7 @@
     payload[:, :, share:] = jnp.broadcast_to(row[:, None, :], (peers, 1, row.shape[1]))
 
 
-def unlift_edges(devices, parts, peers, points, counts, weight, norm, z, winner, edge, far, moments, inner, bias, kgrad):
+def unlift_edges(devices, parts, peers, points, counts, weight, norm, winner, edge, far, moments, inner, bias, kgrad):
     scenes, feats, depth, _ = points.shape
     channels = weight.shape[1]
     full = (feats + 2) * PACK
@@ -911,7 +958,6 @@
             pl.BlockSpec(counts.shape, lambda i: (0, 0)),
             pl.BlockSpec(weight.shape, lambda i: (0, 0)),
             pl.BlockSpec(norm.shape, lambda i: (0, 0)),
-            pl.BlockSpec(memory_space=pltpu.HBM),
             pl.BlockSpec((scenes, LANES, LANES), lambda i: (0, 0, 0)),
         ]
         + [pl.BlockSpec(x.shape, lambda i: (0, 0)) for x in (edge, far, moments, inner, bias, kgrad)],
@@ -922,11 +968,9 @@
             pltpu.VMEM((feats * PACK, LANES), f32),
             pltpu.VMEM((8, LANES), f32),
             pltpu.VMEM((LANES, LANES), f32),
-            pltpu.VMEM((LANES, LANES), f32),
-            pltpu.SemaphoreType.DMA,
         ],
         name="edges",
-    )(points, counts, weight, norm, z, winner, edge, far, moments, inner, bias, kgrad)
+    )(points, counts, weight, norm, winner, edge, far, moments, inner, bias, kgrad)
 
 
 def adam(fixes, w, states, grad, rate):
@@ -1090,10 +1134,10 @@
         kgrad = lax.all_to_all(kgrad, "scene", 0, 0, tiled=True)
     else:
         kgrad = lax.psum(kgrad, "scene")
-    inner, bias = unlift(points, pillar_counts, point_weight, norm_weight, z, winner, slots)
+    inner, bias = unlift(points, pillar_counts, point_weight, norm_weight, winner, slots)
     far, kgrad, inner, bias = lax.optimization_barrier((far, kgrad, inner, bias))
     payload = unlift_edges(
-        devices, parts, peers, points, pillar_counts, point_weight, norm_weight, z, winner, own_edge, far, moments, inner, bias, kgrad
+        devices, parts, peers, points, pillar_counts, point_weight, norm_weight, winner, own_edge, far, moments, inner, bias, kgrad
     )
     got = exchange(payload)
     steps_done = step_count[0].astype(f32)

time: 134 us -> 136 us (1.015)
    all_to_all x4, starting transfers between devices: 19.7 us -> 21.1 us  [exchange(): return lax.all_to_all(x, ('rows', 'scene'), 0, 0, tiled=True)]
where the time goes in v7:
time: 136 us; the launch traced here: 135 us
  Pallas kernels  67.2 us (49%)
  starting transfers between devices  30.6 us (22%)
  waiting for transfers between devices  29.9 us (22%)
  local copies, waits for them, and re-layouts  5.36 us (4%)
  between operations  1.74 us (1%)
    all_to_all x4, waiting for transfers between devices, exchange(): return lax.all_to_all(x, ('rows', 'scene'), 0, 0, tiled=True)  29.9 us
    all_to_all x4, starting transfers between devices, exchange(): return lax.all_to_all(x, ('rows', 'scene'), 0, 0, tiled=True)  21.1 us
    pallas_call x1, Pallas kernels, lift(): pl.pallas_call(lift_body, in_specs=smem(1) + hbm(1) + vmem(5), out_specs=...  16.9 us
    pallas_call x1, Pallas kernels, convolve(): pl.pallas_call(functools.partial(conv_body, devices, parts), in_specs=sme...  16.1 us
    pallas_call x1, Pallas kernels, gradients(): pl.pallas_call(functools.partial(grad_body, cells, devices, parts), in_sp...  14.9 us
    pallas_call x1, Pallas kernels, unlift(): pl.pallas_call(functools.partial(own_copies, unlift_body, small), in_spec...  8.37 us
    ppermute x2, starting transfers between devices, shifted(): return lax.ppermute(x, 'rows', pairs)  6.13 us
    pallas_call x1, Pallas kernels, normalize(): pl.pallas_call(functools.partial(norm_body, cells), in_specs=vmem(1) + hb...  5.61 us
  transfers between devices with their start and end apart: 7, of which 4 were waited for; matrix products, arithmetic and copies ran while one was open for 2% of the time, Pallas kernels for 6%

profile of v7, /device:TPU:0, one launch (start us, length us, event | category | flops | bytes accessed | tf_op | source)
XLA Modules:
  0.0 135.5 jit_solution(5801200148814416862)
XLA Ops:
  0.7 16.9 %lift.1 = (f32[8,768,128]{2,1,0:T(8,128)}, bf16[8,768,128]{2,1,0:T(8,128)(2,1)}, f32[208,128]{1,0:T(8,128)}, f32[32,1,1408]{2,1,0:T(1,128)}, f32[16,128]{1,0:T(8,128)}) custom-call(s32[1,1]{1,0:T(1,128)} %bitcast.mine, bf16[8,9,32,768]{3,2,1,0:T(8,128)(2,1)} %pts.1, s32[8,768]{1,0:T(8,128)} %counts.3, s32[8,768]{1,0:T(8,128)} %pixels.1, ...), custom_call_target="tpu_custom_call" | custom-call | tf_op jit(solution)/shard_map/lift/pallas_call | solution.py:243
  17.6 4.8 %collective-permute-start = (f32[208,128]{1,0:T(8,128)}, f32[208,128]{1,0:T(8,128)S(1)}, u32[]{:S(2)}, u32[]{:S(2)}) collective-permute-start(f32[208,128]{1,0:T(8,128)} %get-tuple-element.46), channel_id=1, source_target_pairs={{0,4},{4,8},{8,12},{12,16},{16,20},{20,24},{24,28},{1,5},{5,9},{9,... | collective-permute-start | bytes 319496 | tf_op jit(solution)/shard_map/ppermute | solution.py:1068
  22.4 4.9 %all-to-all-start = ((f32[32,1,1408]{2,1,0:T(1,128)}), f32[32,1,1408]{2,1,0:T(1,128)S(1)}, u32[]{:S(2)}, u32[]{:S(2)}) async-start(f32[32,1,1408]{2,1,0:T(1,128)} %get-tuple-element.47), calls=%async_computation | async-start | bytes 360448 | tf_op jit(solution)/shard_map/all_to_all | solution.py:1072
  27.4 0.7 reshape.48.pix
  28.2 7.9 %all-to-all-done.got = f32[32,1,1408]{2,1,0:T(1,128)S(1)} async-done(((f32[32,1,1408]{2,1,0:T(1,128)}), f32[32,1,1408]{2,1,0:T(1,128)S(1)}, u32[]{:S(2)}, u32[]{:S(2)}) %all-to-all-start) | async-done | bytes 180256 | tf_op jit(solution)/shard_map/all_to_all | solution.py:1072
  36.1 0.7 copy-done.1
  36.7 16.1 %convolve.1 = (f32[8,4,256,128]{3,2,1,0:T(8,128)}, bf16[8,896,128]{2,1,0:T(8,128)(2,1)}, f32[32,128]{1,0:T(8,128)}, bf16[576,64]{1,0:T(8,128)(2,1)}) custom-call(s32[32,1,192]{2,1,0:T(1,128)} %reshape.48.pix, s32[8,128]{1,0:T(8,128)} %copy-done.8, f32[32,1,1408]{2,1,0:T(1,128)} %copy-done.1, f32[8,768,128]{2,1,0:T(8,128)} %get-tuple-element.48.z_in, ...), custom_call_target="tpu_custom_call" | custom-call | tf_op jit(solution)/shard_map/convolve/pallas_call | solution.py:434
  52.8 2.6 %all-to-all-start.1 = ((f32[32,1,128]{2,1,0:T(1,128)}), f32[32,1,128]{2,1,0:T(1,128)S(1)}, u32[]{:S(2)}, u32[]{:S(2)}) async-start(f32[32,1,128]{2,1,0:T(1,128)} %bitcast.21), calls=%async_computation.1 | async-start | bytes 32768 | tf_op jit(solution)/shard_map/all_to_all | solution.py:1072
  55.4 7.1 %all-to-all-done.1.stats = f32[32,1,128]{2,1,0:T(1,128)S(1)} async-done(((f32[32,1,128]{2,1,0:T(1,128)}), f32[32,1,128]{2,1,0:T(1,128)S(1)}, u32[]{:S(2)}, u32[]{:S(2)}) %all-to-all-start.1) | async-done | bytes 16416 | tf_op jit(solution)/shard_map/all_to_all | solution.py:1072
  63.1 5.6 %normalize.1 = (bf16[8,8,64,256]{3,2,1,0:T(8,128)(2,1)}, f32[32,128]{1,0:T(8,128)}) custom-call(f32[32,1,128]{2,1,0:T(1,128)} %copy-done.4, f32[8,4,256,128]{3,2,1,0:T(8,128)} %get-tuple-element.50.conv_in, bf16[8,8,64,256]{3,2,1,0:T(8,128)(2,1)} %cot_in.3, bf16[4,64]{1,0:T(4,128)(2,1)} %norm.11), custom_call_target="tpu_custom_call" | custom-call | tf_op jit(solution)/shard_map/normalize/pallas_call | solution.py:518
  68.7 2.6 %all-to-all-start.2 = ((f32[32,1,128]{2,1,0:T(1,128)}), f32[32,1,128]{2,1,0:T(1,128)S(1)}, u32[]{:S(2)}, u32[]{:S(2)}) async-start(f32[32,1,128]{2,1,0:T(1,128)} %bitcast.20), calls=%async_computation.2 | async-start | bytes 32768 | tf_op jit(solution)/shard_map/all_to_all | solution.py:1072
  71.3 0.7 reshape.51.idx
  72.0 0.6 broadcast_in_dim.11.phase
  72.7 5.7 %all-to-all-done.2.sums = f32[32,1,128]{2,1,0:T(1,128)S(1)} async-done(((f32[32,1,128]{2,1,0:T(1,128)}), f32[32,1,128]{2,1,0:T(1,128)S(1)}, u32[]{:S(2)}, u32[]{:S(2)}) %all-to-all-start.2) | async-done | bytes 16416 | tf_op jit(solution)/shard_map/all_to_all | solution.py:1072
  79.0 14.9 %gradients.1 = (bf16[8,896,128]{2,1,0:T(8,128)(2,1)}, f32[192,128]{1,0:T(8,128)}, f32[192,128]{1,0:T(8,128)}, f32[32,1152]{1,0:T(8,128)}) custom-call(s32[32,1,208]{2,1,0:T(1,128)} %reshape.51.idx, f32[32,1,128]{2,1,0:T(1,128)} %copy-done.4, f32[32,1,128]{2,1,0:T(1,128)} %copy-done.5, f32[8,4,256,128]{3,2,1,0:T(8,128)} %get-tuple-element.50.conv_in, ...), custom_call_target="tpu_custom_call" | custom-call | tf_op jit(solution)/shard_map/gradients/pallas_call | solution.py:690
  93.8 1.3 collective-permute-start.1
  95.1 3.3 %all-to-all-start.3 = ((f32[4,8,1152]{2,1,0:T(8,128)}), f32[4,8,1152]{2,1,0:T(8,128)S(1)}, u32[]{:S(2)}, u32[]{:S(2)}) async-start(f32[4,8,1152]{2,1,0:T(8,128)} %bitcast.15), calls=%async_computation.3 | async-start | bytes 294912 | tf_op jit(solution)/shard_map/all_to_all | solution.py:1134
  98.5 8.4 %unlift.1 = (f32[72,128]{1,0:T(8,128)}, f32[8,128]{1,0:T(8,128)}) custom-call(bf16[8,9,32,768]{3,2,1,0:T(8,128)(2,1)} %pts.1, s32[8,768]{1,0:T(8,128)} %counts.3, bf16[9,64]{1,0:T(8,128)(2,1)} %weight.5, bf16[4,64]{1,0:T(4,128)(2,1)} %norm.11, bf16[8,768,128]{2,1,0:T(8,128)(2,1)} %get-tuple-element.52.refs_4_.winner, ...), custom_call_target="tpu_custom_call" | custom-call | flops 40000000000 | bytes 16000000 | tf_op jit(solution)/shard_map/unlift/pallas_call | solution.py:863
  106.9 0.6 copy-done.7
  107.6 3.3 %edges.1 = f32[32,1,2048]{2,1,0:T(1,128)} custom-call(bf16[8,9,32,768]{3,2,1,0:T(8,128)(2,1)} %pts.1, s32[8,768]{1,0:T(8,128)} %counts.3, bf16[9,64]{1,0:T(8,128)(2,1)} %weight.5, bf16[4,64]{1,0:T(4,128)(2,1)} %norm.11, bf16[8,768,128]{2,1,0:T(8,128)(2,1)} %get-tuple-element.52.refs_4_.winner, f32[192,128]{1,0:T(8,128)} %get-tuple-element.56.edge, ...), custom_call_target="tpu_custom_call" | custom-call | tf_op jit(solution)/shard_map/edges/pallas_call | solution.py:953
  110.9 11.1 %all-to-all-start.4 = ((f32[32,1,2048]{2,1,0:T(1,128)}), f32[32,1,2048]{2,1,0:T(1,128)S(1)}, u32[]{:S(2)}, u32[]{:S(2)}) async-start(f32[32,1,2048]{2,1,0:T(1,128)} %edges.1), calls=%async_computation.4 | async-start | bytes 524288 | tf_op jit(solution)/shard_map/all_to_all | solution.py:1072
  123.3 9.3 %all-to-all-done.4.got = f32[32,1,2048]{2,1,0:T(1,128)S(1)} async-done(((f32[32,1,2048]{2,1,0:T(1,128)}), f32[32,1,2048]{2,1,0:T(1,128)S(1)}, u32[]{:S(2)}, u32[]{:S(2)}) %all-to-all-start.4) | async-done | bytes 262176 | tf_op jit(solution)/shard_map/all_to_all | solution.py:1072
  132.6 0.7 copy-done
  133.3 2.1 %update.1 = (f32[9,64]{1,0:T(8,128)}, f32[9,2,64]{2,1,0:T(2,128)}, f32[9,64]{1,0:T(8,128)}, bf16[9,64]{1,0:T(8,128)(2,1)}, f32[4,64]{1,0:T(4,128)}, /*index=5*/f...) custom-call(f32[2]{0:T(128)} %pad_maximum_fusion.fix, ...), custom_call_target="tpu_custom_call" | custom-call | tf_op jit(solution)/shard_map/update/pallas_call | solution.py:1055
  (27 shorter events, 2.0 us)
Async XLA Ops:
  0.6 26.7 %copy-start.3 = (s32[8,768]{1,0:T(8,128)S(1)}, s32[8,768]{1,0:T(8,128)}, u32[]{:S(2)}) copy-start(s32[8,768]{1,0:T(8,128)} %pixels.1) | copy-start | bytes 73732
  17.6 10.6 %collective-permute-start = (f32[208,128]{1,0:T(8,128)}, f32[208,128]{1,0:T(8,128)S(1)}, u32[]{:S(2)}, u32[]{:S(2)}) collective-permute-start(f32[208,128]{1,0:T(8,128)} %get-tuple-element.46), channel_id=1, source_target_pairs={{0,4},{4,8},{8,12},{12,16},{16,20},{20,24},{24,28},{1,5},{5,9},{9,... | collective-permute-start | bytes 319496 | tf_op jit(solution)/shard_map/ppermute | solution.py:1068
  22.4 13.7 %all-to-all-start = ((f32[32,1,1408]{2,1,0:T(1,128)}), f32[32,1,1408]{2,1,0:T(1,128)S(1)}, u32[]{:S(2)}, u32[]{:S(2)}) async-start(f32[32,1,1408]{2,1,0:T(1,128)} %get-tuple-element.47), calls=%async_computation | async-start | bytes 360448 | tf_op jit(solution)/shard_map/all_to_all | solution.py:1072
  28.1 7.9 %copy-start.6 = (f32[208,128]{1,0:T(8,128)}, f32[208,128]{1,0:T(8,128)S(1)}, u32[]{:S(2)}) copy-start(f32[208,128]{1,0:T(8,128)S(1)} %collective-permute-done.edge) | copy-start | bytes 319492
  28.2 7.9 %copy-start.8 = (s32[8,128]{1,0:T(8,128)}, s32[8,128]{1,0:T(8,128)S(1)}, u32[]{:S(2)}) copy-start(s32[8,128]{1,0:T(8,128)S(1)} %slice_convert_fusion.far_pix) | copy-start | bytes 12292
  36.1 0.7 copy-start.1
  52.8 9.6 %all-to-all-start.1 = ((f32[32,1,128]{2,1,0:T(1,128)}), f32[32,1,128]{2,1,0:T(1,128)S(1)}, u32[]{:S(2)}, u32[]{:S(2)}) async-start(f32[32,1,128]{2,1,0:T(1,128)} %bitcast.21), calls=%async_computation.1 | async-start | bytes 32768 | tf_op jit(solution)/shard_map/all_to_all | solution.py:1072
  62.5 0.6 copy-start.4
  68.7 9.6 %all-to-all-start.2 = ((f32[32,1,128]{2,1,0:T(1,128)}), f32[32,1,128]{2,1,0:T(1,128)S(1)}, u32[]{:S(2)}, u32[]{:S(2)}) async-start(f32[32,1,128]{2,1,0:T(1,128)} %bitcast.20), calls=%async_computation.2 | async-start | bytes 32768 | tf_op jit(solution)/shard_map/all_to_all | solution.py:1072
  78.4 0.6 copy-start.5
  93.8 13.0 %collective-permute-start.1 = (f32[192,128]{1,0:T(8,128)}, f32[192,128]{1,0:T(8,128)S(1)}, u32[]{:S(2)}, u32[]{:S(2)}) collective-permute-start(f32[192,128]{1,0:T(8,128)} %get-tuple-element.57), channel_id=1, source_target_pairs={{4,0},{8,4},{12,8},{16,12},{20,16},{24,20},{28,24},{5,1},{9,5},{13... | collective-permute-start | bytes 294920 | tf_op jit(solution)/shard_map/ppermute | solution.py:1068
  95.1 11.8 %all-to-all-start.3 = ((f32[4,8,1152]{2,1,0:T(8,128)}), f32[4,8,1152]{2,1,0:T(8,128)S(1)}, u32[]{:S(2)}, u32[]{:S(2)}) async-start(f32[4,8,1152]{2,1,0:T(8,128)} %bitcast.15), calls=%async_computation.3 | async-start | bytes 294912 | tf_op jit(solution)/shard_map/all_to_all | solution.py:1134
  106.9 0.6 copy-start.7
  106.9 0.7 copy-start.2
  110.9 21.7 %all-to-all-start.4 = ((f32[32,1,2048]{2,1,0:T(1,128)}), f32[32,1,2048]{2,1,0:T(1,128)S(1)}, u32[]{:S(2)}, u32[]{:S(2)}) async-start(f32[32,1,2048]{2,1,0:T(1,128)} %edges.1), calls=%async_computation.4 | async-start | bytes 524288 | tf_op jit(solution)/shard_map/all_to_all | solution.py:1072
  132.6 0.7 copy-start

commit v8 on v7

--- a/solution.py
+++ b/solution.py
@@ -115,7 +115,7 @@
 
 def lift_body(
     mine, points, counts, pixels, weight, norm, kernel, z_out, winner_out, edge, payload, moments,
-    table, gram, wide, pts, z, winner, sems,
+    table, gram, wide, pts, z, winner, low, high, sems,
 ):
     feats, channels = weight.shape
     scenes, _, depth, size = points.shape
@@ -139,23 +139,23 @@
         for t in range(size // LANES):
             turned = [jnp.transpose(x[:, t * LANES : (t + 1) * LANES]) for x in inputs]
             for h in range(LANES // ROWS):
+                at = slice(t * LANES + h * ROWS, t * LANES + (h + 1) * ROWS)
                 best = None
                 for part in range(depth // PACK):
                     lhs = turned[part][h * ROWS : (h + 1) * ROWS]
                     for q in range(PACK // 4):
                         l = dot_nn(lhs, table[:, q * 256 : (q + 1) * 256])
-                        one, two = l[:, :LANES], l[:, LANES:]
-                        n_one, n_two = float(part * PACK + q * 4), float(part * PACK + q * 4 + 2)
-                        m = jnp.maximum(one, two)
-                        low = jnp.where(two > one, n_two, n_one)
-                        high = jnp.where(two >= one, n_two, n_one)
-                        if best is None:
-                            best, first, last = m, low, high
-                        else:
-                            first = jnp.where(m > best, low, first)
-                            last = jnp.where(m >= best, high, last)
-                            best = jnp.maximum(best, m)
-                at = slice(t * LANES + h * ROWS, t * LANES + (h + 1) * ROWS)
+                        for k, piece in enumerate((l[:, :LANES], l[:, LANES:])):
+                            n = jnp.full((ROWS, LANES), float(part * PACK + q * 4 + 2 * k), f32)
+                            if best is None:
+                                first = n
+                                high[at, :] = n
+                                best = piece
+                            else:
+                                first = jnp.where(piece > best, n, first)
+                                pltpu.store(high.at[at, :], n, mask=piece >= best)
+                                best = jnp.maximum(best, piece)
+                last = high[at, :]
                 upper = (iota((ROWS, LANES), 1) >= channels).astype(f32)
                 first, last = first + upper, last + upper
                 other = swap_halves(best)
@@ -258,6 +258,8 @@
             pltpu.VMEM(points.shape, bf16),
             pltpu.VMEM((scenes, size, LANES), f32),
             pltpu.VMEM((scenes, size, LANES), bf16),
+            pltpu.VMEM((size, LANES), f32),
+            pltpu.VMEM((size, LANES), f32),
             pltpu.SemaphoreType.DMA((3, scenes)),
         ],
         name="lift",

time: 136 us -> 130 us (0.956)
  starting transfers between devices: 30.6 us -> 26.5 us
  Pallas kernels: 67.2 us -> 65.5 us
    all_to_all x4, starting transfers between devices: 21.1 us -> 17 us  [exchange(): return lax.all_to_all(x, ('rows', 'scene'), 0, 0, tiled=True)]
    pallas_call x1, Pallas kernels: 16.9 us -> 15.2 us  [lift(): pl.pallas_call(lift_body, in_specs=smem(1) + hbm(1) + vmem(5), out_specs=...]
where the time goes in v8:
time: 130 us
  Pallas kernels  65.5 us (50%)
  waiting for transfers between devices  29.9 us (23%)
  starting transfers between devices  26.5 us (20%)
  local copies, waits for them, and re-layouts  5.36 us (4%)
  between operations  1.74 us (1%)
    all_to_all x4, waiting for transfers between devices, exchange(): return lax.all_to_all(x, ('rows', 'scene'), 0, 0, tiled=True)  29.9 us
    all_to_all x4, starting transfers between devices, exchange(): return lax.all_to_all(x, ('rows', 'scene'), 0, 0, tiled=True)  17 us
    pallas_call x1, Pallas kernels, convolve(): pl.pallas_call(functools.partial(conv_body, devices, parts), in_specs=sme...  16.1 us
    pallas_call x1, Pallas kernels, lift(): pl.pallas_call(lift_body, in_specs=smem(1) + hbm(1) + vmem(5), out_specs=...  15.2 us
    pallas_call x1, Pallas kernels, gradients(): pl.pallas_call(functools.partial(grad_body, cells, devices, parts), in_sp...  14.9 us
    pallas_call x1, Pallas kernels, unlift(): pl.pallas_call(functools.partial(own_copies, unlift_body, small), in_spec...  8.37 us
    ppermute x2, starting transfers between devices, shifted(): return lax.ppermute(x, 'rows', pairs)  6.14 us
    pallas_call x1, Pallas kernels, normalize(): pl.pallas_call(functools.partial(norm_body, cells), in_specs=vmem(1) + hb...  5.61 us
  transfers between devices with their start and end apart: 7, of which 4 were waited for; matrix products, arithmetic and copies ran while one was open for 2% of the time, Pallas kernels for 6%

profile of v8, /device:TPU:0, one launch (start us, length us, event | category | flops | bytes accessed | tf_op | source)
XLA Modules:
  0.0 129.6 jit_solution(18426960620606534924)
XLA Ops:
  0.7 15.2 %lift.1 = (f32[8,768,128]{2,1,0:T(8,128)}, bf16[8,768,128]{2,1,0:T(8,128)(2,1)}, f32[208,128]{1,0:T(8,128)}, f32[32,1,1408]{2,1,0:T(1,128)}, f32[16,128]{1,0:T(8,128)}) custom-call(s32[1,1]{1,0:T(1,128)} %bitcast.mine, bf16[8,9,32,768]{3,2,1,0:T(8,128)(2,1)} %pts.1, s32[8,768]{1,0:T(8,128)} %counts.3, s32[8,768]{1,0:T(8,128)} %pixels.1, ...), custom_call_target="tpu_custom_call" | custom-call | tf_op jit(solution)/shard_map/lift/pallas_call | solution.py:243
  15.9 4.8 %collective-permute-start = (f32[208,128]{1,0:T(8,128)}, f32[208,128]{1,0:T(8,128)S(1)}, u32[]{:S(2)}, u32[]{:S(2)}) collective-permute-start(f32[208,128]{1,0:T(8,128)} %get-tuple-element.46), channel_id=1, source_target_pairs={{0,4},{4,8},{8,12},{12,16},{16,20},{20,24},{24,28},{1,5},{5,9},{9,... | collective-permute-start | bytes 319496 | tf_op jit(solution)/shard_map/ppermute | solution.py:1070
  20.7 4.9 %all-to-all-start = ((f32[32,1,1408]{2,1,0:T(1,128)}), f32[32,1,1408]{2,1,0:T(1,128)S(1)}, u32[]{:S(2)}, u32[]{:S(2)}) async-start(f32[32,1,1408]{2,1,0:T(1,128)} %get-tuple-element.47), calls=%async_computation | async-start | bytes 360448 | tf_op jit(solution)/shard_map/all_to_all | solution.py:1074
  25.7 0.7 reshape.48.pix
  26.5 7.9 %all-to-all-done.got = f32[32,1,1408]{2,1,0:T(1,128)S(1)} async-done(((f32[32,1,1408]{2,1,0:T(1,128)}), f32[32,1,1408]{2,1,0:T(1,128)S(1)}, u32[]{:S(2)}, u32[]{:S(2)}) %all-to-all-start) | async-done | bytes 180256 | tf_op jit(solution)/shard_map/all_to_all | solution.py:1074
  34.4 0.7 copy-done.1
  35.0 16.1 %convolve.1 = (f32[8,4,256,128]{3,2,1,0:T(8,128)}, bf16[8,896,128]{2,1,0:T(8,128)(2,1)}, f32[32,128]{1,0:T(8,128)}, bf16[576,64]{1,0:T(8,128)(2,1)}) custom-call(s32[32,1,192]{2,1,0:T(1,128)} %reshape.48.pix, s32[8,128]{1,0:T(8,128)} %copy-done.8, f32[32,1,1408]{2,1,0:T(1,128)} %copy-done.1, f32[8,768,128]{2,1,0:T(8,128)} %get-tuple-element.48.z_in, ...), custom_call_target="tpu_custom_call" | custom-call | tf_op jit(solution)/shard_map/convolve/pallas_call | solution.py:436
  51.1 2.6 %all-to-all-start.1 = ((f32[32,1,128]{2,1,0:T(1,128)}), f32[32,1,128]{2,1,0:T(1,128)S(1)}, u32[]{:S(2)}, u32[]{:S(2)}) async-start(f32[32,1,128]{2,1,0:T(1,128)} %bitcast.21), calls=%async_computation.1 | async-start | bytes 32768 | tf_op jit(solution)/shard_map/all_to_all | solution.py:1074
  53.7 7.1 %all-to-all-done.1.stats = f32[32,1,128]{2,1,0:T(1,128)S(1)} async-done(((f32[32,1,128]{2,1,0:T(1,128)}), f32[32,1,128]{2,1,0:T(1,128)S(1)}, u32[]{:S(2)}, u32[]{:S(2)}) %all-to-all-start.1) | async-done | bytes 16416 | tf_op jit(solution)/shard_map/all_to_all | solution.py:1074
  61.4 5.6 %normalize.1 = (bf16[8,8,64,256]{3,2,1,0:T(8,128)(2,1)}, f32[32,128]{1,0:T(8,128)}) custom-call(f32[32,1,128]{2,1,0:T(1,128)} %copy-done.4, f32[8,4,256,128]{3,2,1,0:T(8,128)} %get-tuple-element.50.conv_in, bf16[8,8,64,256]{3,2,1,0:T(8,128)(2,1)} %cot_in.3, bf16[4,64]{1,0:T(4,128)(2,1)} %norm.11), custom_call_target="tpu_custom_call" | custom-call | tf_op jit(solution)/shard_map/normalize/pallas_call | solution.py:520
  67.0 2.6 %all-to-all-start.2 = ((f32[32,1,128]{2,1,0:T(1,128)}), f32[32,1,128]{2,1,0:T(1,128)S(1)}, u32[]{:S(2)}, u32[]{:S(2)}) async-start(f32[32,1,128]{2,1,0:T(1,128)} %bitcast.20), calls=%async_computation.2 | async-start | bytes 32768 | tf_op jit(solution)/shard_map/all_to_all | solution.py:1074
  69.6 0.7 reshape.51.idx
  70.3 0.6 broadcast_in_dim.11.phase
  71.0 5.7 %all-to-all-done.2.sums = f32[32,1,128]{2,1,0:T(1,128)S(1)} async-done(((f32[32,1,128]{2,1,0:T(1,128)}), f32[32,1,128]{2,1,0:T(1,128)S(1)}, u32[]{:S(2)}, u32[]{:S(2)}) %all-to-all-start.2) | async-done | bytes 16416 | tf_op jit(solution)/shard_map/all_to_all | solution.py:1074
  77.3 14.9 %gradients.1 = (bf16[8,896,128]{2,1,0:T(8,128)(2,1)}, f32[192,128]{1,0:T(8,128)}, f32[192,128]{1,0:T(8,128)}, f32[32,1152]{1,0:T(8,128)}) custom-call(s32[32,1,208]{2,1,0:T(1,128)} %reshape.51.idx, f32[32,1,128]{2,1,0:T(1,128)} %copy-done.4, f32[32,1,128]{2,1,0:T(1,128)} %copy-done.5, f32[8,4,256,128]{3,2,1,0:T(8,128)} %get-tuple-element.50.conv_in, ...), custom_call_target="tpu_custom_call" | custom-call | tf_op jit(solution)/shard_map/gradients/pallas_call | solution.py:692
  92.1 1.3 collective-permute-start.1
  93.4 3.3 %all-to-all-start.3 = ((f32[4,8,1152]{2,1,0:T(8,128)}), f32[4,8,1152]{2,1,0:T(8,128)S(1)}, u32[]{:S(2)}, u32[]{:S(2)}) async-start(f32[4,8,1152]{2,1,0:T(8,128)} %bitcast.15), calls=%async_computation.3 | async-start | bytes 294912 | tf_op jit(solution)/shard_map/all_to_all | solution.py:1136
  96.8 8.4 %unlift.1 = (f32[72,128]{1,0:T(8,128)}, f32[8,128]{1,0:T(8,128)}) custom-call(bf16[8,9,32,768]{3,2,1,0:T(8,128)(2,1)} %pts.1, s32[8,768]{1,0:T(8,128)} %counts.3, bf16[9,64]{1,0:T(8,128)(2,1)} %weight.5, bf16[4,64]{1,0:T(4,128)(2,1)} %norm.11, bf16[8,768,128]{2,1,0:T(8,128)(2,1)} %get-tuple-element.52.refs_4_.winner, ...), custom_call_target="tpu_custom_call" | custom-call | flops 40000000000 | bytes 16000000 | tf_op jit(solution)/shard_map/unlift/pallas_call | solution.py:865
  105.2 0.6 copy-done.7
  105.9 3.3 %edges.1 = f32[32,1,2048]{2,1,0:T(1,128)} custom-call(bf16[8,9,32,768]{3,2,1,0:T(8,128)(2,1)} %pts.1, s32[8,768]{1,0:T(8,128)} %counts.3, bf16[9,64]{1,0:T(8,128)(2,1)} %weight.5, bf16[4,64]{1,0:T(4,128)(2,1)} %norm.11, bf16[8,768,128]{2,1,0:T(8,128)(2,1)} %get-tuple-element.52.refs_4_.winner, f32[192,128]{1,0:T(8,128)} %get-tuple-element.56.edge, ...), custom_call_target="tpu_custom_call" | custom-call | tf_op jit(solution)/shard_map/edges/pallas_call | solution.py:955
  109.2 6.9 %all-to-all-start.4 = ((f32[32,1,2048]{2,1,0:T(1,128)}), f32[32,1,2048]{2,1,0:T(1,128)S(1)}, u32[]{:S(2)}, u32[]{:S(2)}) async-start(f32[32,1,2048]{2,1,0:T(1,128)} %edges.1), calls=%async_computation.4 | async-start | bytes 524288 | tf_op jit(solution)/shard_map/all_to_all | solution.py:1074
  117.4 9.3 %all-to-all-done.4.got = f32[32,1,2048]{2,1,0:T(1,128)S(1)} async-done(((f32[32,1,2048]{2,1,0:T(1,128)}), f32[32,1,2048]{2,1,0:T(1,128)S(1)}, u32[]{:S(2)}, u32[]{:S(2)}) %all-to-all-start.4) | async-done | bytes 262176 | tf_op jit(solution)/shard_map/all_to_all | solution.py:1074
  126.7 0.7 copy-done
  127.4 2.1 %update.1 = (f32[9,64]{1,0:T(8,128)}, f32[9,2,64]{2,1,0:T(2,128)}, f32[9,64]{1,0:T(8,128)}, bf16[9,64]{1,0:T(8,128)(2,1)}, f32[4,64]{1,0:T(4,128)}, /*index=5*/f...) custom-call(f32[2]{0:T(128)} %pad_maximum_fusion.fix, ...), custom_call_target="tpu_custom_call" | custom-call | tf_op jit(solution)/shard_map/update/pallas_call | solution.py:1057
  (27 shorter events, 2.0 us)
Async XLA Ops:
  0.6 25.0 %copy-start.3 = (s32[8,768]{1,0:T(8,128)S(1)}, s32[8,768]{1,0:T(8,128)}, u32[]{:S(2)}) copy-start(s32[8,768]{1,0:T(8,128)} %pixels.1) | copy-start | bytes 73732
  15.9 10.6 %collective-permute-start = (f32[208,128]{1,0:T(8,128)}, f32[208,128]{1,0:T(8,128)S(1)}, u32[]{:S(2)}, u32[]{:S(2)}) collective-permute-start(f32[208,128]{1,0:T(8,128)} %get-tuple-element.46), channel_id=1, source_target_pairs={{0,4},{4,8},{8,12},{12,16},{16,20},{20,24},{24,28},{1,5},{5,9},{9,... | collective-permute-start | bytes 319496 | tf_op jit(solution)/shard_map/ppermute | solution.py:1070
  20.7 13.7 %all-to-all-start = ((f32[32,1,1408]{2,1,0:T(1,128)}), f32[32,1,1408]{2,1,0:T(1,128)S(1)}, u32[]{:S(2)}, u32[]{:S(2)}) async-start(f32[32,1,1408]{2,1,0:T(1,128)} %get-tuple-element.47), calls=%async_computation | async-start | bytes 360448 | tf_op jit(solution)/shard_map/all_to_all | solution.py:1074
  26.5 7.9 %copy-start.6 = (f32[208,128]{1,0:T(8,128)}, f32[208,128]{1,0:T(8,128)S(1)}, u32[]{:S(2)}) copy-start(f32[208,128]{1,0:T(8,128)S(1)} %collective-permute-done.edge) | copy-start | bytes 319492
  26.5 7.9 %copy-start.8 = (s32[8,128]{1,0:T(8,128)}, s32[8,128]{1,0:T(8,128)S(1)}, u32[]{:S(2)}) copy-start(s32[8,128]{1,0:T(8,128)S(1)} %slice_convert_fusion.far_pix) | copy-start | bytes 12292
  34.4 0.7 copy-start.1
  51.1 9.6 %all-to-all-start.1 = ((f32[32,1,128]{2,1,0:T(1,128)}), f32[32,1,128]{2,1,0:T(1,128)S(1)}, u32[]{:S(2)}, u32[]{:S(2)}) async-start(f32[32,1,128]{2,1,0:T(1,128)} %bitcast.21), calls=%async_computation.1 | async-start | bytes 32768 | tf_op jit(solution)/shard_map/all_to_all | solution.py:1074
  60.8 0.6 copy-start.4
  67.0 9.6 %all-to-all-start.2 = ((f32[32,1,128]{2,1,0:T(1,128)}), f32[32,1,128]{2,1,0:T(1,128)S(1)}, u32[]{:S(2)}, u32[]{:S(2)}) async-start(f32[32,1,128]{2,1,0:T(1,128)} %bitcast.20), calls=%async_computation.2 | async-start | bytes 32768 | tf_op jit(solution)/shard_map/all_to_all | solution.py:1074
  76.7 0.6 copy-start.5
  92.1 13.0 %collective-permute-start.1 = (f32[192,128]{1,0:T(8,128)}, f32[192,128]{1,0:T(8,128)S(1)}, u32[]{:S(2)}, u32[]{:S(2)}) collective-permute-start(f32[192,128]{1,0:T(8,128)} %get-tuple-element.57), channel_id=1, source_target_pairs={{4,0},{8,4},{12,8},{16,12},{20,16},{24,20},{28,24},{5,1},{9,5},{13... | collective-permute-start | bytes 294920 | tf_op jit(solution)/shard_map/ppermute | solution.py:1070
  93.4 11.8 %all-to-all-start.3 = ((f32[4,8,1152]{2,1,0:T(8,128)}), f32[4,8,1152]{2,1,0:T(8,128)S(1)}, u32[]{:S(2)}, u32[]{:S(2)}) async-start(f32[4,8,1152]{2,1,0:T(8,128)} %bitcast.15), calls=%async_computation.3 | async-start | bytes 294912 | tf_op jit(solution)/shard_map/all_to_all | solution.py:1136
  105.2 0.6 copy-start.7
  105.2 0.7 copy-start.2
  109.2 17.5 %all-to-all-start.4 = ((f32[32,1,2048]{2,1,0:T(1,128)}), f32[32,1,2048]{2,1,0:T(1,128)S(1)}, u32[]{:S(2)}, u32[]{:S(2)}) async-start(f32[32,1,2048]{2,1,0:T(1,128)} %edges.1), calls=%async_computation.4 | async-start | bytes 524288 | tf_op jit(solution)/shard_map/all_to_all | solution.py:1074
  126.7 0.7 copy-start
